TPU v7x, 256 devices: a whole 4x4x8 slice. The times are simulated.
256 devices in a mesh: dp: 16 (over y_lo, z), tm: 16 (over y_hi, x, core).
Axes of the slice: x: 4, y: 4 (y_hi: 2, y_lo: 2; y = y_hi * 2 + y_lo), z: 8, core: 2. Of those that a mesh axis runs over, the one named last changes fastest.
Arguments:
- signal: bfloat16 [16, 32768, 256], P('dp', 'tm'), may hold values from -6 to 6
- timesteps: int32 [16], P('dp'), may hold values from 0 to 999
- cotangent: bfloat16 [16, 8192, 512], P('dp', 'tm'), may hold values from -6 to 6
- conv_one: bfloat16 [768, 256], replicated, may hold values from -0.21875 to 0.21875
- down_proj: bfloat16 [1024, 512], replicated, may hold values from -0.1875 to 0.1875
- conv_two: bfloat16 [1536, 512], replicated, may hold values from -0.15625 to 0.15625
- time_proj: bfloat16 [256, 256], replicated, may hold values from -0.375 to 0.375
Outputs:
- encoded: bfloat16 [16, 8192, 512], P('dp', 'tm')
- signal_grad: bfloat16 [16, 32768, 256], P('dp', 'tm')
- conv_one_grad: float32 [768, 256], P('dp', 'tm')
- down_proj_grad: float32 [1024, 512], P('dp', 'tm')
- conv_two_grad: float32 [1536, 512], P('dp', 'tm')
- time_proj_grad: float32 [256, 256], P('dp', 'tm')
All inputs are finite; a program needn't handle non-finite values.
Results may differ from a plain program's by a relative error of at most 0.022.
Values may be sent and summed in bfloat16 or wider, within the bound.
No kernel may reach another device: no remote copies, remote signals or barrier semaphores. Data moves between devices by JAX's collectives and lax.ppermute only.
A program may use at most 64 MiB of HBM per device.

v0:
```python
import math

import jax
import jax.numpy as jnp
from jax import lax
from jax.sharding import PartitionSpec as P

EPS = 1e-06


def with_halo(block, sides, width):
    for axis, dim in sides:
        count = lax.axis_size(axis)
        forward = [(i, i + 1) for i in range(count - 1)]
        backward = [(target, source) for source, target in forward]
        low = lax.ppermute(
            lax.slice_in_dim(block, block.shape[dim] - width, None, axis=dim), axis, forward
        )
        high = lax.ppermute(lax.slice_in_dim(block, 0, width, axis=dim), axis, backward)
        block = jnp.concatenate([low, block, high], axis=dim)
    return block


def passed_along(value, axis, steps):
    count = lax.axis_size(axis)
    initial, last = (max(0, -steps), min(count, count - steps))
    return lax.ppermute(value, axis, [(source, source + steps) for source in range(initial, last)])


def cut_along(shard, dim, count):
    before, after = (shard.shape[:dim], shard.shape[dim + 1 :])
    return jnp.moveaxis(shard.reshape(*before, count, -1, *after), dim, 0)


def sum_together(arrays, axis, dims):
    count = lax.axis_size(axis)
    pieces = [cut_along(a, dim, count) for a, dim in zip(arrays, dims)]
    lines = jnp.concatenate([b.reshape(count, -1) for b in pieces], axis=1)
    width = max(16, -(-lines.shape[1] // 1024) * 8)
    lines = jnp.pad(lines, ((0, 0), (0, width * 128 - lines.shape[1]))).reshape(-1, 128)
    line, at, done = (lax.psum_scatter(lines, axis, tiled=True).reshape(-1), 0, [])
    for b in pieces:
        part = b[0]
        done.append(line[at : at + part.size].reshape(part.shape))
        at += part.size
    return tuple(done)


def sum_at_owner(shard, axis, dim):
    pieces = cut_along(shard, dim, lax.axis_size(axis))
    arrived = lax.all_to_all(pieces, axis, split_axis=0, concat_axis=0, tiled=True)
    return arrived.astype(jnp.float32).sum(axis=0)


def in_one_piece(arrays, axis, dim, along):
    both = jnp.concatenate(arrays, axis=along)
    out, at, done = (sum_at_owner(both, axis, dim), 0, [])
    for a in arrays:
        done.append(lax.slice_in_dim(out, at, at + a.shape[along], axis=along))
        at += a.shape[along]
    return tuple(done)


def rms_fwd(values):
    meansq = jnp.mean(values * values, -1, keepdims=True)
    factor = lax.rsqrt(meansq + EPS)
    return (values * factor, factor)


def rms_back(dnorm, normed, factor):
    return factor * (dnorm - normed * jnp.mean(dnorm * normed, -1, keepdims=True))


def silu_slope(values):
    sigm = jax.nn.sigmoid(values)
    return sigm * (1.0 + values * (1.0 - sigm))


def embed(stamps, width):
    half = width // 2
    freqs = jnp.exp(-math.log(10000.0) * jnp.arange(half, dtype=jnp.float32) / half)
    angles = stamps.astype(jnp.float32)[:, None] * freqs[None, :]
    return jnp.concatenate([jnp.sin(angles), jnp.cos(angles)], axis=-1)


def unfold(padded, length):
    return jnp.concatenate([padded[:, offset : offset + length] for offset in range(3)], axis=2)


def back_partial(gradient, weight, fetch):
    batch, length, _ = gradient.shape
    width = weight.shape[0] // 3
    parts = lax.dot_general(
        gradient.reshape(batch * length, -1),
        weight,
        (((1,), (1,)), ((), ())),
        preferred_element_type=jnp.float32,
    ).reshape(batch, length, 3 * width)
    first = parts[:, :, :width]
    middle = parts[:, :, width : 2 * width]
    last = parts[:, :, 2 * width :]
    lead_in, tail_in = fetch(first[:, :1], last[:, -1:])
    return (
        middle
        + jnp.concatenate([first[:, 1:], lead_in], axis=1)
        + jnp.concatenate([tail_in, last[:, :-1]], axis=1)
    )


def per_device(signal, timesteps, cotangent, conv_one, down_proj, conv_two, time_proj):
    batch, length, width_a = signal.shape
    width_b = down_proj.shape[1]
    short = length // 4
    contract = (((0,), (0,)), ((), ()))
    emb_rows = embed(timesteps, time_proj.shape[0])
    temb = jnp.dot(emb_rows, time_proj.astype(jnp.float32), precision=lax.Precision.HIGHEST)
    x32 = signal.astype(jnp.float32)
    normed, factor = rms_fwd(x32)
    pre = normed + temb[:, None, :]
    act_a = jax.nn.silu(pre).astype(jnp.bfloat16)
    padded_a = with_halo(act_a, (("tm", 1),), 1)
    rows_a = unfold(padded_a, length).reshape(batch * length, 3 * width_a)
    hidden_a = jnp.dot(rows_a, conv_one, preferred_element_type=jnp.float32)
    merged = (x32.reshape(batch * length, width_a) + hidden_a).astype(jnp.bfloat16)
    grouped = merged.reshape(batch * short, 4 * width_a)
    coarse = jnp.dot(grouped, down_proj, preferred_element_type=jnp.float32).astype(jnp.bfloat16)
    c32 = coarse.astype(jnp.float32)
    normed_b, factor_b = rms_fwd(c32)
    act_b = jax.nn.silu(normed_b).astype(jnp.bfloat16).reshape(batch, short, width_b)
    padded_b = with_halo(act_b, (("tm", 1),), 1)
    rows_b = unfold(padded_b, short).reshape(batch * short, 3 * width_b)
    encoded = (
        (c32 + jnp.dot(rows_b, conv_two, preferred_element_type=jnp.float32))
        .astype(jnp.bfloat16)
        .reshape(batch, short, width_b)
    )
    grad_rows = cotangent.reshape(batch * short, width_b)
    raw_two = lax.dot_general(rows_b, grad_rows, contract, preferred_element_type=jnp.float32)
    back_b = back_partial(
        cotangent,
        conv_two,
        lambda lead, tail: (passed_along(lead, "tm", -1), passed_along(tail, "tm", 1)),
    )
    slope_b = back_b.reshape(batch * short, width_b) * silu_slope(normed_b)
    d_coarse = (grad_rows.astype(jnp.float32) + rms_back(slope_b, normed_b, factor_b)).astype(
        jnp.bfloat16
    )
    raw_down = lax.dot_general(grouped, d_coarse, contract, preferred_element_type=jnp.float32)
    d_merged = lax.dot_general(
        d_coarse, down_proj, (((1,), (1,)), ((), ())), preferred_element_type=jnp.float32
    ).reshape(batch * length, width_a)
    d_hidden = d_merged.astype(jnp.bfloat16)
    raw_one = lax.dot_general(rows_a, d_hidden, contract, preferred_element_type=jnp.float32)
    d_hidden_3d = d_hidden.reshape(batch, length, width_a)
    back_a = back_partial(
        d_hidden_3d,
        conv_one,
        lambda lead, tail: (passed_along(lead, "tm", -1), passed_along(tail, "tm", 1)),
    )
    d_pre = back_a * silu_slope(pre)
    dtemb = jnp.sum(d_pre, axis=1)
    raw_time = lax.dot_general(
        emb_rows,
        dtemb,
        contract,
        precision=lax.Precision.HIGHEST,
        preferred_element_type=jnp.float32,
    )
    signal_grad = (
        d_merged.reshape(batch, length, width_a) + rms_back(d_pre, normed, factor)
    ).astype(jnp.bfloat16)
    scaling = 1.0 / math.sqrt(batch * lax.axis_size("dp") * length * lax.axis_size("tm"))
    grads = (raw_one * scaling, raw_down * scaling, raw_two * scaling, raw_time * scaling)
    partial_sums = tuple(
        (
            part.astype(jnp.float32)
            for part in sum_together(
                (
                    grads[0].astype(jnp.bfloat16),
                    grads[1].astype(jnp.bfloat16),
                    grads[2].astype(jnp.bfloat16),
                    grads[3].astype(jnp.bfloat16),
                ),
                "dp",
                (0, 0, 0, 0),
            )
        )
    )
    summed = (
        sum_at_owner(partial_sums[0].astype(jnp.bfloat16), "tm", 1),
        *in_one_piece(
            (partial_sums[1].astype(jnp.bfloat16), partial_sums[2].astype(jnp.bfloat16)), "tm", 1, 0
        ),
        sum_at_owner(partial_sums[3].astype(jnp.bfloat16), "tm", 1),
    )
    return (encoded, signal_grad, summed[0], summed[1], summed[2], summed[3])


def solution(mesh):
    return jax.shard_map(
        per_device,
        mesh=mesh,
        in_specs=(P("dp", "tm", None), P("dp"), P("dp", "tm", None), P(), P(), P(), P()),
        out_specs=(
            P("dp", "tm", None),
            P("dp", "tm", None),
            P("dp", "tm"),
            P("dp", "tm"),
            P("dp", "tm"),
            P("dp", "tm"),
        ),
        check_vma=False,
    )
```

profile of v0, /device:TPU:32, one launch (start us, length us, event | category | flops | bytes accessed | tf_op | source)
XLA Modules:
  0.0 222.9 jit_solution(8063906528513420759)
XLA Ops:
  18.7 5.6 %collective-permute-start.5 = (f32[1,1,512]{2,1,0:T(1,128)}, f32[1,1,512]{2,1,0:T(1,128)}, u32[]{:S(2)}, u32[]{:S(2)}) collective-permute-start(f32[1,1,512]{2,1,0:T(1,128)} %get-tuple-element.30), channel_id=1, source_target_pairs={{0,1},{1,2},{2,3},{3,4},{4,5},{5,6},{6,7},{7,8},{8,9},{9,10},{10,1... | collective-permute-start | bytes 6152 | tf_op jit(solution)/shard_map/ppermute | solution.py:27
  27.1 3.3 %fusion.10 = bf16[2048,256]{1,0:T(8,128)(2,1)} fusion(bf16[768,256]{1,0:T(8,128)(2,1)S(1)} %copy-done.15, bf16[1,2048,256]{2,1,0:T(8,128)(2,1)S(1)} %copy-done.2, bf16[1,1,256]{2,1,0:T(2,128)(2,1)S(1)} %collective-permute-done.1, bf16[1,2048,256]{2,1,0:T(8,128)(2,1)S(1)} %fusion.14, bf16[1,1,256]{2,1,0:T(2,128)(2,1)S(1)} %collective-permute-done), kind=kOutput, calls=%fused_computation.20 | convolution fusion | flops 822607872 | bytes 3539968 | tf_op jit(solution)/shard_map/dot_general | solution.py:123
  30.4 2.5 %reshape.150 = bf16[512,1024]{1,0:T(8,128)(2,1)} reshape(bf16[2048,256]{1,0:T(8,128)(2,1)} %fusion.10) | data formatting | bytes 2097152 | tf_op jit(solution)/shard_map/reshape | solution.py:125
  32.9 2.5 %fusion.48 = (f32[512]{0:T(512)S(1)}, bf16[512,512]{1,0:T(8,128)(2,1)S(1)}) fusion(bf16[512,1024]{1,0:T(8,128)(2,1)} %reshape.150, bf16[1024,512]{1,0:T(8,128)(2,1)} %param.11), kind=kOutput, calls=%fused_computation.67 | convolution fusion | flops 537918976 | bytes 2623488 | tf_op jit(solution)/shard_map/dot_general | solution.py:126
  40.7 2.4 %fusion.75 = (bf16[512,1024]{1,0:T(8,128)(2,1)}, f32[512,1024]{1,0:T(8,128)}) fusion(bf16[512,512]{1,0:T(8,128)(2,1)S(1)} %get-tuple-element.33, bf16[1024,512]{1,0:T(8,128)(2,1)S(1)} %copy-done.13), kind=kOutput, calls=%fused_computation.100 | convolution fusion | flops 537395200 | bytes 4718592 | tf_op jit(solution)/shard_map/dot_general | solution.py:149
  43.7 3.6 %collective-permute-start.2 = (bf16[1,1,512]{2,1,0:T(2,128)(2,1)}, bf16[1,1,512]{2,1,0:T(2,128)(2,1)}, u32[]{:S(2)}, u32[]{:S(2)}) collective-permute-start(bf16[1,1,512]{2,1,0:T(2,128)(2,1)} %get-tuple-element.35), channel_id=1, source_target_pairs={{0,1},{1,2},{2,3},{3,4},{4,5},{5,6},{6,7},{7,8},{8,9},{9,10},{10,1... | collective-permute-start | bytes 3080 | tf_op jit(solution)/shard_map/ppermute | solution.py:16
  48.6 2.5 %convert_element_type.81 = bf16[2048,256]{1,0:T(8,128)(2,1)} reshape(bf16[512,1024]{1,0:T(8,128)(2,1)} %get-tuple-element.39) | data formatting | bytes 2097152 | tf_op jit(solution)/shard_map/convert_element_type | solution.py:152
  56.4 3.9 %fusion.34 = bf16[768,256]{1,0:T(8,128)(2,1)} fusion(bf16[2048,256]{1,0:T(8,128)(2,1)S(1)} %copy-done.4, bf16[1,1,256]{2,1,0:T(2,128)(2,1)S(1)} %copy-done.19, bf16[1,2048,256]{2,1,0:T(8,128)(2,1)S(1)} %copy-done.11, bf16[1,1,256]{2,1,0:T(2,128)(2,1)S(1)} %copy-done.17), kind=kOutput, calls=%fused_computation.53 | convolution fusion | flops 821428224 | bytes 2491392 | tf_op jit(solution)/shard_map/dot_general | solution.py:153
  60.8 2.3 %reshape_reshape.17 = bf16[16,32768]{1,0:T(8,128)(2,1)} reshape(bf16[1024,512]{1,0:T(8,128)(2,1)} %multiply_convert_fusion) | data formatting | bytes 2097152 | tf_op jit(solution)/shard_map/reshape;reshape | solution.py:38
  65.7 4.2 %collective-permute-start.7 = (f32[1,1,256]{2,1,0:T(1,128)}, f32[1,1,256]{2,1,0:T(1,128)}, u32[]{:S(2)}, u32[]{:S(2)}) collective-permute-start(f32[1,1,256]{2,1,0:T(1,128)} %get-tuple-element.26), channel_id=1, source_target_pairs={{0,1},{1,2},{2,3},{3,4},{4,5},{5,6},{6,7},{7,8},{8,9},{9,10},{10,1... | collective-permute-start | bytes 3080 | tf_op jit(solution)/shard_map/ppermute | solution.py:27
  69.9 3.6 %fusion.3 = bf16[1536,512]{1,0:T(8,128)(2,1)} fusion(bf16[1,512,512]{2,1,0:T(8,128)(2,1)S(1)} %copy-done.7, bf16[1,1,512]{2,1,0:T(2,128)(2,1)} %collective-permute-done.3, bf16[1,512,512]{2,1,0:T(8,128)(2,1)} %copy-done.14, bf16[1,1,512]{2,1,0:T(2,128)(2,1)} %collective-permute-done.2), kind=kOutput, calls=%fused_computation.12 | convolution fusion | flops 814743552 | bytes 2623488 | tf_op jit(solution)/shard_map/dot_general | solution.py:138
  73.5 2.8 %reshape_reshape.18 = bf16[16,49152]{1,0:T(8,128)(2,1)} reshape(bf16[1536,512]{1,0:T(8,128)(2,1)} %fusion.3) | data formatting | bytes 3145728 | tf_op jit(solution)/shard_map/reshape;reshape | solution.py:38
  76.3 5.0 %fusion.66 = (f32[256]{0:T(256)S(1)}, f32[2048]{0:T(1024)S(1)}, f32[1,2048,256]{2,1,0:T(8,128)}) fusion(f32[2048]{0:T(1024)S(1)} %add_rsqrt_fusion, bf16[1,2048,256]{2,1,0:T(8,128)(2,1)S(1)} %copy-done.2, f32[256]{0:T(256)S(1)} %bitcast.61, f32[1,2047,256]{2,1,0:T(8,128)} %get-tuple-element.24, f32[1,1,256]{2,1,0:T(1,128)} %collective-permute-done.7, ...), kind=kLoop, calls=%fused_computation.93 | loop fusion | flops 9434880 | bytes 9455616 | tf_op jit(solution)/shard_map/reduce_sum | solution.py:161
  81.5 3.1 %pad_maximum_fusion.2 = bf16[16,98304]{1,0:T(8,128)(2,1)} fusion(bf16[16,4096]{1,0:T(8,128)(2,1)S(1)} %reshape_reshape.19, bf16[16,49152]{1,0:T(8,128)(2,1)} %reshape_reshape.18, bf16[16,32768]{1,0:T(8,128)(2,1)} %reshape_reshape.17, bf16[16,12288]{1,0:T(8,128)(2,1)S(1)} %reshape_reshape.16), kind=kLoop, calls=%fused_computation.8 | loop fusion | flops 12582912 | bytes 6291456 | tf_op jit(solution)/shard_map/concatenate | solution.py:38
  84.6 4.0 %reshape.158 = bf16[12288,128]{1,0:T(8,128)(2,1)} reshape(bf16[16,98304]{1,0:T(8,128)(2,1)} %pad_maximum_fusion.2) | data formatting | bytes 6291456 | tf_op jit(solution)/shard_map/reshape | solution.py:40
  88.6 2.9 %reshape_reshape.15 = f32[1,2048,256]{2,1,0:T(8,128)} reshape(f32[512,1024]{1,0:T(8,128)} %get-tuple-element.40) | data formatting | bytes 4194304 | tf_op jit(solution)/shard_map/reshape;reshape | solution.py:170
  91.5 3.4 %fusion.22 = bf16[1,2048,256]{2,1,0:T(8,128)(2,1)} fusion(f32[1,2048,256]{2,1,0:T(8,128)} %reshape_reshape.15, f32[1,2048,256]{2,1,0:T(8,128)} %get-tuple-element.20, bf16[1,2048,256]{2,1,0:T(8,128)(2,1)S(1)} %copy-done.2, f32[2048]{0:T(1024)S(1)} %broadcast_multiply_fusion, f32[2048]{0:T(1024)S(1)} %add_rsqrt_fusion), kind=kLoop, calls=%fused_computation.32 | loop fusion | flops 3670016 | bytes 6307840 | tf_op jit(solution)/shard_map/convert_element_type | solution.py:171
  94.9 78.7 %reduce-scatter.2.cloned.1.call-done = bf16[768,128]{1,0:T(8,128)(2,1)} async-done(((bf16[12288,128]{1,0:T(8,128)(2,1)}), bf16[768,128]{1,0:T(8,128)(2,1)}) %reduce-scatter.2.cloned.1.call-update) | async-done | bytes 196624 | tf_op jit(solution)/shard_map/reduce_scatter | solution.py:41
  175.2 6.4 %all-to-all-start.2 = ((bf16[16,2,128]{2,1,0:T(2,128)(2,1)}), bf16[16,2,128]{2,1,0:T(2,128)(2,1)S(1)}, u32[]{:S(2)}, u32[]{:S(2)}) async-start(bf16[16,2,128]{2,1,0:T(2,128)(2,1)} %reshape.165), calls=%async_computation.3 | async-start | bytes 16384 | tf_op jit(solution)/shard_map/all_to_all | solution.py:51
  181.6 3.2 %fusion.35 = bf16[1,512,512]{2,1,0:T(8,128)(2,1)} fusion(bf16[1536,512]{1,0:T(8,128)(2,1)S(1)} %copy-done, bf16[512,512]{1,0:T(8,128)(2,1)S(1)} %copy-done.9, bf16[1,1,512]{2,1,0:T(2,128)(2,1)} %collective-permute-done.3, bf16[1,512,512]{2,1,0:T(8,128)(2,1)} %copy-done.14, bf16[1,1,512]{2,1,0:T(2,128)(2,1)} %collective-permute-done.2), kind=kOutput, calls=%fused_computation.54 | convolution fusion | flops 813957120 | bytes 3147776 | tf_op jit(solution)/shard_map/dot_general | solution.py:133
  189.1 5.1 %all-to-all-start = ((bf16[16,2,384]{2,1,0:T(2,128)(2,1)}), bf16[16,2,384]{2,1,0:T(2,128)(2,1)S(1)}, u32[]{:S(2)}, u32[]{:S(2)}) async-start(bf16[16,2,384]{2,1,0:T(2,128)(2,1)} %reshape.163), calls=%async_computation.1 | async-start | bytes 49152 | tf_op jit(solution)/shard_map/all_to_all | solution.py:51
  195.2 6.6 %all-to-all-done = bf16[16,2,384]{2,1,0:T(2,128)(2,1)S(1)} async-done(((bf16[16,2,384]{2,1,0:T(2,128)(2,1)}), bf16[16,2,384]{2,1,0:T(2,128)(2,1)S(1)}, u32[]{:S(2)}, u32[]{:S(2)}) %all-to-all-start) | async-done | bytes 24608 | tf_op jit(solution)/shard_map/all_to_all | solution.py:51
  201.8 3.5 %all-to-all-start.1 = ((bf16[16,160,32]{1,2,0:T(8,128)(2,1)}), bf16[16,160,32]{1,2,0:T(8,128)(2,1)S(1)}, u32[]{:S(2)}, u32[]{:S(2)}) async-start(bf16[16,160,32]{1,2,0:T(8,128)(2,1)} %maximum_bitcast_fusion), calls=%async_computation.2 | async-start | bytes 524288 | tf_op jit(solution)/shard_map/all_to_all | solution.py:51
  206.7 8.0 %all-to-all-done.1 = bf16[16,160,32]{1,2,0:T(8,128)(2,1)S(1)} async-done(((bf16[16,160,32]{1,2,0:T(8,128)(2,1)}), bf16[16,160,32]{1,2,0:T(8,128)(2,1)S(1)}, u32[]{:S(2)}, u32[]{:S(2)}) %all-to-all-start.1) | async-done | bytes 163872 | tf_op jit(solution)/shard_map/all_to_all | solution.py:51
  (104 shorter events, 38.3 us)
Async XLA Ops:
  7.2 8.6 %copy-start = (bf16[1536,512]{1,0:T(8,128)(2,1)S(1)}, bf16[1536,512]{1,0:T(8,128)(2,1)}, u32[]{:S(2)}) copy-start(bf16[1536,512]{1,0:T(8,128)(2,1)} %param.12) | copy-start | bytes 4718596
  7.2 8.6 %copy-start.7 = (bf16[1,512,512]{2,1,0:T(8,128)(2,1)S(1)}, bf16[1,512,512]{2,1,0:T(8,128)(2,1)}, u32[]{:S(2)}) copy-start(bf16[1,512,512]{2,1,0:T(8,128)(2,1)} %param.9) | copy-start | bytes 1572868
  7.2 166.4 %reduce-scatter.2.cloned.1.call-start = ((), (), s32[]{:S(2)}) async-start(), calls=%async_computation.4 | async-start | bytes 3342336 | tf_op jit(solution)/shard_map/reduce_scatter | solution.py:41
  12.7 13.3 %copy-start.10 = (bf16[1,2048,256]{2,1,0:T(8,128)(2,1)}, bf16[1,2048,256]{2,1,0:T(8,128)(2,1)S(1)}, u32[]{:S(2)}) copy-start(bf16[1,2048,256]{2,1,0:T(8,128)(2,1)S(1)} %fusion.14) | copy-start | bytes 3145732
  12.7 13.3 %collective-permute-start = (bf16[1,1,256]{2,1,0:T(2,128)(2,1)S(1)}, bf16[1,1,256]{2,1,0:T(2,128)(2,1)S(1)}, u32[]{:S(2)}, u32[]{:S(2)}) collective-permute-start(bf16[1,1,256]{2,1,0:T(2,128)(2,1)S(1)} %get-tuple-element.31), channel_id=1, source_target_pairs={{0,1},{1,2},{2,3},{3,4},{4,5},{5,6},{6,7},{7,8},{8,9},{9,10},{10,1... | collective-permute-start | bytes 1544 | tf_op jit(solution)/shard_map/ppermute | solution.py:16
  14.4 11.6 %collective-permute-start.1 = (bf16[1,1,256]{2,1,0:T(2,128)(2,1)S(1)}, bf16[1,1,256]{2,1,0:T(2,128)(2,1)S(1)}, u32[]{:S(2)}, u32[]{:S(2)}) collective-permute-start(bf16[1,1,256]{2,1,0:T(2,128)(2,1)S(1)} %get-tuple-element.32), channel_id=1, source_target_pairs={{1,0},{2,1},{3,2},{4,3},{5,4},{6,5},{7,6},{8,7},{9,8},{10,9},{11,1... | collective-permute-start | bytes 1544 | tf_op jit(solution)/shard_map/ppermute | solution.py:19
  16.8 9.2 %copy-start.3 = (f32[1,512,1536]{2,1,0:T(8,128)}, f32[1,512,1536]{2,1,0:T(8,128)S(1)}, u32[]{:S(2)}) copy-start(f32[1,512,1536]{2,1,0:T(8,128)S(1)} %convolution_bitcast_fusion.1) | copy-start | bytes 9437188
  17.4 18.0 %collective-permute-start.4 = (f32[1,1,512]{2,1,0:T(1,128)}, f32[1,1,512]{2,1,0:T(1,128)}, u32[]{:S(2)}, u32[]{:S(2)}) collective-permute-start(f32[1,1,512]{2,1,0:T(1,128)} %get-tuple-element.29), channel_id=1, source_target_pairs={{1,0},{2,1},{3,2},{4,3},{5,4},{6,5},{7,6},{8,7},{9,8},{10,9},{11,1... | collective-permute-start | bytes 6152 | tf_op jit(solution)/shard_map/ppermute | solution.py:27
  18.7 8.4 %copy-start.2 = (bf16[1,2048,256]{2,1,0:T(8,128)(2,1)S(1)}, bf16[1,2048,256]{2,1,0:T(8,128)(2,1)}, u32[]{:S(2)}) copy-start(bf16[1,2048,256]{2,1,0:T(8,128)(2,1)} %param.7) | copy-start | bytes 3145732
  18.7 8.4 %copy-start.15 = (bf16[768,256]{1,0:T(8,128)(2,1)S(1)}, bf16[768,256]{1,0:T(8,128)(2,1)}, u32[]{:S(2)}) copy-start(bf16[768,256]{1,0:T(8,128)(2,1)} %param.10) | copy-start | bytes 1179652
  18.7 16.7 %collective-permute-start.5 = (f32[1,1,512]{2,1,0:T(1,128)}, f32[1,1,512]{2,1,0:T(1,128)}, u32[]{:S(2)}, u32[]{:S(2)}) collective-permute-start(f32[1,1,512]{2,1,0:T(1,128)} %get-tuple-element.30), channel_id=1, source_target_pairs={{0,1},{1,2},{2,3},{3,4},{4,5},{5,6},{6,7},{7,8},{8,9},{9,10},{10,1... | collective-permute-start | bytes 6152 | tf_op jit(solution)/shard_map/ppermute | solution.py:27
  38.3 4.8 %copy-start.14 = (bf16[1,512,512]{2,1,0:T(8,128)(2,1)}, bf16[1,512,512]{2,1,0:T(8,128)(2,1)S(1)}, u32[]{:S(2)}) copy-start(bf16[1,512,512]{2,1,0:T(8,128)(2,1)S(1)} %get-tuple-element.34) | copy-start | bytes 1572868
  43.7 26.2 %collective-permute-start.2 = (bf16[1,1,512]{2,1,0:T(2,128)(2,1)}, bf16[1,1,512]{2,1,0:T(2,128)(2,1)}, u32[]{:S(2)}, u32[]{:S(2)}) collective-permute-start(bf16[1,1,512]{2,1,0:T(2,128)(2,1)} %get-tuple-element.35), channel_id=1, source_target_pairs={{0,1},{1,2},{2,3},{3,4},{4,5},{5,6},{6,7},{7,8},{8,9},{9,10},{10,1... | collective-permute-start | bytes 3080 | tf_op jit(solution)/shard_map/ppermute | solution.py:16
  47.3 22.6 %collective-permute-start.3 = (bf16[1,1,512]{2,1,0:T(2,128)(2,1)}, bf16[1,1,512]{2,1,0:T(2,128)(2,1)}, u32[]{:S(2)}, u32[]{:S(2)}) collective-permute-start(bf16[1,1,512]{2,1,0:T(2,128)(2,1)} %get-tuple-element.36), channel_id=1, source_target_pairs={{1,0},{2,1},{3,2},{4,3},{5,4},{6,5},{7,6},{8,7},{9,8},{10,9},{11,1... | collective-permute-start | bytes 3080 | tf_op jit(solution)/shard_map/ppermute | solution.py:19
  53.3 7.0 %copy-start.1 = (f32[1,2048,768]{2,1,0:T(8,128)}, f32[1,2048,768]{2,1,0:T(8,128)S(1)}, u32[]{:S(2)}) copy-start(f32[1,2048,768]{2,1,0:T(8,128)S(1)} %convolution_bitcast_fusion) | copy-start | bytes 18874372
  64.3 11.9 %collective-permute-start.6 = (f32[1,1,256]{2,1,0:T(1,128)}, f32[1,1,256]{2,1,0:T(1,128)}, u32[]{:S(2)}, u32[]{:S(2)}) collective-permute-start(f32[1,1,256]{2,1,0:T(1,128)} %get-tuple-element.25), channel_id=1, source_target_pairs={{1,0},{2,1},{3,2},{4,3},{5,4},{6,5},{7,6},{8,7},{9,8},{10,9},{11,1... | collective-permute-start | bytes 3080 | tf_op jit(solution)/shard_map/ppermute | solution.py:27
  65.7 10.6 %collective-permute-start.7 = (f32[1,1,256]{2,1,0:T(1,128)}, f32[1,1,256]{2,1,0:T(1,128)}, u32[]{:S(2)}, u32[]{:S(2)}) collective-permute-start(f32[1,1,256]{2,1,0:T(1,128)} %get-tuple-element.26), channel_id=1, source_target_pairs={{0,1},{1,2},{2,3},{3,4},{4,5},{5,6},{6,7},{7,8},{8,9},{9,10},{10,1... | collective-permute-start | bytes 3080 | tf_op jit(solution)/shard_map/ppermute | solution.py:27
  91.5 90.1 %copy-start.9 = (bf16[512,512]{1,0:T(8,128)(2,1)S(1)}, bf16[512,512]{1,0:T(8,128)(2,1)}, u32[]{:S(2)}) copy-start(bf16[512,512]{1,0:T(8,128)(2,1)} %copy-done.8) | copy-start | bytes 1572868
  175.2 13.9 %all-to-all-start.2 = ((bf16[16,2,128]{2,1,0:T(2,128)(2,1)}), bf16[16,2,128]{2,1,0:T(2,128)(2,1)S(1)}, u32[]{:S(2)}, u32[]{:S(2)}) async-start(bf16[16,2,128]{2,1,0:T(2,128)(2,1)} %reshape.165), calls=%async_computation.3 | async-start | bytes 16384 | tf_op jit(solution)/shard_map/all_to_all | solution.py:51
  181.6 3.3 %slice-start = ((bf16[768,128]{1,0:T(8,128)(2,1)}), bf16[96,128]{1,0:T(8,128)(2,1)S(1)}, s32[]{:S(2)}) async-start(bf16[768,128]{1,0:T(8,128)(2,1)} %reduce-scatter.2.cloned.1.call-done), calls=%async_computation.5 | async-start | bytes 49152 | tf_op jit(solution)/shard_map/slice | solution.py:44
  181.6 4.4 %slice-start.1 = ((bf16[768,128]{1,0:T(8,128)(2,1)}), bf16[256,128]{1,0:T(8,128)(2,1)S(1)}, s32[]{:S(2)}) async-start(bf16[768,128]{1,0:T(8,128)(2,1)} %reduce-scatter.2.cloned.1.call-done), calls=%async_computation.6 | async-start | bytes 131072 | tf_op jit(solution)/shard_map/slice | solution.py:44
  181.6 4.8 %slice-start.2 = ((bf16[768,128]{1,0:T(8,128)(2,1)}), bf16[384,128]{1,0:T(8,128)(2,1)S(1)}, s32[]{:S(2)}) async-start(bf16[768,128]{1,0:T(8,128)(2,1)} %reduce-scatter.2.cloned.1.call-done), calls=%async_computation.7 | async-start | bytes 196608 | tf_op jit(solution)/shard_map/slice | solution.py:44
  189.1 12.7 %all-to-all-start = ((bf16[16,2,384]{2,1,0:T(2,128)(2,1)}), bf16[16,2,384]{2,1,0:T(2,128)(2,1)S(1)}, u32[]{:S(2)}, u32[]{:S(2)}) async-start(bf16[16,2,384]{2,1,0:T(2,128)(2,1)} %reshape.163), calls=%async_computation.1 | async-start | bytes 49152 | tf_op jit(solution)/shard_map/all_to_all | solution.py:51
  201.8 12.9 %all-to-all-start.1 = ((bf16[16,160,32]{1,2,0:T(8,128)(2,1)}), bf16[16,160,32]{1,2,0:T(8,128)(2,1)S(1)}, u32[]{:S(2)}, u32[]{:S(2)}) async-start(bf16[16,160,32]{1,2,0:T(8,128)(2,1)} %maximum_bitcast_fusion), calls=%async_computation.2 | async-start | bytes 524288 | tf_op jit(solution)/shard_map/all_to_all | solution.py:51
  (11 other events, 23.5 us)
Sparse Core Ops, SparseCore 0:
  88.7 84.8 reduce-scatter.1
where the time goes:
time: 227 us; the launch traced here: 223 us
  waiting for transfers between devices  95.5 us (42%)
  starting transfers between devices  35.5 us (16%)
  local copies, waits for them, and re-layouts  31.5 us (14%)
  matrix products  25 us (11%)
  other arithmetic  20.1 us (9%)
  between operations  15.3 us (7%)
    reduce_scatter x1, waiting for transfers between devices, sum_together(): lax.psum_scatter(lines, axis, tiled=True).reshape(-1)  78.7 us
    all_to_all x3, waiting for transfers between devices, sum_at_owner(): lax.all_to_all(pieces, axis, split_axis=0, concat_axis=0, tiled=True)  16.7 us
    all_to_all x3, starting transfers between devices, sum_at_owner(): lax.all_to_all(pieces, axis, split_axis=0, concat_axis=0, tiled=True)  15.1 us
    ppermute x4, starting transfers between devices, passed_along(): lax.ppermute(value, axis, [(source, source + steps) for source in range(i...  12.4 us
    another operation x4, local copies, waits for them, and re-layouts, sum_together(): lines = jnp.concatenate([b.reshape(count, -1) for b in pieces], axis=1)  6.36 us
    ppermute x2, starting transfers between devices, with_halo(): lax.ppermute(lax.slice_in_dim(block, block.shape[dim] - width, None, axis...  5.37 us
    reduce_sum x1, other arithmetic, per_device(): dtemb = jnp.sum(d_pre, axis=1)  5.04 us
  transfers between devices with their start and end apart: 12, of which 4 were waited for; matrix products, arithmetic and copies ran while one was open for 21% of the time, Pallas kernels for 0%

commit v1 on v0

v1 whole, which is shorter than its diff:
```python
import math

import jax
import jax.numpy as jnp
from jax import lax
from jax.experimental import pallas as pl
from jax.experimental.pallas import tpu as pltpu
from jax.sharding import PartitionSpec as P

EPS = 1e-06
CA, CB, EMB = 256, 512, 256
S = 512
E = 528
STEP = 176
F32, BF16 = jnp.float32, jnp.bfloat16
AXES = ("dp", "tm")
NT = (((1,), (1,)), ((), ()))


def dot(a, b):
    return jnp.dot(a, b, preferred_element_type=F32)


def dot_nt(a, b):
    return lax.dot_general(a, b, NT, preferred_element_type=F32)


def rows_of(i, size):
    return pl.ds(pl.multiple_of(i * size, 16), size)


def sigmoid(v):
    return 1.0 / (1.0 + jnp.exp(-v))


def inside(idx_ref, start, size, margin):
    row = lax.broadcasted_iota(jnp.int32, (size, 1), 0) + start
    past = jnp.logical_and(row >= S, row < S + margin)
    before = row >= E - margin
    off = jnp.logical_or(
        jnp.logical_and(past, idx_ref[4] == 1), jnp.logical_and(before, idx_ref[3] == 1)
    )
    return jnp.where(off, 0.0, 1.0)


def phase(ref, start, size):
    return jnp.concatenate([ref[h, pl.ds(start, size, stride=4), :] for h in range(2)], axis=1)


def later(v):
    return pltpu.roll(v, 1, 0)


def sooner(v):
    return pltpu.roll(v, v.shape[0] - 1, 0)


def grads_kernel(
    idx_ref, x_ref, left_ref, right_ref, cot_ref, temb_ref, one_ref, down_ref, two_ref,
    ga_ref, gb_ref, dc_ref, ab_ref, co_ref,
    xs_ref, uw_ref, mw_ref, ubw_ref, cw_ref, slope_ref, normed_ref, fac_ref, dh_ref,
):
    @pl.loop(0, 16)
    def _(i):
        r = rows_of(i, 128)
        v = x_ref[r, :].astype(F32)
        xs_ref[0, r, :] = v[:, :128]
        xs_ref[1, r, :] = v[:, 128:]

    for h in range(2):
        lanes = slice(h * 128, (h + 1) * 128)
        xs_ref[h, 2048:2056, :] = right_ref[:, lanes].astype(F32)
        xs_ref[h, 2056:2104, :] = jnp.zeros((48, 128), F32)
        xs_ref[h, 2104:2112, :] = left_ref[:, lanes].astype(F32)

    @pl.loop(0, 11)
    def _(i):
        r = rows_of(i, 48)
        keep = inside(idx_ref, i * 48, 48, 2)
        for j in range(4):
            v = phase(xs_ref, i * 192 + j, 48)
            pre = v * lax.rsqrt(jnp.mean(v * v, -1, keepdims=True) + EPS) + temb_ref[...]
            act = pre * sigmoid(pre) * keep
            uw_ref[r, (j + 1) * CA : (j + 2) * CA] = act.astype(BF16)

    uw_ref[:, :CA] = later(uw_ref[:, 4 * CA : 5 * CA].astype(F32)).astype(BF16)
    uw_ref[:, 5 * CA :] = sooner(uw_ref[:, CA : 2 * CA].astype(F32)).astype(BF16)

    zeros = jnp.zeros((12, CB), F32)
    cot = jnp.concatenate(
        [
            cot_ref[...].astype(F32),
            right_ref[:2, CA:].astype(F32),
            zeros,
            left_ref[6:, CA:].astype(F32),
        ],
        axis=0,
    )
    cw_ref[:, CB : 2 * CB] = cot.astype(BF16)
    cw_ref[:, :CB] = sooner(cot).astype(BF16)
    cw_ref[:, 2 * CB :] = later(cot).astype(BF16)

    @pl.loop(0, 3)
    def _(i):
        r = rows_of(i, STEP)
        for j in range(4):
            hidden = dot(uw_ref[r, j * CA : (j + 3) * CA], one_ref[...])
            v = phase(xs_ref, i * STEP * 4 + j, STEP)
            mw_ref[r, j * CA : (j + 1) * CA] = (v + hidden).astype(BF16)
        coarse = dot(mw_ref[r, :], down_ref[...]).astype(BF16)
        co_ref[r, :] = coarse
        c32 = coarse.astype(F32)
        factor = lax.rsqrt(jnp.mean(c32 * c32, -1, keepdims=True) + EPS)
        normed = c32 * factor
        sig = sigmoid(normed)
        keep = inside(idx_ref, i * STEP, STEP, 1)
        ubw_ref[r, CB : 2 * CB] = (normed * sig * keep).astype(BF16)
        fac_ref[r, :] = jnp.broadcast_to(factor, (STEP, 128))
        normed_ref[r, :] = normed
        slope_ref[r, :] = sig * (1.0 + normed * (1.0 - sig))

    act_b = ubw_ref[:, CB : 2 * CB]
    ab_ref[...] = act_b
    act_b = act_b.astype(F32)
    ubw_ref[:, :CB] = later(act_b).astype(BF16)
    ubw_ref[:, 2 * CB :] = sooner(act_b).astype(BF16)

    @pl.loop(0, 3)
    def _(i):
        r = rows_of(i, STEP)
        back = dot_nt(cw_ref[r, :CB], two_ref[:CB, :])
        back += dot_nt(cw_ref[r, CB : 2 * CB], two_ref[CB : 2 * CB, :])
        back += dot_nt(cw_ref[r, 2 * CB :], two_ref[2 * CB :, :])
        normed = normed_ref[r, :]
        q = back * slope_ref[r, :]
        m = jnp.mean(q * normed, -1, keepdims=True)
        keep = inside(idx_ref, i * STEP, STEP, 1)
        grad = cw_ref[r, CB : 2 * CB].astype(F32) + fac_ref[r, :1] * (q - normed * m)
        d_coarse = (grad * keep).astype(BF16)
        dc_ref[r, :] = d_coarse
        dh_ref[r, :] = dot_nt(d_coarse, down_ref[...]).astype(BF16)

    scaling = 1.0 / math.sqrt(16 * 32768)
    core, x, yhi = idx_ref[0], idx_ref[1], idx_ref[2]

    def place(chunk):
        c, xx, y = chunk % 2, (chunk // 2) % 4, chunk // 8
        return ((c + core) % 2) * 8 + ((xx + 4 - x) % 4) * 2 + (y + yhi) % 2

    def turned(ref, lanes):
        return ref[:S, lanes].astype(F32).T.astype(BF16)

    @pl.loop(0, 4)
    def _(i):
        lanes = pl.ds(pl.multiple_of(i * 128, 128), 128)
        at = cw_ref[:S, pl.ds(pl.multiple_of(CB + i * 128, 128), 128)].astype(F32).T.astype(BF16)
        two = (dot(at, ubw_ref[:S, :]) * scaling).astype(BF16)
        for c in range(4):
            ga_ref[place(i * 4 + c)] = two[c * 32 : (c + 1) * 32, :]
        at = turned(dc_ref, lanes)
        down = (dot(at, mw_ref[:S, :]) * scaling).astype(BF16)
        for c in range(4):
            gb_ref[place(i * 4 + c), :32] = down[c * 32 : (c + 1) * 32, :]

    @pl.loop(0, 2)
    def _(i):
        total = jnp.zeros((128, 3 * CA), F32)
        for j in range(4):
            lanes = pl.ds(pl.multiple_of(j * CA + i * 128, 128), 128)
            total += dot(turned(dh_ref, lanes), uw_ref[:S, j * CA : (j + 3) * CA])
        total = (total * scaling).astype(BF16)
        for c in range(8):
            gb_ref[place(i * 8 + c), 32:, : 3 * CA] = total[c * 16 : (c + 1) * 16, :]
            gb_ref[place(i * 8 + c), 32:, 3 * CA :] = jnp.zeros((16, EMB), BF16)


def outputs_kernel(
    x_ref, co_ref, ab_ref, dc_ref, temb_ref, one_ref, down_ref, two_ref,
    enc_ref, sg_ref, dt_ref,
    xs_ref, ys_ref, ubw_ref, dm_ref, dhw_ref,
):
    @pl.loop(0, 16)
    def _(i):
        r = rows_of(i, 128)
        v = x_ref[r, :].astype(F32)
        xs_ref[0, r, :] = v[:, :128]
        xs_ref[1, r, :] = v[:, 128:]

    act_b = ab_ref[...].astype(F32)
    ubw_ref[:, CB : 2 * CB] = ab_ref[...]
    ubw_ref[:, :CB] = later(act_b).astype(BF16)
    ubw_ref[:, 2 * CB :] = sooner(act_b).astype(BF16)

    @pl.loop(0, 4)
    def _(i):
        r = rows_of(i, 128)
        enc = co_ref[r, :].astype(F32) + dot(ubw_ref[r, :], two_ref[...])
        enc_ref[r, :] = enc.astype(BF16)

    @pl.loop(0, 3)
    def _(i):
        r = rows_of(i, STEP)
        dm = dot_nt(dc_ref[r, :], down_ref[...])
        dm_ref[r, :] = dm
        dhw_ref[r, CA : 5 * CA] = dm.astype(BF16)

    dhw_ref[:, :CA] = later(dhw_ref[:, 4 * CA : 5 * CA].astype(F32)).astype(BF16)
    dhw_ref[:, 5 * CA :] = sooner(dhw_ref[:, CA : 2 * CA].astype(F32)).astype(BF16)
    dt_ref[...] = jnp.zeros((8, CA), F32)

    @pl.loop(0, 4)
    def _(i):
        r = rows_of(i, 128)
        for j in range(4):
            back = dot_nt(dhw_ref[r, (j + 2) * CA : (j + 3) * CA], one_ref[:CA, :])
            back += dot_nt(dhw_ref[r, (j + 1) * CA : (j + 2) * CA], one_ref[CA : 2 * CA, :])
            back += dot_nt(dhw_ref[r, j * CA : (j + 1) * CA], one_ref[2 * CA :, :])
            v = phase(xs_ref, i * 512 + j, 128)
            factor = lax.rsqrt(jnp.mean(v * v, -1, keepdims=True) + EPS)
            normed = v * factor
            pre = normed + temb_ref[...]
            sig = sigmoid(pre)
            d_pre = back * (sig * (1.0 + pre * (1.0 - sig)))
            dt_ref[...] += d_pre.reshape(16, 8, CA).sum(0)
            m = jnp.mean(d_pre * normed, -1, keepdims=True)
            grad = dm_ref[r, j * CA : (j + 1) * CA] + factor * (d_pre - normed * m)
            ys_ref[0, pl.ds(i * 512 + j, 128, stride=4), :] = grad[:, :128]
            ys_ref[1, pl.ds(i * 512 + j, 128, stride=4), :] = grad[:, 128:]

    @pl.loop(0, 16)
    def _(i):
        r = rows_of(i, 128)
        sg_ref[r, :128] = ys_ref[0, r, :].astype(BF16)
        sg_ref[r, 128:] = ys_ref[1, r, :].astype(BF16)


def embed(stamps, width):
    half = width // 2
    freqs = jnp.exp(-math.log(10000.0) * jnp.arange(half, dtype=F32) / half)
    angles = stamps.astype(F32)[:, None] * freqs[None, :]
    return jnp.concatenate([jnp.sin(angles), jnp.cos(angles)], axis=-1)


def moved(value, target):
    pairs = [(i, target(i // 8, i // 2 % 4, i % 2)) for i in range(16)]
    return lax.ppermute(value, "tm", pairs)


def summed(first, *others):
    total = first.astype(F32)
    for other in others:
        total = total + other.astype(F32)
    return total.astype(BF16)


def pieces(value):
    return jnp.moveaxis(value.reshape(value.shape[0], 16, -1), 1, 0)


def per_device(signal, timesteps, cotangent, conv_one, down_proj, conv_two, time_proj):
    x, cot = signal[0], cotangent[0]
    forward = [(i, i + 1) for i in range(15)]
    backward = [(i + 1, i) for i in range(15)]
    left = lax.ppermute(jnp.concatenate([x[-8:], cot[-8:]], axis=1), "tm", forward)
    right = lax.ppermute(jnp.concatenate([x[:8], cot[:8]], axis=1), "tm", backward)
    emb_row = embed(timesteps, EMB)
    temb = jnp.dot(emb_row, time_proj.astype(F32), precision=lax.Precision.HIGHEST)
    tm = lax.axis_index("tm")
    idx = jnp.stack(
        [tm % 2, tm // 2 % 4, tm // 8, (tm == 0).astype(jnp.int32), (tm == 15).astype(jnp.int32)]
    ).astype(jnp.int32)
    smem = pl.BlockSpec(memory_space=pltpu.SMEM)
    vmem = pl.BlockSpec(memory_space=pltpu.VMEM)
    sds = jax.ShapeDtypeStruct
    ga, gb, dc, ab, co = pl.pallas_call(
        grads_kernel,
        name="grads",
        in_specs=[smem] + [vmem] * 8,
        out_specs=[vmem] * 5,
        out_shape=[
            sds((16, 32, 3 * CB), BF16),
            sds((16, 48, 4 * CA), BF16),
            sds((E, CB), BF16),
            sds((E, CB), BF16),
            sds((E, CB), BF16),
        ],
        scratch_shapes=[
            pltpu.VMEM((2, 4 * E, 128), F32),
            pltpu.VMEM((E, 6 * CA), BF16),
            pltpu.VMEM((E, 4 * CA), BF16),
            pltpu.VMEM((E, 3 * CB), BF16),
            pltpu.VMEM((E, 3 * CB), BF16),
            pltpu.VMEM((E, CB), F32),
            pltpu.VMEM((E, CB), F32),
            pltpu.VMEM((E, 128), F32),
            pltpu.VMEM((E, 4 * CA), BF16),
        ],
        cost_estimate=pl.CostEstimate(
            flops=4_900_000_000, bytes_accessed=10_000_000, transcendentals=1_600_000
        ),
        compiler_params=pltpu.CompilerParams(vmem_limit_bytes=48 << 20),
    )(idx, x, left, right, cot, temb, conv_one, down_proj, conv_two)

    def swap_core(v):
        return moved(v, lambda y, xx, c: y * 8 + xx * 2 + 1 - c)

    ra, rb = swap_core(ga[8:]), swap_core(gb[8:])
    encoded, signal_grad, dtemb = pl.pallas_call(
        outputs_kernel,
        name="outputs",
        in_specs=[vmem] * 8,
        out_specs=[vmem] * 3,
        out_shape=[sds((S, CB), BF16), sds((4 * S, CA), BF16), sds((8, CA), F32)],
        scratch_shapes=[
            pltpu.VMEM((2, 4 * S, 128), F32),
            pltpu.VMEM((2, 4 * S, 128), F32),
            pltpu.VMEM((E, 3 * CB), BF16),
            pltpu.VMEM((E, 4 * CA), F32),
            pltpu.VMEM((E, 6 * CA), BF16),
        ],
        cost_estimate=pl.CostEstimate(
            flops=2_150_000_000, bytes_accessed=7_000_000, transcendentals=600_000
        ),
        compiler_params=pltpu.CompilerParams(vmem_limit_bytes=48 << 20),
    )(x, co, ab, dc, temb, conv_one, down_proj, conv_two)

    def ring_x(v):
        return [
            moved(
                v[2 * k : 2 * k + 2], lambda y, xx, c, k=k: y * 8 + (xx + k) % 4 * 2 + c
            )
            for k in (1, 2, 3)
        ]

    def swap_y(v):
        return moved(v, lambda y, xx, c: (1 - y) * 8 + xx * 2 + c)

    ga, gb = summed(ga[:8], ra), summed(gb[:8], rb)
    ra, rb = ring_x(ga), ring_x(gb)
    ga, gb = summed(ga[:2], *ra), summed(gb[:2], *rb)
    ga, gb = summed(ga[0], swap_y(ga[1])), summed(gb[0], swap_y(gb[1]))

    scaling = 1.0 / math.sqrt(16 * 32768)
    cols = lax.all_to_all(dtemb.sum(0).reshape(16, 16), "tm", 0, 0, tiled=True).sum(0)
    time = (emb_row[0].reshape(16, 16)[:, None, :] * cols[None, :, None] * scaling).astype(BF16)

    two, down, one = pieces(ga), pieces(gb[:32]), pieces(gb[32:, : 3 * CA])
    lines = jnp.concatenate(
        [v.reshape(16, -1) for v in (two, down, one, time)], axis=1
    ).reshape(16, 48, 128)
    line = lax.all_to_all(lines, "dp", 0, 0, tiled=True).astype(F32).sum(0).reshape(-1)
    outs, at = [], 0
    for n, k in ((32, 96), (32, 64), (16, 48), (16, 16)):
        outs.append(line[at : at + n * k].reshape(n, k).T)
        at += n * k
    return encoded[None], signal_grad[None], outs[2], outs[1], outs[0], outs[3]


def solution(mesh):
    return jax.shard_map(
        per_device,
        mesh=mesh,
        in_specs=(P("dp", "tm", None), P("dp"), P("dp", "tm", None), P(), P(), P(), P()),
        out_specs=(
            P("dp", "tm", None),
            P("dp", "tm", None),
            P("dp", "tm"),
            P("dp", "tm"),
            P("dp", "tm"),
            P("dp", "tm"),
        ),
        check_vma=False,
    )
```

time: 227 us -> 111 us (0.49); the launches traced: 223 us -> 110 us
  waiting for transfers between devices: 95.5 us -> 25.6 us
  matrix products: 25 us -> 0.14 us
  Pallas kernels: 0 us -> 23.8 us
  local copies, waits for them, and re-layouts: 31.5 us -> 13.6 us
  blocking collectives: 0 us -> 17 us
  other arithmetic: 20.1 us -> 3.32 us
  between operations: 15.3 us -> 1.61 us
  starting transfers between devices: 35.5 us -> 24.9 us
    reduce_scatter x1 -> x0, waiting for transfers between devices: 78.7 us -> none  [sum_together(): lax.psum_scatter(lines, axis, tiled=True).reshape(-1)]
    dot_general x10 -> x1, matrix products: 25 us -> 0.14 us  [per_device(): jnp.dot(emb_row, time_proj.astype(F32), precision=lax.Precision.HIGHEST)]
    pallas_call x0 -> x2, Pallas kernels: none -> 23.8 us  [the longest x1 15.7 us: per_device(): pl.pallas_call(grads_kernel, name='grads', in_specs=[smem] + [vmem] * 8,...]
    ppermute x8 -> x12, waiting for transfers between devices: 0.02 us -> 18.3 us  [the longest x10 16.2 us: moved(): return lax.ppermute(value, 'tm', pairs)]
    all_to_all x0 -> x1, blocking collectives: none -> 17 us  [per_device(): lax.all_to_all(lines, 'dp', 0, 0, tiled=True).astype(F32).sum(0).reshape(-1)]
    reduce_sum x6 -> x3, other arithmetic: 10.2 us -> 0.07 us  [the longest x1 0.03 us: per_device(): lax.all_to_all(lines, 'dp', 0, 0, tiled=True).astype(F32).sum(0).reshape(-1)]
    all_to_all x3 -> x1, waiting for transfers between devices: 16.7 us -> 7.28 us  [per_device(): lax.all_to_all(dtemb.sum(0).reshape(16, 16), 'tm', 0, 0, tiled=True).sum(0)]
    another operation x5 -> x1, local copies, waits for them, and re-layouts: 9.27 us -> 0.13 us  [per_device(): jnp.stack([tm % 2, tm // 2 % 4, tm // 8, (tm == 0).astype(jnp.int32), (tm...]
  transfers between devices with their start and end apart: 12 -> 13, of which waited for: 4 -> 5; matrix products, arithmetic and copies ran while one was open for 21% -> 5% of each run, Pallas kernels for 0% -> 7%
where the time goes in v1:
time: 111 us; the launch traced here: 110 us
  waiting for transfers between devices  25.6 us (23%)
  starting transfers between devices  24.9 us (22%)
  Pallas kernels  23.8 us (21%)
  blocking collectives  17 us (15%)
  local copies, waits for them, and re-layouts  13.6 us (12%)
  other arithmetic  3.32 us (3%)
  between operations  1.61 us (1%)
    all_to_all x1, blocking collectives, per_device(): lax.all_to_all(lines, 'dp', 0, 0, tiled=True).astype(F32).sum(0).reshape(-1)  17 us
    ppermute x10, waiting for transfers between devices, moved(): return lax.ppermute(value, 'tm', pairs)  16.2 us
    pallas_call x1, Pallas kernels, per_device(): pl.pallas_call(grads_kernel, name='grads', in_specs=[smem] + [vmem] * 8,...  15.7 us
    ppermute x10, starting transfers between devices, moved(): return lax.ppermute(value, 'tm', pairs)  12.5 us
    all_to_all x1, starting transfers between devices, per_device(): lax.all_to_all(dtemb.sum(0).reshape(16, 16), 'tm', 0, 0, tiled=True).sum(0)  9.44 us
    pallas_call x1, Pallas kernels, per_device(): pl.pallas_call(outputs_kernel, name='outputs', in_specs=[vmem] * 8, out_s...  8.08 us
    all_to_all x1, waiting for transfers between devices, per_device(): lax.all_to_all(dtemb.sum(0).reshape(16, 16), 'tm', 0, 0, tiled=True).sum(0)  7.28 us
    unnamed x22, local copies, waits for them, and re-layouts  5.22 us
  transfers between devices with their start and end apart: 13, of which 5 were waited for; matrix products, arithmetic and copies ran while one was open for 5% of the time, Pallas kernels for 7%

profile of v1, /device:TPU:32, one launch (start us, length us, event | category | flops | bytes accessed | tf_op | source)
XLA Modules:
  0.0 110.0 jit_solution(3782474978048844365)
XLA Ops:
  2.1 1.7 %collective-permute-start = (bf16[8,768]{1,0:T(8,128)(2,1)S(1)}, bf16[8,768]{1,0:T(8,128)(2,1)S(1)}, u32[]{:S(2)}, u32[]{:S(2)}) collective-permute-start(bf16[8,768]{1,0:T(8,128)(2,1)S(1)} %pad_maximum_fusion), channel_id=1, source_target_pairs={{0,1},{1,2},{2,3},{3,4},{4,5},{5,6},{6,7},{7,8},{8,9},{9,10},{10,1... | collective-permute-start | bytes 36872 | tf_op jit(solution)/shard_map/ppermute | solution.py:264
  3.9 1.3 %collective-permute-start.1 = (bf16[8,768]{1,0:T(8,128)(2,1)S(1)}, bf16[8,768]{1,0:T(8,128)(2,1)S(1)}, u32[]{:S(2)}, u32[]{:S(2)}) collective-permute-start(bf16[8,768]{1,0:T(8,128)(2,1)S(1)} %pad_maximum_fusion.1), channel_id=1, source_target_pairs={{1,0},{2,1},{3,2},{4,3},{5,4},{6,5},{7,6},{8,7},{9,8},{10,9},{11,1... | collective-permute-start | bytes 36872 | tf_op jit(solution)/shard_map/ppermute | solution.py:265
  6.1 2.1 %collective-permute-done.1.right_ref = bf16[8,768]{1,0:T(8,128)(2,1)S(1)} collective-permute-done((bf16[8,768]{1,0:T(8,128)(2,1)S(1)}, bf16[8,768]{1,0:T(8,128)(2,1)S(1)}, u32[]{:S(2)}, u32[]{:S(2)}) %collective-permute-start.1) | collective-permute-done | bytes 12320 | tf_op jit(solution)/shard_map/ppermute | solution.py:265
  8.2 1.0 copy-done.1
  9.3 1.2 %copy-done.2 = bf16[1,2048,256]{2,1,0:T(8,128)(2,1)S(1)} copy-done((bf16[1,2048,256]{2,1,0:T(8,128)(2,1)S(1)}, bf16[1,2048,256]{2,1,0:T(8,128)(2,1)}, u32[]{:S(2)}) %copy-start.2) | copy-done | bytes 1048600
  10.5 1.2 %copy-done.4 = bf16[1024,512]{1,0:T(8,128)(2,1)S(1)} copy-done((bf16[1024,512]{1,0:T(8,128)(2,1)S(1)}, bf16[1024,512]{1,0:T(8,128)(2,1)}, u32[]{:S(2)}) %copy-start.4) | copy-done | bytes 1048600
  12.7 15.7 %grads.1 = (bf16[16,32,1536]{2,1,0:T(8,128)(2,1)}, bf16[16,48,1024]{2,1,0:T(8,128)(2,1)}, bf16[528,512]{1,0:T(8,128)(2,1)S(1)}, bf16[528,512]{1,0:T(8,128)(2,1)S(1)}, bf16[528,512]{1,0:T(8,128)(2,1)S(1)}) custom-call(s32[5]{0:T(128)S(1)} %stack.31.idx_ref, bf16[2048,256]{1,0:T(8,128)(2,1)S(1)} %bitcast.56, bf16[8,768]{1,0:T(8,128)(2,1)S(1)} %collective-permute-done.left_ref, ...), custom_call_target="tpu_custom_call" | custom-call | flops 4899999744 | bytes 10000000 | tf_op jit(solution)/shard_map/grads/pallas_call | solution.py:275
  28.4 1.3 %slice.111 = bf16[8,48,1024]{2,1,0:T(8,128)(2,1)S(1)} slice(bf16[16,48,1024]{2,1,0:T(8,128)(2,1)} %get-tuple-element.20), slice={[8:16], [0:48], [0:1024]} | slice | bytes 1572864 | tf_op jit(solution)/shard_map/slice | solution.py:307
  29.7 2.5 %collective-permute-start.7 = (bf16[8,48,1024]{2,1,0:T(8,128)(2,1)S(1)}, bf16[8,48,1024]{2,1,0:T(8,128)(2,1)}, u32[]{:S(2)}, u32[]{:S(2)}) collective-permute-start(bf16[8,48,1024]{2,1,0:T(8,128)(2,1)S(1)} %slice.111), channel_id=1, source_target_pairs={{0,1},{1,0},{2,3},{3,2},{4,5},{5,4},{6,7},{7,6},{8,9},{9,8},{10,11... | collective-permute-start | bytes 2359304 | tf_op jit(solution)/shard_map/ppermute | solution.py:246
  32.3 1.2 %slice.103 = bf16[8,32,1536]{2,1,0:T(8,128)(2,1)S(1)} slice(bf16[16,32,1536]{2,1,0:T(8,128)(2,1)} %get-tuple-element.19), slice={[8:16], [0:32], [0:1536]} | slice | bytes 1572864 | tf_op jit(solution)/shard_map/slice | solution.py:307
  33.6 8.1 %outputs.1 = (bf16[512,512]{1,0:T(8,128)(2,1)}, bf16[2048,256]{1,0:T(8,128)(2,1)}, f32[8,256]{1,0:T(8,128)S(1)}) custom-call(bf16[2048,256]{1,0:T(8,128)(2,1)S(1)} %bitcast.57, bf16[528,512]{1,0:T(8,128)(2,1)S(1)} %get-tuple-element.14.co_ref, bf16[528,512]{1,0:T(8,128)(2,1)S(1)} %get-tuple-element.15.ab_ref, bf16[528,512]{1,0:T(8,128)(2,1)S(1)} %get-tuple-element.16.dc_ref, ...), custom_call_target="tpu_custom_call" | custom-call | flops 2150000128 | bytes 7000000 | tf_op jit(solution)/shard_map/outputs/pallas_call | solution.py:308
  42.4 9.4 %all-to-all-start = ((f32[16,1,16]{2,1,0:T(1,128)}), f32[16,1,16]{2,1,0:T(1,128)S(1)}, u32[]{:S(2)}, u32[]{:S(2)}) async-start(f32[16,1,16]{2,1,0:T(1,128)} %all_to_all.9), calls=%async_computation | async-start | bytes 16384 | tf_op jit(solution)/shard_map/all_to_all | solution.py:344
  52.1 7.3 %all-to-all-done = f32[16,1,16]{2,1,0:T(1,128)S(1)} async-done(((f32[16,1,16]{2,1,0:T(1,128)}), f32[16,1,16]{2,1,0:T(1,128)S(1)}, u32[]{:S(2)}, u32[]{:S(2)}) %all-to-all-start) | async-done | bytes 1056 | tf_op jit(solution)/shard_map/all_to_all | solution.py:344
  59.6 1.6 %add_convert_fusion = bf16[8,48,1024]{2,1,0:T(8,128)(2,1)S(1)} fusion(bf16[8,48,1024]{2,1,0:T(8,128)(2,1)} %collective-permute-done.7, bf16[16,48,1024]{2,1,0:T(8,128)(2,1)S(1)} %copy-done.9), kind=kLoop, calls=%fused_computation | loop fusion | flops 1572864 | bytes 2359296 | tf_op jit(solution)/shard_map/convert_element_type | solution.py:253
  61.2 1.3 %collective-permute-start.10 = (bf16[2,48,1024]{2,1,0:T(8,128)(2,1)S(1)}, bf16[2,48,1024]{2,1,0:T(8,128)(2,1)S(1)}, u32[]{:S(2)}, u32[]{:S(2)}) collective-permute-start(bf16[2,48,1024]{2,1,0:T(8,128)(2,1)S(1)} %get-tuple-element.46), channel_id=1, source_target_pairs={{0,6},{1,7},{2,0},{3,1},{4,2},{5,3},{6,4},{7,5},{8,14},{9,15},{10,... | collective-permute-start | bytes 589832 | tf_op jit(solution)/shard_map/ppermute | solution.py:246
  63.3 1.2 %collective-permute-start.9 = (bf16[2,48,1024]{2,1,0:T(8,128)(2,1)S(1)}, bf16[2,48,1024]{2,1,0:T(8,128)(2,1)S(1)}, u32[]{:S(2)}, u32[]{:S(2)}) collective-permute-start(bf16[2,48,1024]{2,1,0:T(8,128)(2,1)S(1)} %get-tuple-element.47), channel_id=1, source_target_pairs={{0,4},{1,5},{2,6},{3,7},{4,0},{5,1},{6,2},{7,3},{8,12},{9,13},{10,... | collective-permute-start | bytes 589832 | tf_op jit(solution)/shard_map/ppermute | solution.py:246
  64.5 1.3 %add_convert_fusion.1 = bf16[8,32,1536]{2,1,0:T(8,128)(2,1)S(1)} fusion(bf16[8,32,1536]{2,1,0:T(8,128)(2,1)} %collective-permute-done.2, bf16[16,32,1536]{2,1,0:T(8,128)(2,1)S(1)} %copy-done.8), kind=kLoop, calls=%fused_computation.1 | loop fusion | flops 1572864 | bytes 2359296 | tf_op jit(solution)/shard_map/convert_element_type | solution.py:253
  65.8 2.1 %collective-permute-start.3 = (bf16[2,32,1536]{2,1,0:T(8,128)(2,1)S(1)}, bf16[2,32,1536]{2,1,0:T(8,128)(2,1)S(1)}, u32[]{:S(2)}, u32[]{:S(2)}) collective-permute-start(bf16[2,32,1536]{2,1,0:T(8,128)(2,1)S(1)} %get-tuple-element.42), channel_id=1, source_target_pairs={{0,2},{1,3},{2,4},{3,5},{4,6},{5,7},{6,0},{7,1},{8,10},{9,11},{10,... | collective-permute-start | bytes 589832 | tf_op jit(solution)/shard_map/ppermute | solution.py:246
  68.0 1.5 %collective-permute-start.4 = (bf16[2,32,1536]{2,1,0:T(8,128)(2,1)S(1)}, bf16[2,32,1536]{2,1,0:T(8,128)(2,1)S(1)}, u32[]{:S(2)}, u32[]{:S(2)}) collective-permute-start(bf16[2,32,1536]{2,1,0:T(8,128)(2,1)S(1)} %get-tuple-element.44), channel_id=1, source_target_pairs={{0,4},{1,5},{2,6},{3,7},{4,0},{5,1},{6,2},{7,3},{8,12},{9,13},{10,... | collective-permute-start | bytes 589832 | tf_op jit(solution)/shard_map/ppermute | solution.py:246
  69.4 1.7 %collective-permute-start.5 = (bf16[2,32,1536]{2,1,0:T(8,128)(2,1)S(1)}, bf16[2,32,1536]{2,1,0:T(8,128)(2,1)S(1)}, u32[]{:S(2)}, u32[]{:S(2)}) collective-permute-start(bf16[2,32,1536]{2,1,0:T(8,128)(2,1)S(1)} %get-tuple-element.43), channel_id=1, source_target_pairs={{0,6},{1,7},{2,0},{3,1},{4,2},{5,3},{6,4},{7,5},{8,14},{9,15},{10,... | collective-permute-start | bytes 589832 | tf_op jit(solution)/shard_map/ppermute | solution.py:246
  71.1 4.5 %collective-permute-done.8 = bf16[2,48,1024]{2,1,0:T(8,128)(2,1)S(1)} collective-permute-done((bf16[2,48,1024]{2,1,0:T(8,128)(2,1)S(1)}, bf16[2,48,1024]{2,1,0:T(8,128)(2,1)S(1)}, u32[]{:S(2)}, u32[]{:S(2)}) %collective-permute-start.8) | collective-permute-done | bytes 196640 | tf_op jit(solution)/shard_map/ppermute | solution.py:246
  76.4 6.2 %collective-permute-done.3 = bf16[2,32,1536]{2,1,0:T(8,128)(2,1)S(1)} collective-permute-done((bf16[2,32,1536]{2,1,0:T(8,128)(2,1)S(1)}, bf16[2,32,1536]{2,1,0:T(8,128)(2,1)S(1)}, u32[]{:S(2)}, u32[]{:S(2)}) %collective-permute-start.3) | collective-permute-done | bytes 196640 | tf_op jit(solution)/shard_map/ppermute | solution.py:246
  83.5 5.5 %collective-permute-done.6 = bf16[32,1536]{1,0:T(8,128)(2,1)S(1)} collective-permute-done((bf16[32,1536]{1,0:T(8,128)(2,1)S(1)}, bf16[32,1536]{1,0:T(8,128)(2,1)S(1)}, u32[]{:S(2)}, u32[]{:S(2)}) %collective-permute-start.6) | collective-permute-done | bytes 98336 | tf_op jit(solution)/shard_map/ppermute | solution.py:246
  90.1 17.0 %all_to_all.14 = bf16[16,48,128]{2,1,0:T(8,128)(2,1)S(1)} all-to-all(bf16[16,48,128]{2,1,0:T(8,128)(2,1)S(1)} %bitcast.58), channel_id=1, replica_groups=mesh['dp'=16,'tm'=16] {'dp'}, dimensions={0} | all-to-all | bytes 393216 | tf_op jit(solution)/shard_map/all_to_all | solution.py:351
  (77 shorter events, 10.4 us)
Async XLA Ops:
  0.6 5.2 %copy-start = (bf16[256,256]{1,0:T(8,128)(2,1)S(1)}, bf16[256,256]{1,0:T(8,128)(2,1)}, u32[]{:S(2)}) copy-start(bf16[256,256]{1,0:T(8,128)(2,1)} %param.13) | copy-start | bytes 393220
  2.1 4.0 %collective-permute-start = (bf16[8,768]{1,0:T(8,128)(2,1)S(1)}, bf16[8,768]{1,0:T(8,128)(2,1)S(1)}, u32[]{:S(2)}, u32[]{:S(2)}) collective-permute-start(bf16[8,768]{1,0:T(8,128)(2,1)S(1)} %pad_maximum_fusion), channel_id=1, source_target_pairs={{0,1},{1,2},{2,3},{3,4},{4,5},{5,6},{6,7},{7,8},{8,9},{9,10},{10,1... | collective-permute-start | bytes 36872 | tf_op jit(solution)/shard_map/ppermute | solution.py:264
  3.9 4.3 %collective-permute-start.1 = (bf16[8,768]{1,0:T(8,128)(2,1)S(1)}, bf16[8,768]{1,0:T(8,128)(2,1)S(1)}, u32[]{:S(2)}, u32[]{:S(2)}) collective-permute-start(bf16[8,768]{1,0:T(8,128)(2,1)S(1)} %pad_maximum_fusion.1), channel_id=1, source_target_pairs={{1,0},{2,1},{3,2},{4,3},{5,4},{6,5},{7,6},{8,7},{9,8},{10,9},{11,1... | collective-permute-start | bytes 36872 | tf_op jit(solution)/shard_map/ppermute | solution.py:265
  8.2 1.0 copy-start.1
  9.3 1.2 %copy-start.2 = (bf16[1,2048,256]{2,1,0:T(8,128)(2,1)S(1)}, bf16[1,2048,256]{2,1,0:T(8,128)(2,1)}, u32[]{:S(2)}) copy-start(bf16[1,2048,256]{2,1,0:T(8,128)(2,1)} %param.7) | copy-start | bytes 3145732
  10.5 1.2 %copy-start.4 = (bf16[1024,512]{1,0:T(8,128)(2,1)S(1)}, bf16[1024,512]{1,0:T(8,128)(2,1)}, u32[]{:S(2)}) copy-start(bf16[1024,512]{1,0:T(8,128)(2,1)} %down_ref.3) | copy-start | bytes 3145732
  11.7 1.0 copy-start.6
  28.4 5.2 %copy-start.3 = (bf16[1536,512]{1,0:T(8,128)(2,1)S(1)}, bf16[1536,512]{1,0:T(8,128)(2,1)}, u32[]{:S(2)}) copy-start(bf16[1536,512]{1,0:T(8,128)(2,1)} %two_ref.3) | copy-start | bytes 4718596
  28.4 5.2 %copy-start.5 = (bf16[1024,512]{1,0:T(8,128)(2,1)S(1)}, bf16[1024,512]{1,0:T(8,128)(2,1)}, u32[]{:S(2)}) copy-start(bf16[1024,512]{1,0:T(8,128)(2,1)} %down_ref.3) | copy-start | bytes 3145732
  28.4 5.2 %copy-start.7 = (bf16[768,256]{1,0:T(8,128)(2,1)S(1)}, bf16[768,256]{1,0:T(8,128)(2,1)}, u32[]{:S(2)}) copy-start(bf16[768,256]{1,0:T(8,128)(2,1)} %one_ref.3) | copy-start | bytes 1179652
  29.7 29.8 %collective-permute-start.7 = (bf16[8,48,1024]{2,1,0:T(8,128)(2,1)S(1)}, bf16[8,48,1024]{2,1,0:T(8,128)(2,1)}, u32[]{:S(2)}, u32[]{:S(2)}) collective-permute-start(bf16[8,48,1024]{2,1,0:T(8,128)(2,1)S(1)} %slice.111), channel_id=1, source_target_pairs={{0,1},{1,0},{2,3},{3,2},{4,5},{5,4},{6,7},{7,6},{8,9},{9,8},{10,11... | collective-permute-start | bytes 2359304 | tf_op jit(solution)/shard_map/ppermute | solution.py:246
  33.5 31.0 %collective-permute-start.2 = (bf16[8,32,1536]{2,1,0:T(8,128)(2,1)S(1)}, bf16[8,32,1536]{2,1,0:T(8,128)(2,1)}, u32[]{:S(2)}, u32[]{:S(2)}) collective-permute-start(bf16[8,32,1536]{2,1,0:T(8,128)(2,1)S(1)} %slice.103), channel_id=1, source_target_pairs={{0,1},{1,0},{2,3},{3,2},{4,5},{5,4},{6,7},{7,6},{8,9},{9,8},{10,11... | collective-permute-start | bytes 2359304 | tf_op jit(solution)/shard_map/ppermute | solution.py:246
  33.6 26.0 %copy-start.9 = (bf16[16,48,1024]{2,1,0:T(8,128)(2,1)S(1)}, bf16[16,48,1024]{2,1,0:T(8,128)(2,1)}, u32[]{:S(2)}) copy-start(bf16[16,48,1024]{2,1,0:T(8,128)(2,1)} %get-tuple-element.20) | copy-start | bytes 4718596
  42.4 17.0 %all-to-all-start = ((f32[16,1,16]{2,1,0:T(1,128)}), f32[16,1,16]{2,1,0:T(1,128)S(1)}, u32[]{:S(2)}, u32[]{:S(2)}) async-start(f32[16,1,16]{2,1,0:T(1,128)} %all_to_all.9), calls=%async_computation | async-start | bytes 16384 | tf_op jit(solution)/shard_map/all_to_all | solution.py:344
  59.5 4.9 %copy-start.8 = (bf16[16,32,1536]{2,1,0:T(8,128)(2,1)S(1)}, bf16[16,32,1536]{2,1,0:T(8,128)(2,1)}, u32[]{:S(2)}) copy-start(bf16[16,32,1536]{2,1,0:T(8,128)(2,1)} %get-tuple-element.19) | copy-start | bytes 4718596
  61.2 8.3 %collective-permute-start.10 = (bf16[2,48,1024]{2,1,0:T(8,128)(2,1)S(1)}, bf16[2,48,1024]{2,1,0:T(8,128)(2,1)S(1)}, u32[]{:S(2)}, u32[]{:S(2)}) collective-permute-start(bf16[2,48,1024]{2,1,0:T(8,128)(2,1)S(1)} %get-tuple-element.46), channel_id=1, source_target_pairs={{0,6},{1,7},{2,0},{3,1},{4,2},{5,3},{6,4},{7,5},{8,14},{9,15},{10,... | collective-permute-start | bytes 589832 | tf_op jit(solution)/shard_map/ppermute | solution.py:246
  62.4 13.2 %collective-permute-start.8 = (bf16[2,48,1024]{2,1,0:T(8,128)(2,1)S(1)}, bf16[2,48,1024]{2,1,0:T(8,128)(2,1)S(1)}, u32[]{:S(2)}, u32[]{:S(2)}) collective-permute-start(bf16[2,48,1024]{2,1,0:T(8,128)(2,1)S(1)} %get-tuple-element.45), channel_id=1, source_target_pairs={{0,2},{1,3},{2,4},{3,5},{4,6},{5,7},{6,0},{7,1},{8,10},{9,11},{10,... | collective-permute-start | bytes 589832 | tf_op jit(solution)/shard_map/ppermute | solution.py:246
  63.3 12.4 %collective-permute-start.9 = (bf16[2,48,1024]{2,1,0:T(8,128)(2,1)S(1)}, bf16[2,48,1024]{2,1,0:T(8,128)(2,1)S(1)}, u32[]{:S(2)}, u32[]{:S(2)}) collective-permute-start(bf16[2,48,1024]{2,1,0:T(8,128)(2,1)S(1)} %get-tuple-element.47), channel_id=1, source_target_pairs={{0,4},{1,5},{2,6},{3,7},{4,0},{5,1},{6,2},{7,3},{8,12},{9,13},{10,... | collective-permute-start | bytes 589832 | tf_op jit(solution)/shard_map/ppermute | solution.py:246
  65.8 16.8 %collective-permute-start.3 = (bf16[2,32,1536]{2,1,0:T(8,128)(2,1)S(1)}, bf16[2,32,1536]{2,1,0:T(8,128)(2,1)S(1)}, u32[]{:S(2)}, u32[]{:S(2)}) collective-permute-start(bf16[2,32,1536]{2,1,0:T(8,128)(2,1)S(1)} %get-tuple-element.42), channel_id=1, source_target_pairs={{0,2},{1,3},{2,4},{3,5},{4,6},{5,7},{6,0},{7,1},{8,10},{9,11},{10,... | collective-permute-start | bytes 589832 | tf_op jit(solution)/shard_map/ppermute | solution.py:246
  68.0 14.7 %collective-permute-start.4 = (bf16[2,32,1536]{2,1,0:T(8,128)(2,1)S(1)}, bf16[2,32,1536]{2,1,0:T(8,128)(2,1)S(1)}, u32[]{:S(2)}, u32[]{:S(2)}) collective-permute-start(bf16[2,32,1536]{2,1,0:T(8,128)(2,1)S(1)} %get-tuple-element.44), channel_id=1, source_target_pairs={{0,4},{1,5},{2,6},{3,7},{4,0},{5,1},{6,2},{7,3},{8,12},{9,13},{10,... | collective-permute-start | bytes 589832 | tf_op jit(solution)/shard_map/ppermute | solution.py:246
  69.4 13.2 %collective-permute-start.5 = (bf16[2,32,1536]{2,1,0:T(8,128)(2,1)S(1)}, bf16[2,32,1536]{2,1,0:T(8,128)(2,1)S(1)}, u32[]{:S(2)}, u32[]{:S(2)}) collective-permute-start(bf16[2,32,1536]{2,1,0:T(8,128)(2,1)S(1)} %get-tuple-element.43), channel_id=1, source_target_pairs={{0,6},{1,7},{2,0},{3,1},{4,2},{5,3},{6,4},{7,5},{8,14},{9,15},{10,... | collective-permute-start | bytes 589832 | tf_op jit(solution)/shard_map/ppermute | solution.py:246
  75.8 7.6 %collective-permute-start.11 = (bf16[48,1024]{1,0:T(8,128)(2,1)S(1)}, bf16[48,1024]{1,0:T(8,128)(2,1)S(1)}, u32[]{:S(2)}, u32[]{:S(2)}) collective-permute-start(bf16[48,1024]{1,0:T(8,128)(2,1)S(1)} %slice_bitcast_fusion), channel_id=1, source_target_pairs={{0,8},{1,9},{2,10},{3,11},{4,12},{5,13},{6,14},{7,15},{8,0},{9,1},... | collective-permute-start | bytes 294920 | tf_op jit(solution)/shard_map/ppermute | solution.py:246
  82.8 6.2 %collective-permute-start.6 = (bf16[32,1536]{1,0:T(8,128)(2,1)S(1)}, bf16[32,1536]{1,0:T(8,128)(2,1)S(1)}, u32[]{:S(2)}, u32[]{:S(2)}) collective-permute-start(bf16[32,1536]{1,0:T(8,128)(2,1)S(1)} %slice_bitcast_fusion.2), channel_id=1, source_target_pairs={{0,8},{1,9},{2,10},{3,11},{4,12},{5,13},{6,14},{7,15},{8,0},{9,1},... | collective-permute-start | bytes 294920 | tf_op jit(solution)/shard_map/ppermute | solution.py:246

commit v2 on v1

v2 whole, which is shorter than its diff:
```python
import math

import jax
import jax.numpy as jnp
from jax import lax
from jax.experimental import pallas as pl
from jax.experimental.pallas import tpu as pltpu
from jax.sharding import PartitionSpec as P


EPS = 1e-06
CA, CB, EMB = 256, 512, 256
S = 512
E = 528
F32, BF16 = jnp.float32, jnp.bfloat16
AXES = ("dp", "tm")
NT = (((1,), (1,)), ((), ()))


def dot(a, b):
    return jnp.dot(a, b, preferred_element_type=F32)


def dot_nt(a, b):
    return lax.dot_general(a, b, NT, preferred_element_type=F32)


def rows_of(i, size):
    return pl.ds(pl.multiple_of(i * size, 16), size)


def sigmoid(v):
    return 1.0 / (1.0 + jnp.exp(-v))


def inside(idx_ref, start, size, margin):
    row = lax.broadcasted_iota(jnp.int32, (size, 1), 0) + start
    past = jnp.logical_and(row >= S, row < S + margin)
    before = row >= E - margin
    off = jnp.logical_or(
        jnp.logical_and(past, idx_ref[4] == 1), jnp.logical_and(before, idx_ref[3] == 1)
    )
    return jnp.where(off, 0.0, 1.0)


def phase(ref, start, size):
    return jnp.concatenate([ref[h, pl.ds(start, size, stride=4), :] for h in range(2)], axis=1)


def later(v):
    return pltpu.roll(v, 1, 0)


def sooner(v):
    return pltpu.roll(v, v.shape[0] - 1, 0)


def places(idx_ref, xx, y):
    apart = xx ^ idx_ref[1]
    side = y ^ idx_ref[2]
    first = jnp.where(apart == 3, 1, jnp.where(apart == 0, 0, apart + 1))
    second = jnp.where(apart < 2, apart, 5 - apart)
    return first * 2 + side, 8 + second * 2 + side


def put(idx_ref, keep_ref, send_ref, xx, y, rows, even, odd, at=0):
    core, half = idx_ref[0], keep_ref.shape[2]
    keep = jnp.where(core == 0, even, odd).astype(BF16)
    send = jnp.where(core == 0, odd, even).astype(BF16)
    for h, where in enumerate(places(idx_ref, xx, y)):
        low, high = max(at, h * half), min(at + even.shape[1], (h + 1) * half)
        if low < high:
            lanes = slice(low - h * half, high - h * half)
            keep_ref[where, rows, lanes] = keep[:, low - at : high - at]
            send_ref[where, rows, lanes] = send[:, low - at : high - at]


def rms(v):
    return lax.rsqrt(jnp.mean(v * v, -1, keepdims=True) + EPS)


def turned(v):
    return v.astype(F32).T.astype(BF16)


def edges_kernel(x_ref, cot_ref, first_ref, last_ref, sem):
    copies = []
    for out, at in ((first_ref, 0), (last_ref, 1)):
        n = len(copies)
        rows = (pl.ds(0, 8), pl.ds(4 * S - 8, 8))[at]
        copies.append(pltpu.make_async_copy(x_ref.at[rows, :], out.at[:, :CA], sem.at[n]))
        rows = (pl.ds(0, 8), pl.ds(S - 8, 8))[at]
        copies.append(pltpu.make_async_copy(cot_ref.at[rows, :], out.at[:, CA:], sem.at[n + 1]))
    for copy in copies:
        copy.start()
    for copy in copies:
        copy.wait()


def act_kernel(
    x_ref, cot_ref, one_ref, down_ref, temb_ref,
    xp_ref, act_ref, cot_out, one_out, down_out,
    xs_ref, xb_ref, sem,
):
    parts = []
    for k in range(4):
        rows = pl.ds(512 * k, 512)
        parts.append(pltpu.make_async_copy(x_ref.at[rows, :], xb_ref.at[rows, :], sem.at[k]))
    whole = [
        pltpu.make_async_copy(one_ref, one_out, sem.at[4]),
        pltpu.make_async_copy(cot_ref, cot_out, sem.at[5]),
        pltpu.make_async_copy(down_ref, down_out, sem.at[6]),
    ]
    for copy in parts + whole:
        copy.start()
    for k in range(4):
        parts[k].wait()

        @pl.loop(0, 2)
        def _(n):
            i = 2 * k + n
            r = rows_of(i, 256)
            v = xb_ref[r, :].astype(F32)
            xs_ref[0, r, :] = v[:, :128]
            xs_ref[1, r, :] = v[:, 128:]
            r = rows_of(i, 64)
            for j in range(4):
                v = phase(xs_ref, i * 256 + j, 64)
                pre = v * rms(v) + temb_ref[...]
                lanes = slice(j * CA, (j + 1) * CA)
                xp_ref[r, lanes] = v.astype(BF16)
                act_ref[r, lanes] = (pre * sigmoid(pre)).astype(BF16)

    for copy in whole:
        copy.wait()


def forward_kernel(
    idx_ref, xp_ref, act_ref, left_ref, right_ref, cot_ref, temb_ref, one_ref, down_ref,
    keep_ref, send_ref, mw_ref, uw_ref, ab_ref, co_ref,
    xs_ref, xe_ref, ubw_ref,
):
    for h in range(2):
        lanes = slice(h * 128, (h + 1) * 128)
        xs_ref[h, :8, :] = right_ref[:, lanes].astype(F32)
        xs_ref[h, 8:56, :] = jnp.zeros((48, 128), F32)
        xs_ref[h, 56:, :] = left_ref[:, lanes].astype(F32)
    inner = inside(idx_ref, S, E - S, 2)
    for j in range(4):
        v = phase(xs_ref, j, 16)
        pre = v * rms(v) + temb_ref[...]
        xe_ref[:, j * CA : (j + 1) * CA] = v
        uw_ref[S:, (j + 1) * CA : (j + 2) * CA] = (pre * sigmoid(pre) * inner).astype(BF16)
    uw_ref[:S, CA : 5 * CA] = act_ref[...]
    uw_ref[:, :CA] = later(uw_ref[:, 4 * CA : 5 * CA].astype(F32)).astype(BF16)
    uw_ref[:, 5 * CA :] = sooner(uw_ref[:, CA : 2 * CA].astype(F32)).astype(BF16)

    def block(r, size, start, x_of):
        for j in range(4):
            lanes = slice(j * CA, (j + 1) * CA)
            hidden = dot(uw_ref[r, j * CA : (j + 3) * CA], one_ref[...])
            mw_ref[r, lanes] = (x_of(lanes) + hidden).astype(BF16)
        coarse = dot(mw_ref[r, :], down_ref[...]).astype(BF16)
        co_ref[r, :] = coarse
        c32 = coarse.astype(F32)
        normed = c32 * rms(c32)
        keep = inside(idx_ref, start, size, 1)
        ubw_ref[r, CB : 2 * CB] = (normed * sigmoid(normed) * keep).astype(BF16)

    @pl.loop(0, 2)
    def _(i):
        r = rows_of(i, 256)
        block(r, 256, i * 256, lambda lanes: xp_ref[r, lanes].astype(F32))

    block(slice(S, E), E - S, S, lambda lanes: xe_ref[:, lanes])

    act_b = ubw_ref[:, CB : 2 * CB]
    ab_ref[...] = act_b
    act_b = act_b.astype(F32)
    ubw_ref[:, :CB] = later(act_b).astype(BF16)
    ubw_ref[:, 2 * CB :] = sooner(act_b).astype(BF16)

    scaling = 1.0 / math.sqrt(16 * 32768)

    @pl.loop(0, 4)
    def _(i):
        at = turned(cot_ref[:, pl.ds(pl.multiple_of(i * 128, 128), 128)])
        two = dot(at, ubw_ref[:S, :]) * scaling
        for c in range(2):
            even, odd = two[64 * c : 64 * c + 32], two[64 * c + 32 : 64 * c + 64]
            put(idx_ref, keep_ref, send_ref, (2 * i + c) % 4, i // 2, slice(None), even, odd)


def coarse_kernel(
    idx_ref, co_ref, cot_ref, left_ref, right_ref, down_ref, two_ref,
    dc_ref, dh_ref, dm_ref, cw_ref,
):
    cot = jnp.concatenate(
        [
            cot_ref[...].astype(F32),
            right_ref[:2, CA:].astype(F32),
            jnp.zeros((12, CB), F32),
            left_ref[6:, CA:].astype(F32),
        ],
        axis=0,
    )
    cw_ref[:, CB : 2 * CB] = cot.astype(BF16)
    cw_ref[:, :CB] = sooner(cot).astype(BF16)
    cw_ref[:, 2 * CB :] = later(cot).astype(BF16)

    def block(r, size, start):
        back = dot_nt(cw_ref[r, :CB], two_ref[:CB, :])
        back += dot_nt(cw_ref[r, CB : 2 * CB], two_ref[CB : 2 * CB, :])
        back += dot_nt(cw_ref[r, 2 * CB :], two_ref[2 * CB :, :])
        c32 = co_ref[r, :].astype(F32)
        factor = rms(c32)
        normed = c32 * factor
        sig = sigmoid(normed)
        q = back * (sig * (1.0 + normed * (1.0 - sig)))
        m = jnp.mean(q * normed, -1, keepdims=True)
        grad = cw_ref[r, CB : 2 * CB].astype(F32) + factor * (q - normed * m)
        d_coarse = (grad * inside(idx_ref, start, size, 1)).astype(BF16)
        dc_ref[r, :] = d_coarse
        return dot_nt(d_coarse, down_ref[...])

    @pl.loop(0, 2)
    def _(i):
        r = rows_of(i, 256)
        dm = block(r, 256, i * 256)
        dm_ref[r, :] = dm
        dh_ref[r, :] = dm.astype(BF16)

    dh_ref[S:, :] = block(slice(S, E), E - S, S).astype(BF16)


def fine_kernel(
    idx_ref, xp_ref, dc_ref, dh_ref, dm_ref, mw_ref, uw_ref, temb_ref, emb_ref, one_ref,
    keep_ref, send_ref, sg_ref,
    dhw_ref, ys_ref, dt_ref,
):
    scaling = 1.0 / math.sqrt(16 * 32768)
    dhw_ref[:, CA : 5 * CA] = dh_ref[...]
    dhw_ref[:, :CA] = later(dh_ref[:, 3 * CA :].astype(F32)).astype(BF16)
    dhw_ref[:, 5 * CA :] = sooner(dh_ref[:, :CA].astype(F32)).astype(BF16)
    dt_ref[...] = jnp.zeros((8, CA), F32)

    @pl.loop(0, 4)
    def _(i):
        r = rows_of(i, 128)
        for j in range(4):
            lanes = slice(j * CA, (j + 1) * CA)
            back = dot_nt(dhw_ref[r, (j + 2) * CA : (j + 3) * CA], one_ref[:CA, :])
            back += dot_nt(dhw_ref[r, (j + 1) * CA : (j + 2) * CA], one_ref[CA : 2 * CA, :])
            back += dot_nt(dhw_ref[r, lanes], one_ref[2 * CA :, :])
            v = xp_ref[r, lanes].astype(F32)
            factor = rms(v)
            normed = v * factor
            pre = normed + temb_ref[...]
            sig = sigmoid(pre)
            d_pre = back * (sig * (1.0 + pre * (1.0 - sig)))
            dt_ref[...] += d_pre.reshape(16, 8, CA).sum(0)
            m = jnp.mean(d_pre * normed, -1, keepdims=True)
            grad = dm_ref[r, lanes] + factor * (d_pre - normed * m)
            ys_ref[0, pl.ds(i * 512 + j, 128, stride=4), :] = grad[:, :128]
            ys_ref[1, pl.ds(i * 512 + j, 128, stride=4), :] = grad[:, 128:]

    @pl.loop(0, 16)
    def _(i):
        r = rows_of(i, 128)
        sg_ref[r, :128] = ys_ref[0, r, :].astype(BF16)
        sg_ref[r, 128:] = ys_ref[1, r, :].astype(BF16)

    @pl.loop(0, 4)
    def _(i):
        at = turned(dc_ref[:S, pl.ds(pl.multiple_of(i * 128, 128), 128)])
        down = dot(at, mw_ref[:S, :]) * scaling
        for c in range(2):
            even, odd = down[64 * c : 64 * c + 32], down[64 * c + 32 : 64 * c + 64]
            put(idx_ref, keep_ref, send_ref, (2 * i + c) % 4, i // 2, slice(0, 32), even, odd)

    dt = jnp.sum(dt_ref[...].T, axis=1, keepdims=True)
    for i in range(2):
        one = jnp.zeros((128, 3 * CA), F32)
        for j in range(4):
            at = turned(dh_ref[:S, j * CA + i * 128 : j * CA + (i + 1) * 128])
            one += dot(at, uw_ref[:S, j * CA : (j + 3) * CA])
        one *= scaling
        time = dt[i * 128 : (i + 1) * 128] * (emb_ref[...] * scaling)
        for xx in range(4):
            even, odd = slice(32 * xx, 32 * xx + 16), slice(32 * xx + 16, 32 * xx + 32)
            rows = slice(32, 48)
            put(idx_ref, keep_ref, send_ref, xx, i, rows, one[even], one[odd])
            put(idx_ref, keep_ref, send_ref, xx, i, rows, time[even], time[odd], 3 * CA)


def encoded_kernel(co_ref, ab_ref, two_ref, enc_ref, ubw_ref):
    act_b = ab_ref[...].astype(F32)
    ubw_ref[:, CB : 2 * CB] = ab_ref[...]
    ubw_ref[:, :CB] = later(act_b).astype(BF16)
    ubw_ref[:, 2 * CB :] = sooner(act_b).astype(BF16)

    @pl.loop(0, 2)
    def _(i):
        r = rows_of(i, 256)
        enc = co_ref[r, :].astype(F32) + dot(ubw_ref[r, :], two_ref[...])
        enc_ref[r, :] = enc.astype(BF16)


def add_kernel(terms, *refs):
    at = 0
    for out in refs[terms:]:
        rows = slice(at, at + out.shape[0])
        total = refs[0][rows].astype(F32)
        for ref in refs[1:terms]:
            total = total + ref[rows].astype(F32)
        out[...] = total.astype(BF16)
        at += out.shape[0]


def join_kernel(own_u, got_u, own_v, got_v, own_ref, send_ref):
    half = own_u.shape[2]
    for own, got, lanes in (
        (own_u, got_u, slice(0, half)),
        (own_v, got_v, slice(half, 2 * half)),
    ):
        own_ref[:, lanes] = (own[0].astype(F32) + got[0].astype(F32)).astype(BF16)
        send_ref[:, lanes] = (own[1].astype(F32) + got[1].astype(F32)).astype(BF16)


def lines_kernel(a_ref, a_got, b_ref, b_got, out_ref):
    two = a_ref[...].astype(F32) + a_got[...].astype(F32)
    rest = b_ref[...].astype(F32) + b_got[...].astype(F32)
    for d in range(16):
        down = rest[:32, 64 * d : 64 * d + 64]
        last = rest[32:, 48 * d : 48 * d + 48]
        time = rest[32:, 3 * CA + 16 * d : 3 * CA + 16 * d + 16]
        top = jnp.concatenate([two[:, 96 * d : 96 * d + 96], down[:, :32]], axis=1)
        low = jnp.concatenate([down[:16, 32:], down[16:, 32:], last, time], axis=1)
        out_ref[d] = jnp.concatenate([top, low], axis=0).astype(BF16)


def last_kernel(in_ref, one_ref, down_ref, two_ref, time_ref):
    line = in_ref[0].astype(F32)
    for d in range(1, 16):
        line = line + in_ref[d].astype(F32)
    two_ref[...] = line[:32, :96]
    down_ref[:, :32] = line[:32, 96:]
    down_ref[:16, 32:] = line[32:, :32]
    down_ref[16:, 32:] = line[32:, 32:64]
    one_ref[...] = line[32:, 64:112]
    time_ref[...] = line[32:, 112:].T


def call(kernel, operands, outs, scratch=(), flops=0, nbytes=0, smem=False, far=0, sems=0,
         room=24):
    vmem = pl.BlockSpec(memory_space=pltpu.VMEM)
    first = pl.BlockSpec(memory_space=pltpu.SMEM) if smem else vmem
    return pl.pallas_call(
        kernel,
        in_specs=[pl.BlockSpec(memory_space=pltpu.HBM)] * far
        + [vmem if far else first]
        + [vmem] * (len(operands) - far - 1)
        if far < len(operands)
        else [pl.BlockSpec(memory_space=pltpu.HBM)] * far,
        out_specs=[vmem] * len(outs),
        out_shape=[jax.ShapeDtypeStruct(shape, kind) for shape, kind in outs],
        scratch_shapes=[pltpu.VMEM(shape, kind) for shape, kind in scratch]
        + [pltpu.SemaphoreType.DMA((sems,))] * (sems > 0),
        cost_estimate=pl.CostEstimate(flops=flops, bytes_accessed=nbytes, transcendentals=0),
        compiler_params=pltpu.CompilerParams(vmem_limit_bytes=int(room * 2**20)),
    )(*operands)


def embed(stamps, width):
    half = width // 2
    freqs = jnp.exp(-math.log(10000.0) * jnp.arange(half, dtype=F32) / half)
    angles = stamps.astype(F32)[:, None] * freqs[None, :]
    return jnp.concatenate([jnp.sin(angles), jnp.cos(angles)], axis=-1)


def moved(value, target):
    pairs = [(i, target(i // 8, i // 2 % 4, i % 2)) for i in range(16)]
    return lax.ppermute(value, "tm", pairs)


def swap_core(v):
    return moved(v, lambda y, x, c: y * 8 + x * 2 + 1 - c)


def swap_x(v, apart):
    return moved(v, lambda y, x, c: y * 8 + (x ^ apart) * 2 + c)


def swap_y(v):
    pairs = [(i, i ^ (8 * 16 + 8)) for i in range(256)]
    return lax.ppermute(v, AXES, pairs)


def ring(parts):
    u, su, v, sv = parts
    gu = swap_x(su, 1)
    gv = swap_x(sv, 3)
    u, su = added([u, gu], (2, 2))
    v, sv = added([v, gv], (2, 2))
    gu = swap_x(su, 3)
    gv = swap_x(sv, 1)
    rows, half = u.shape[1:]
    own, send = call(
        join_kernel, [u, gu, v, gv], [((rows, 2 * half), BF16)] * 2,
        nbytes=600_000,
    )
    return own, swap_y(send)


def added(terms, cuts):
    tail = terms[0].shape[1:]
    size = math.prod(terms[0].shape) * 2
    return call(
        lambda *refs: add_kernel(len(terms), *refs), terms,
        [((n,) + tail, BF16) for n in cuts], nbytes=size * (len(terms) + 1),
    )


def per_device(signal, timesteps, cotangent, conv_one, down_proj, conv_two, time_proj):
    x, cot = signal[0], cotangent[0]
    forward = [(i, i + 1) for i in range(15)]
    backward = [(i + 1, i) for i in range(15)]
    first, last = call(
        edges_kernel, [x, cot], [((8, CA + CB), BF16)] * 2, nbytes=50_000, far=2, sems=4,
        room=60,
    )
    left = lax.ppermute(last, "tm", forward)
    right = lax.ppermute(first, "tm", backward)
    emb = embed(timesteps, EMB)
    temb = jnp.dot(emb, time_proj.astype(F32), precision=lax.Precision.HIGHEST)
    tm = lax.axis_index("tm")
    idx = jnp.stack(
        [tm & 1, (tm >> 1) & 3, tm >> 3, (tm == 0).astype(jnp.int32), (tm == 15).astype(jnp.int32)]
    ).astype(jnp.int32)

    xp, act, cot, conv_one, down_proj = call(
        act_kernel, [x, cot, conv_one, down_proj, temb],
        [((S, 4 * CA), BF16)] * 2
        + [(v.shape, BF16) for v in (cot, conv_one, down_proj)],
        [((2, 4 * S, 128), F32), ((4 * S, CA), BF16)], 50_000_000, 6_500_000, far=4, sems=7,
        room=48,
    )
    a_keep, a_send, mw, uw, ab, co = call(
        forward_kernel,
        [idx, xp, act, left, right, cot, temb, conv_one, down_proj],
        [((16, 32, 3 * CB // 2), BF16)] * 2
        + [((E, 4 * CA), BF16), ((E, 6 * CA), BF16), ((E, CB), BF16), ((E, CB), BF16)],
        [((2, 64, 128), F32), ((E - S, 4 * CA), F32), ((E, 3 * CB), BF16)],
        2_200_000_000, 10_000_000, smem=True,
    )
    a_got = swap_core(a_send)
    dc, dh, dm = call(
        coarse_kernel, [idx, co, cot, left, right, down_proj, conv_two],
        [((E, CB), BF16), ((E, 4 * CA), BF16), ((S, 4 * CA), F32)],
        [((E, 3 * CB), BF16)], 1_400_000_000, 7_000_000, smem=True,
    )
    a_parts = added([a_keep, a_got], (4, 4, 4, 4))
    a_own, a_got = ring(a_parts)
    b_keep, b_send, signal_grad = call(
        fine_kernel, [idx, xp, dc, dh, dm, mw, uw, temb, emb, conv_one],
        [((16, 48, 2 * CA), BF16)] * 2 + [((4 * S, CA), BF16)],
        [((E, 6 * CA), BF16), ((2, 4 * S, 128), F32), ((8, CA), F32)],
        2_200_000_000, 11_000_000, smem=True,
    )
    b_got = swap_core(b_send)
    (encoded,) = call(
        encoded_kernel, [co, ab, conv_two], [((S, CB), BF16)],
        [((E, 3 * CB), BF16)], 800_000_000, 3_000_000,
    )
    b_parts = added([b_keep, b_got], (4, 4, 4, 4))
    b_own, b_got = ring(b_parts)
    (lines,) = call(
        lines_kernel, [a_own, a_got, b_own, b_got],
        [((16, 48, 128), BF16)], nbytes=900_000,
    )
    lines = lax.all_to_all(lines, "dp", 0, 0, tiled=True)
    outs = call(
        last_kernel, [lines],
        [((16, 48), F32), ((32, 64), F32), ((32, 96), F32), ((16, 16), F32)], nbytes=300_000,
    )
    one, down, two, time = outs
    return encoded[None], signal_grad[None], one.T, down.T, two.T, time


def solution(mesh):
    return jax.shard_map(
        per_device,
        mesh=mesh,
        in_specs=(P("dp", "tm", None), P("dp"), P("dp", "tm", None), P(), P(), P(), P()),
        out_specs=(
            P("dp", "tm", None),
            P("dp", "tm", None),
            P("dp", "tm"),
            P("dp", "tm"),
            P("dp", "tm"),
            P("dp", "tm"),
        ),
        check_vma=False,
    )
```

time: 111 us -> 78.7 us (0.71)
  blocking collectives: 17 us -> 0 us
  local copies, waits for them, and re-layouts: 13.6 us -> 1.15 us
  waiting for transfers between devices: 25.6 us -> 13.4 us
  starting transfers between devices: 24.9 us -> 36.7 us
  other arithmetic: 3.32 us -> 0.05 us
  Pallas kernels: 23.8 us -> 25.4 us
    all_to_all x1 -> x0, blocking collectives: 17 us -> none  [per_device(): lax.all_to_all(lines, 'dp', 0, 0, tiled=True).astype(F32).sum(0).reshape(-1)]
    ppermute x10, waiting for transfers between devices: 16.2 us -> 2.47 us  [moved(): return lax.ppermute(value, 'tm', pairs)]
    ppermute x10, starting transfers between devices: 12.5 us -> 21.8 us  [moved(): return lax.ppermute(value, 'tm', pairs)]
    unnamed x22 -> x10, local copies, waits for them, and re-layouts: 5.22 us -> 1.02 us
    slice x12 -> x0, local copies, waits for them, and re-layouts: 4.09 us -> none  [the longest x2 2.52 us: per_device(): ra, rb = (swap_core(ga[8:]), swap_core(gb[8:]))]
    ppermute x2 -> x4, starting transfers between devices: 3.02 us -> 6.36 us  [the longest x2 3.33 us: swap_y(): return lax.ppermute(v, AXES, pairs)]
    convert_element_type x7 -> x0, other arithmetic: 3.16 us -> none  [the longest x6 3.15 us: summed(): return total.astype(BF16)]
    reshape x13 -> x0, local copies, waits for them, and re-layouts: 3.08 us -> none  [the longest x4 2.1 us: per_device(): outs.append(line[at:at + n * k].reshape(n, k).T)]
  transfers between devices with their start and end apart: 13 -> 15, of which waited for: 5 -> 6; matrix products, arithmetic and copies ran while one was open for 5% -> 0% of each run, Pallas kernels for 7% -> 21%
where the time goes in v2:
time: 78.7 us; the launch traced here: 78.4 us
  starting transfers between devices  36.7 us (47%)
  Pallas kernels  25.4 us (32%)
  waiting for transfers between devices  13.4 us (17%)
  between operations  1.46 us (2%)
  local copies, waits for them, and re-layouts  1.15 us (1%)
    pallas_call x16, Pallas kernels, call(): pl.pallas_call(kernel, in_specs=[pl.BlockSpec(memory_space=pltpu.HBM)] *...  25.4 us
    ppermute x10, starting transfers between devices, moved(): return lax.ppermute(value, 'tm', pairs)  21.8 us
    all_to_all x1, starting transfers between devices, per_device(): lines = lax.all_to_all(lines, 'dp', 0, 0, tiled=True)  8.59 us
    all_to_all x1, waiting for transfers between devices, per_device(): lines = lax.all_to_all(lines, 'dp', 0, 0, tiled=True)  6.29 us
    ppermute x2, waiting for transfers between devices, swap_y(): return lax.ppermute(v, AXES, pairs)  4.67 us
    ppermute x2, starting transfers between devices, swap_y(): return lax.ppermute(v, AXES, pairs)  3.33 us
    ppermute x10, waiting for transfers between devices, moved(): return lax.ppermute(value, 'tm', pairs)  2.47 us
    ppermute x1, starting transfers between devices, per_device(): left = lax.ppermute(last, 'tm', forward)  1.74 us
  transfers between devices with their start and end apart: 15, of which 6 were waited for; matrix products, arithmetic and copies ran while one was open for 0% of the time, Pallas kernels for 21%

profile of v2, /device:TPU:32, one launch (start us, length us, event | category | flops | bytes accessed | tf_op | source)
XLA Modules:
  0.0 78.4 jit_solution(18267556269984656882)
XLA Ops:
  0.7 1.5 %shard_map.119 = (bf16[8,768]{1,0:T(8,128)(2,1)}, bf16[8,768]{1,0:T(8,128)(2,1)}) custom-call(bf16[2048,256]{1,0:T(8,128)(2,1)} %bitcast.19, bf16[512,512]{1,0:T(8,128)(2,1)} %bitcast.21), custom_call_target="tpu_custom_call" | custom-call | bytes 50000 | tf_op jit(solution)/shard_map/pallas_call | solution.py:358
  2.2 1.7 %collective-permute-start = (bf16[8,768]{1,0:T(8,128)(2,1)}, bf16[8,768]{1,0:T(8,128)(2,1)S(1)}, u32[]{:S(2)}, u32[]{:S(2)}) collective-permute-start(bf16[8,768]{1,0:T(8,128)(2,1)} %get-tuple-element.51), channel_id=1, source_target_pairs={{0,1},{1,2},{2,3},{3,4},{4,5},{5,6},{6,7},{7,8},{8,9},{9,10},{10,1... | collective-permute-start | bytes 36872 | tf_op jit(solution)/shard_map/ppermute | solution.py:432
  3.9 1.3 %collective-permute-start.1 = (bf16[8,768]{1,0:T(8,128)(2,1)}, bf16[8,768]{1,0:T(8,128)(2,1)S(1)}, u32[]{:S(2)}, u32[]{:S(2)}) collective-permute-start(bf16[8,768]{1,0:T(8,128)(2,1)} %get-tuple-element.52), channel_id=1, source_target_pairs={{1,0},{2,1},{3,2},{4,3},{5,4},{6,5},{7,6},{8,7},{9,8},{10,9},{11,1... | collective-permute-start | bytes 36872 | tf_op jit(solution)/shard_map/ppermute | solution.py:433
  6.2 1.0 %copy-done.4 = bf16[768,256]{1,0:T(8,128)(2,1)S(1)} copy-done((bf16[768,256]{1,0:T(8,128)(2,1)S(1)}, bf16[768,256]{1,0:T(8,128)(2,1)}, u32[]{:S(2)}) %copy-start.4) | copy-done | bytes 393240
  7.2 2.1 %shard_map.118 = (bf16[512,1024]{1,0:T(8,128)(2,1)S(1)}, bf16[512,1024]{1,0:T(8,128)(2,1)S(1)}, bf16[512,512]{1,0:T(8,128)(2,1)S(1)}, bf16[768,256]{1,0:T(8,128)(2,1)S(1)}, bf16[1024,512]{1,0:T(8,128)(2,1)S(1)}) custom-call(bf16[2048,256]{1,0:T(8,128)(2,1)S(1)} %bitcast.20, bf16[512,512]{1,0:T(8,128)(2,1)S(1)} %bitcast.22, bf16[768,256]{1,0:T(8,128)(2,1)S(1)} %copy-done.4, ...), custom_call_target="tpu_custom_call" | custom-call | flops 50000000 | bytes 6500000 | tf_op jit(solution)/shard_map/pallas_call | solution.py:358
  9.3 5.7 %shard_map.120 = (bf16[16,32,768]{2,1,0:T(8,128)(2,1)S(1)}, bf16[16,32,768]{2,1,0:T(8,128)(2,1)S(1)}, bf16[528,1024]{1,0:T(8,128)(2,1)S(1)}, bf16[528,1536]{1,0:...) custom-call(s32[5]{0:T(128)S(1)} %stack.31.idx_ref, ...), custom_call_target="tpu_custom_call" | custom-call | flops 2200000000 | bytes 10000000 | tf_op jit(solution)/shard_map/pallas_call | solution.py:358
  15.0 2.5 %collective-permute-start.2 = (bf16[16,32,768]{2,1,0:T(8,128)(2,1)S(1)}, bf16[16,32,768]{2,1,0:T(8,128)(2,1)S(1)}, u32[]{:S(2)}, u32[]{:S(2)}) collective-permute-start(bf16[16,32,768]{2,1,0:T(8,128)(2,1)S(1)} %get-tuple-element.65), channel_id=1, source_target_pairs={{0,1},{1,0},{2,3},{3,2},{4,5},{5,4},{6,7},{7,6},{8,9},{9,8},{10,11... | collective-permute-start | bytes 2359304 | tf_op jit(solution)/shard_map/ppermute | solution.py:383
  17.5 4.0 %shard_map.122 = (bf16[528,512]{1,0:T(8,128)(2,1)S(1)}, bf16[528,1024]{1,0:T(8,128)(2,1)S(1)}, f32[512,1024]{1,0:T(8,128)S(1)}) custom-call(s32[5]{0:T(128)S(1)} %stack.31.idx_ref, bf16[528,512]{1,0:T(8,128)(2,1)S(1)} %get-tuple-element.56.co_ref, bf16[512,512]{1,0:T(8,128)(2,1)S(1)} %get-tuple-element.53.cot_ref, ...), custom_call_target="tpu_custom_call" | custom-call | flops 1400000000 | bytes 7000000 | tf_op jit(solution)/shard_map/pallas_call | solution.py:358
  21.5 7.6 %shard_map.123 = (bf16[16,48,512]{2,1,0:T(8,128)(2,1)S(1)}, bf16[16,48,512]{2,1,0:T(8,128)(2,1)S(1)}, bf16[2048,256]{1,0:T(8,128)(2,1)}) custom-call(s32[5]{0:T(128)S(1)} %stack.31.idx_ref, bf16[512,1024]{1,0:T(8,128)(2,1)S(1)} %get-tuple-element.49.xp_ref, bf16[528,512]{1,0:T(8,128)(2,1)S(1)} %get-tuple-element.58.dc_ref, ...), custom_call_target="tpu_custom_call" | custom-call | flops 2200000000 | bytes 11000000 | tf_op jit(solution)/shard_map/pallas_call | solution.py:358
  29.3 2.2 %collective-permute-start.3 = (bf16[4,32,768]{2,1,0:T(8,128)(2,1)S(1)}, bf16[4,32,768]{2,1,0:T(8,128)(2,1)S(1)}, u32[]{:S(2)}, u32[]{:S(2)}) collective-permute-start(bf16[4,32,768]{2,1,0:T(8,128)(2,1)S(1)} %get-tuple-element.67), channel_id=1, source_target_pairs={{0,2},{1,3},{2,0},{3,1},{4,6},{5,7},{6,4},{7,5},{8,10},{9,11},{10,... | collective-permute-start | bytes 589832 | tf_op jit(solution)/shard_map/ppermute | solution.py:383
  31.5 5.2 %collective-permute-start.5 = (bf16[4,32,768]{2,1,0:T(8,128)(2,1)S(1)}, bf16[4,32,768]{2,1,0:T(8,128)(2,1)S(1)}, u32[]{:S(2)}, u32[]{:S(2)}) collective-permute-start(bf16[4,32,768]{2,1,0:T(8,128)(2,1)S(1)} %get-tuple-element.71), channel_id=1, source_target_pairs={{0,6},{1,7},{2,4},{3,5},{4,2},{5,3},{6,0},{7,1},{8,14},{9,15},{10,... | collective-permute-start | bytes 589832 | tf_op jit(solution)/shard_map/ppermute | solution.py:383
  36.9 1.4 %collective-permute-start.9 = (bf16[4,48,512]{2,1,0:T(8,128)(2,1)S(1)}, bf16[4,48,512]{2,1,0:T(8,128)(2,1)S(1)}, u32[]{:S(2)}, u32[]{:S(2)}) collective-permute-start(bf16[4,48,512]{2,1,0:T(8,128)(2,1)S(1)} %get-tuple-element.79), channel_id=1, source_target_pairs={{0,2},{1,3},{2,0},{3,1},{4,6},{5,7},{6,4},{7,5},{8,10},{9,11},{10,... | collective-permute-start | bytes 589832 | tf_op jit(solution)/shard_map/ppermute | solution.py:383
  38.3 0.7 collective-permute-start.11
  39.0 5.5 %collective-permute-start.4 = (bf16[2,32,768]{2,1,0:T(8,128)(2,1)S(1)}, bf16[2,32,768]{2,1,0:T(8,128)(2,1)S(1)}, u32[]{:S(2)}, u32[]{:S(2)}) collective-permute-start(bf16[2,32,768]{2,1,0:T(8,128)(2,1)S(1)} %get-tuple-element.69), channel_id=1, source_target_pairs={{0,6},{1,7},{2,4},{3,5},{4,2},{5,3},{6,0},{7,1},{8,14},{9,15},{10,... | collective-permute-start | bytes 294920 | tf_op jit(solution)/shard_map/ppermute | solution.py:383
  44.7 4.2 %collective-permute-start.10 = (bf16[2,48,512]{2,1,0:T(8,128)(2,1)S(1)}, bf16[2,48,512]{2,1,0:T(8,128)(2,1)S(1)}, u32[]{:S(2)}, u32[]{:S(2)}) collective-permute-start(bf16[2,48,512]{2,1,0:T(8,128)(2,1)S(1)} %get-tuple-element.81), channel_id=1, source_target_pairs={{0,6},{1,7},{2,4},{3,5},{4,2},{5,3},{6,0},{7,1},{8,14},{9,15},{10,... | collective-permute-start | bytes 294920 | tf_op jit(solution)/shard_map/ppermute | solution.py:383
  49.3 2.1 %collective-permute-start.7 = (bf16[32,1536]{1,0:T(8,128)(2,1)S(1)}, bf16[32,1536]{1,0:T(8,128)(2,1)S(1)}, u32[]{:S(2)}, u32[]{:S(2)}) collective-permute-start(bf16[32,1536]{1,0:T(8,128)(2,1)S(1)} %get-tuple-element.75), channel_id=1, source_target_pairs={{0,136},{1,137},{2,138},{3,139},{4,140},{5,141},{6,142},{7,143},{8... | collective-permute-start | bytes 294920 | tf_op jit(solution)/shard_map/ppermute | solution.py:396
  51.5 2.2 %collective-permute-done.12.got_v = bf16[2,48,512]{2,1,0:T(8,128)(2,1)S(1)} collective-permute-done((bf16[2,48,512]{2,1,0:T(8,128)(2,1)S(1)}, bf16[2,48,512]{2,1,0:T(8,128)(2,1)S(1)}, u32[]{:S(2)}, u32[]{:S(2)}) %collective-permute-start.12) | collective-permute-done | bytes 98336 | tf_op jit(solution)/shard_map/ppermute | solution.py:383
  53.7 1.2 %collective-permute-start.13 = (bf16[48,1024]{1,0:T(8,128)(2,1)S(1)}, bf16[48,1024]{1,0:T(8,128)(2,1)S(1)}, u32[]{:S(2)}, u32[]{:S(2)}) collective-permute-start(bf16[48,1024]{1,0:T(8,128)(2,1)S(1)} %get-tuple-element.87), channel_id=1, source_target_pairs={{0,136},{1,137},{2,138},{3,139},{4,140},{5,141},{6,142},{7,143},{8... | collective-permute-start | bytes 294920 | tf_op jit(solution)/shard_map/ppermute | solution.py:396
  55.2 4.4 %collective-permute-done.13.b_got = bf16[48,1024]{1,0:T(8,128)(2,1)S(1)} collective-permute-done((bf16[48,1024]{1,0:T(8,128)(2,1)S(1)}, bf16[48,1024]{1,0:T(8,128)(2,1)S(1)}, u32[]{:S(2)}, u32[]{:S(2)}) %collective-permute-start.13) | collective-permute-done | bytes 98336 | tf_op jit(solution)/shard_map/ppermute | solution.py:396
  59.6 0.9 %shard_map.132 = bf16[16,48,128]{2,1,0:T(8,128)(2,1)} custom-call(bf16[32,1536]{1,0:T(8,128)(2,1)S(1)} %get-tuple-element.74.a_ref, bf16[32,1536]{1,0:T(8,128)(2,1)S(1)} %collective-permute-done.7.a_got, bf16[48,1024]{1,0:T(8,128)(2,1)S(1)} %get-tuple-element.86.b_ref, bf16[48,1024]{1,0:T(8,128)(2,1)S(1)} %collective-permute-done.13.b_got), custom_call_target="tpu_custom_call" | custom-call | bytes 900000 | tf_op jit(solution)/shard_map/pallas_call | solution.py:358
  60.5 8.6 %all-to-all-start = ((bf16[16,48,128]{2,1,0:T(8,128)(2,1)}), bf16[16,48,128]{2,1,0:T(8,128)(2,1)S(1)}, u32[]{:S(2)}, u32[]{:S(2)}) async-start(bf16[16,48,128]{2,1,0:T(8,128)(2,1)} %shard_map.132), calls=%async_computation | async-start | bytes 393216 | tf_op jit(solution)/shard_map/all_to_all | solution.py:481
  69.1 2.2 %shard_map.121 = bf16[512,512]{1,0:T(8,128)(2,1)} custom-call(bf16[528,512]{1,0:T(8,128)(2,1)S(1)} %get-tuple-element.56.co_ref, bf16[528,512]{1,0:T(8,128)(2,1)S(1)} %get-tuple-element.57.ab_ref, bf16[1536,512]{1,0:T(8,128)(2,1)S(1)} %copy-done.3), custom_call_target="tpu_custom_call" | custom-call | flops 800000000 | bytes 3000000 | tf_op jit(solution)/shard_map/pallas_call | solution.py:358
  71.3 6.3 %all-to-all-done.in_ref = bf16[16,48,128]{2,1,0:T(8,128)(2,1)S(1)} async-done(((bf16[16,48,128]{2,1,0:T(8,128)(2,1)}), bf16[16,48,128]{2,1,0:T(8,128)(2,1)S(1)}, u32[]{:S(2)}, u32[]{:S(2)}) %all-to-all-start) | async-done | bytes 196640 | tf_op jit(solution)/shard_map/all_to_all | solution.py:481
  77.6 0.8 shard_map.133
  (36 shorter events, 1.8 us)
Async XLA Ops:
  0.6 5.3 %copy-start = (bf16[256,256]{1,0:T(8,128)(2,1)S(1)}, bf16[256,256]{1,0:T(8,128)(2,1)}, u32[]{:S(2)}) copy-start(bf16[256,256]{1,0:T(8,128)(2,1)} %param.13) | copy-start | bytes 393220
  0.6 5.6 %copy-start.2 = (bf16[1,512,512]{2,1,0:T(8,128)(2,1)S(1)}, bf16[1,512,512]{2,1,0:T(8,128)(2,1)}, u32[]{:S(2)}) copy-start(bf16[1,512,512]{2,1,0:T(8,128)(2,1)} %param.9) | copy-start | bytes 1572868
  0.7 5.6 %copy-start.1 = (bf16[1,2048,256]{2,1,0:T(8,128)(2,1)S(1)}, bf16[1,2048,256]{2,1,0:T(8,128)(2,1)}, u32[]{:S(2)}) copy-start(bf16[1,2048,256]{2,1,0:T(8,128)(2,1)} %param.7) | copy-start | bytes 3145732
  2.2 7.1 %collective-permute-start = (bf16[8,768]{1,0:T(8,128)(2,1)}, bf16[8,768]{1,0:T(8,128)(2,1)S(1)}, u32[]{:S(2)}, u32[]{:S(2)}) collective-permute-start(bf16[8,768]{1,0:T(8,128)(2,1)} %get-tuple-element.51), channel_id=1, source_target_pairs={{0,1},{1,2},{2,3},{3,4},{4,5},{5,6},{6,7},{7,8},{8,9},{9,10},{10,1... | collective-permute-start | bytes 36872 | tf_op jit(solution)/shard_map/ppermute | solution.py:432
  3.9 5.4 %collective-permute-start.1 = (bf16[8,768]{1,0:T(8,128)(2,1)}, bf16[8,768]{1,0:T(8,128)(2,1)S(1)}, u32[]{:S(2)}, u32[]{:S(2)}) collective-permute-start(bf16[8,768]{1,0:T(8,128)(2,1)} %get-tuple-element.52), channel_id=1, source_target_pairs={{1,0},{2,1},{3,2},{4,3},{5,4},{6,5},{7,6},{8,7},{9,8},{10,9},{11,1... | collective-permute-start | bytes 36872 | tf_op jit(solution)/shard_map/ppermute | solution.py:433
  6.2 1.0 %copy-start.4 = (bf16[768,256]{1,0:T(8,128)(2,1)S(1)}, bf16[768,256]{1,0:T(8,128)(2,1)}, u32[]{:S(2)}) copy-start(bf16[768,256]{1,0:T(8,128)(2,1)} %one_ref.1) | copy-start | bytes 1179652
  9.3 8.2 %copy-start.3 = (bf16[1536,512]{1,0:T(8,128)(2,1)S(1)}, bf16[1536,512]{1,0:T(8,128)(2,1)}, u32[]{:S(2)}) copy-start(bf16[1536,512]{1,0:T(8,128)(2,1)} %two_ref.3) | copy-start | bytes 4718596
  15.0 14.1 %collective-permute-start.2 = (bf16[16,32,768]{2,1,0:T(8,128)(2,1)S(1)}, bf16[16,32,768]{2,1,0:T(8,128)(2,1)S(1)}, u32[]{:S(2)}, u32[]{:S(2)}) collective-permute-start(bf16[16,32,768]{2,1,0:T(8,128)(2,1)S(1)} %get-tuple-element.65), channel_id=1, source_target_pairs={{0,1},{1,0},{2,3},{3,2},{4,5},{5,4},{6,7},{7,6},{8,9},{9,8},{10,11... | collective-permute-start | bytes 2359304 | tf_op jit(solution)/shard_map/ppermute | solution.py:383
  29.1 7.6 %collective-permute-start.8 = (bf16[16,48,512]{2,1,0:T(8,128)(2,1)S(1)}, bf16[16,48,512]{2,1,0:T(8,128)(2,1)S(1)}, u32[]{:S(2)}, u32[]{:S(2)}) collective-permute-start(bf16[16,48,512]{2,1,0:T(8,128)(2,1)S(1)} %get-tuple-element.77), channel_id=1, source_target_pairs={{0,1},{1,0},{2,3},{3,2},{4,5},{5,4},{6,7},{7,6},{8,9},{9,8},{10,11... | collective-permute-start | bytes 2359304 | tf_op jit(solution)/shard_map/ppermute | solution.py:383
  29.3 9.6 %collective-permute-start.3 = (bf16[4,32,768]{2,1,0:T(8,128)(2,1)S(1)}, bf16[4,32,768]{2,1,0:T(8,128)(2,1)S(1)}, u32[]{:S(2)}, u32[]{:S(2)}) collective-permute-start(bf16[4,32,768]{2,1,0:T(8,128)(2,1)S(1)} %get-tuple-element.67), channel_id=1, source_target_pairs={{0,2},{1,3},{2,0},{3,1},{4,6},{5,7},{6,4},{7,5},{8,10},{9,11},{10,... | collective-permute-start | bytes 589832 | tf_op jit(solution)/shard_map/ppermute | solution.py:383
  31.5 13.0 %collective-permute-start.5 = (bf16[4,32,768]{2,1,0:T(8,128)(2,1)S(1)}, bf16[4,32,768]{2,1,0:T(8,128)(2,1)S(1)}, u32[]{:S(2)}, u32[]{:S(2)}) collective-permute-start(bf16[4,32,768]{2,1,0:T(8,128)(2,1)S(1)} %get-tuple-element.71), channel_id=1, source_target_pairs={{0,6},{1,7},{2,4},{3,5},{4,2},{5,3},{6,0},{7,1},{8,14},{9,15},{10,... | collective-permute-start | bytes 589832 | tf_op jit(solution)/shard_map/ppermute | solution.py:383
  36.9 7.8 %collective-permute-start.9 = (bf16[4,48,512]{2,1,0:T(8,128)(2,1)S(1)}, bf16[4,48,512]{2,1,0:T(8,128)(2,1)S(1)}, u32[]{:S(2)}, u32[]{:S(2)}) collective-permute-start(bf16[4,48,512]{2,1,0:T(8,128)(2,1)S(1)} %get-tuple-element.79), channel_id=1, source_target_pairs={{0,2},{1,3},{2,0},{3,1},{4,6},{5,7},{6,4},{7,5},{8,10},{9,11},{10,... | collective-permute-start | bytes 589832 | tf_op jit(solution)/shard_map/ppermute | solution.py:383
  38.3 10.6 %collective-permute-start.11 = (bf16[4,48,512]{2,1,0:T(8,128)(2,1)S(1)}, bf16[4,48,512]{2,1,0:T(8,128)(2,1)S(1)}, u32[]{:S(2)}, u32[]{:S(2)}) collective-permute-start(bf16[4,48,512]{2,1,0:T(8,128)(2,1)S(1)} %get-tuple-element.83), channel_id=1, source_target_pairs={{0,6},{1,7},{2,4},{3,5},{4,2},{5,3},{6,0},{7,1},{8,14},{9,15},{10,... | collective-permute-start | bytes 589832 | tf_op jit(solution)/shard_map/ppermute | solution.py:383
  39.0 10.0 %collective-permute-start.4 = (bf16[2,32,768]{2,1,0:T(8,128)(2,1)S(1)}, bf16[2,32,768]{2,1,0:T(8,128)(2,1)S(1)}, u32[]{:S(2)}, u32[]{:S(2)}) collective-permute-start(bf16[2,32,768]{2,1,0:T(8,128)(2,1)S(1)} %get-tuple-element.69), channel_id=1, source_target_pairs={{0,6},{1,7},{2,4},{3,5},{4,2},{5,3},{6,0},{7,1},{8,14},{9,15},{10,... | collective-permute-start | bytes 294920 | tf_op jit(solution)/shard_map/ppermute | solution.py:383
  44.5 4.7 %collective-permute-start.6 = (bf16[2,32,768]{2,1,0:T(8,128)(2,1)S(1)}, bf16[2,32,768]{2,1,0:T(8,128)(2,1)S(1)}, u32[]{:S(2)}, u32[]{:S(2)}) collective-permute-start(bf16[2,32,768]{2,1,0:T(8,128)(2,1)S(1)} %get-tuple-element.73), channel_id=1, source_target_pairs={{0,2},{1,3},{2,0},{3,1},{4,6},{5,7},{6,4},{7,5},{8,10},{9,11},{10,... | collective-permute-start | bytes 294920 | tf_op jit(solution)/shard_map/ppermute | solution.py:383
  44.7 6.8 %collective-permute-start.10 = (bf16[2,48,512]{2,1,0:T(8,128)(2,1)S(1)}, bf16[2,48,512]{2,1,0:T(8,128)(2,1)S(1)}, u32[]{:S(2)}, u32[]{:S(2)}) collective-permute-start(bf16[2,48,512]{2,1,0:T(8,128)(2,1)S(1)} %get-tuple-element.81), channel_id=1, source_target_pairs={{0,6},{1,7},{2,4},{3,5},{4,2},{5,3},{6,0},{7,1},{8,14},{9,15},{10,... | collective-permute-start | bytes 294920 | tf_op jit(solution)/shard_map/ppermute | solution.py:383
  48.9 4.7 %collective-permute-start.12 = (bf16[2,48,512]{2,1,0:T(8,128)(2,1)S(1)}, bf16[2,48,512]{2,1,0:T(8,128)(2,1)S(1)}, u32[]{:S(2)}, u32[]{:S(2)}) collective-permute-start(bf16[2,48,512]{2,1,0:T(8,128)(2,1)S(1)} %get-tuple-element.85), channel_id=1, source_target_pairs={{0,2},{1,3},{2,0},{3,1},{4,6},{5,7},{6,4},{7,5},{8,10},{9,11},{10,... | collective-permute-start | bytes 294920 | tf_op jit(solution)/shard_map/ppermute | solution.py:383
  49.3 5.9 %collective-permute-start.7 = (bf16[32,1536]{1,0:T(8,128)(2,1)S(1)}, bf16[32,1536]{1,0:T(8,128)(2,1)S(1)}, u32[]{:S(2)}, u32[]{:S(2)}) collective-permute-start(bf16[32,1536]{1,0:T(8,128)(2,1)S(1)} %get-tuple-element.75), channel_id=1, source_target_pairs={{0,136},{1,137},{2,138},{3,139},{4,140},{5,141},{6,142},{7,143},{8... | collective-permute-start | bytes 294920 | tf_op jit(solution)/shard_map/ppermute | solution.py:396
  53.7 5.9 %collective-permute-start.13 = (bf16[48,1024]{1,0:T(8,128)(2,1)S(1)}, bf16[48,1024]{1,0:T(8,128)(2,1)S(1)}, u32[]{:S(2)}, u32[]{:S(2)}) collective-permute-start(bf16[48,1024]{1,0:T(8,128)(2,1)S(1)} %get-tuple-element.87), channel_id=1, source_target_pairs={{0,136},{1,137},{2,138},{3,139},{4,140},{5,141},{6,142},{7,143},{8... | collective-permute-start | bytes 294920 | tf_op jit(solution)/shard_map/ppermute | solution.py:396
  60.5 17.1 %all-to-all-start = ((bf16[16,48,128]{2,1,0:T(8,128)(2,1)}), bf16[16,48,128]{2,1,0:T(8,128)(2,1)S(1)}, u32[]{:S(2)}, u32[]{:S(2)}) async-start(bf16[16,48,128]{2,1,0:T(8,128)(2,1)} %shard_map.132), calls=%async_computation | async-start | bytes 393216 | tf_op jit(solution)/shard_map/all_to_all | solution.py:481

commit v3 on v2

--- a/solution.py
+++ b/solution.py
@@ -12,6 +12,7 @@
 CA, CB, EMB = 256, 512, 256
 S = 512
 E = 528
+STEP = 176
 F32, BF16 = jnp.float32, jnp.bfloat16
 AXES = ("dp", "tm")
 NT = (((1,), (1,)), ((), ()))
@@ -30,7 +31,7 @@
 
 
 def sigmoid(v):
-    return 1.0 / (1.0 + jnp.exp(-v))
+    return 0.5 * jnp.tanh(0.5 * v) + 0.5
 
 
 def inside(idx_ref, start, size, margin):
@@ -83,18 +84,28 @@
     return v.astype(F32).T.astype(BF16)
 
 
-def edges_kernel(x_ref, cot_ref, first_ref, last_ref, sem):
+def edges_kernel(idx_ref, x_ref, cot_ref, one_ref, two_ref, sem):
     copies = []
-    for out, at in ((first_ref, 0), (last_ref, 1)):
-        n = len(copies)
-        rows = (pl.ds(0, 8), pl.ds(4 * S - 8, 8))[at]
-        copies.append(pltpu.make_async_copy(x_ref.at[rows, :], out.at[:, :CA], sem.at[n]))
-        rows = (pl.ds(0, 8), pl.ds(S - 8, 8))[at]
-        copies.append(pltpu.make_async_copy(cot_ref.at[rows, :], out.at[:, CA:], sem.at[n + 1]))
+    for n, out in enumerate((one_ref, two_ref)):
+        last = idx_ref[0] ^ n
+        rows = pl.ds(pl.multiple_of(last * (4 * S - 8), 8), 8)
+        copies.append(pltpu.make_async_copy(x_ref.at[rows, :], out.at[:, :CA], sem.at[2 * n]))
+        rows = pl.ds(pl.multiple_of(last * (S - 8), 8), 8)
+        copies.append(
+            pltpu.make_async_copy(cot_ref.at[rows, :], out.at[:, CA:], sem.at[2 * n + 1])
+        )
     for copy in copies:
         copy.start()
     for copy in copies:
         copy.wait()
+
+
+def sides(idx_ref, chip_ref, core_ref, rows, lanes):
+    chip = chip_ref[:, lanes].astype(F32)
+    core = core_ref[:, lanes].astype(F32)
+    even = idx_ref[0] == 0
+    before, behind = jnp.where(even, chip, core), jnp.where(even, core, chip)
+    return before[8 - rows :], behind[:rows]
 
 
 def act_kernel(
@@ -136,43 +147,44 @@
 
 
 def forward_kernel(
-    idx_ref, xp_ref, act_ref, left_ref, right_ref, cot_ref, temb_ref, one_ref, down_ref,
+    idx_ref, xp_ref, act_ref, chip_ref, core_ref, cot_ref, temb_ref, one_ref, down_ref,
     keep_ref, send_ref, mw_ref, uw_ref, ab_ref, co_ref,
-    xs_ref, xe_ref, ubw_ref,
+    xs_ref, ubw_ref, at_ref,
 ):
+    before, behind = sides(idx_ref, chip_ref, core_ref, 8, slice(0, CA))
     for h in range(2):
         lanes = slice(h * 128, (h + 1) * 128)
-        xs_ref[h, :8, :] = right_ref[:, lanes].astype(F32)
+        xs_ref[h, :8, :] = behind[:, lanes]
         xs_ref[h, 8:56, :] = jnp.zeros((48, 128), F32)
-        xs_ref[h, 56:, :] = left_ref[:, lanes].astype(F32)
+        xs_ref[h, 56:, :] = before[:, lanes]
     inner = inside(idx_ref, S, E - S, 2)
     for j in range(4):
         v = phase(xs_ref, j, 16)
         pre = v * rms(v) + temb_ref[...]
-        xe_ref[:, j * CA : (j + 1) * CA] = v
         uw_ref[S:, (j + 1) * CA : (j + 2) * CA] = (pre * sigmoid(pre) * inner).astype(BF16)
     uw_ref[:S, CA : 5 * CA] = act_ref[...]
     uw_ref[:, :CA] = later(uw_ref[:, 4 * CA : 5 * CA].astype(F32)).astype(BF16)
     uw_ref[:, 5 * CA :] = sooner(uw_ref[:, CA : 2 * CA].astype(F32)).astype(BF16)
-
-    def block(r, size, start, x_of):
-        for j in range(4):
-            lanes = slice(j * CA, (j + 1) * CA)
-            hidden = dot(uw_ref[r, j * CA : (j + 3) * CA], one_ref[...])
-            mw_ref[r, lanes] = (x_of(lanes) + hidden).astype(BF16)
-        coarse = dot(mw_ref[r, :], down_ref[...]).astype(BF16)
-        co_ref[r, :] = coarse
-        c32 = coarse.astype(F32)
+    for i in range(4):
+        lanes = slice(i * 128, (i + 1) * 128)
+        at_ref[lanes, :] = turned(cot_ref[:, lanes])
+
+    for j in range(4):
+        lanes = slice(j * CA, (j + 1) * CA)
+        hidden = dot(uw_ref[:, j * CA : (j + 3) * CA], one_ref[...])
+        mw_ref[:S, lanes] = (xp_ref[:, lanes].astype(F32) + hidden[:S]).astype(BF16)
+        mw_ref[S:, lanes] = (phase(xs_ref, j, 16) + hidden[S:]).astype(BF16)
+    for n in range(2):
+        lanes = slice(n * CA, (n + 1) * CA)
+        co_ref[:, lanes] = dot(mw_ref[...], down_ref[:, lanes]).astype(BF16)
+
+    @pl.loop(0, 3)
+    def _(i):
+        r = rows_of(i, STEP)
+        c32 = co_ref[r, :].astype(F32)
         normed = c32 * rms(c32)
-        keep = inside(idx_ref, start, size, 1)
+        keep = inside(idx_ref, i * STEP, STEP, 1)
         ubw_ref[r, CB : 2 * CB] = (normed * sigmoid(normed) * keep).astype(BF16)
-
-    @pl.loop(0, 2)
-    def _(i):
-        r = rows_of(i, 256)
-        block(r, 256, i * 256, lambda lanes: xp_ref[r, lanes].astype(F32))
-
-    block(slice(S, E), E - S, S, lambda lanes: xe_ref[:, lanes])
 
     act_b = ubw_ref[:, CB : 2 * CB]
     ab_ref[...] = act_b
@@ -181,72 +193,72 @@
     ubw_ref[:, 2 * CB :] = sooner(act_b).astype(BF16)
 
     scaling = 1.0 / math.sqrt(16 * 32768)
-
-    @pl.loop(0, 4)
-    def _(i):
-        at = turned(cot_ref[:, pl.ds(pl.multiple_of(i * 128, 128), 128)])
-        two = dot(at, ubw_ref[:S, :]) * scaling
-        for c in range(2):
+    for n in range(6):
+        two = dot(at_ref[...], ubw_ref[:S, n * CA : (n + 1) * CA]) * scaling
+        for c in range(8):
             even, odd = two[64 * c : 64 * c + 32], two[64 * c + 32 : 64 * c + 64]
-            put(idx_ref, keep_ref, send_ref, (2 * i + c) % 4, i // 2, slice(None), even, odd)
+            put(idx_ref, keep_ref, send_ref, c % 4, c // 4, slice(None), even, odd, n * CA)
 
 
 def coarse_kernel(
-    idx_ref, co_ref, cot_ref, left_ref, right_ref, down_ref, two_ref,
-    dc_ref, dh_ref, dm_ref, cw_ref,
+    idx_ref, co_ref, cot_ref, chip_ref, core_ref, down_ref, two_ref,
+    dc_ref, dh_ref, dm_ref,
+    cw_ref, back_ref,
 ):
+    before, behind = sides(idx_ref, chip_ref, core_ref, 2, slice(CA, None))
     cot = jnp.concatenate(
-        [
-            cot_ref[...].astype(F32),
-            right_ref[:2, CA:].astype(F32),
-            jnp.zeros((12, CB), F32),
-            left_ref[6:, CA:].astype(F32),
-        ],
-        axis=0,
+        [cot_ref[...].astype(F32), behind, jnp.zeros((12, CB), F32), before], axis=0
     )
     cw_ref[:, CB : 2 * CB] = cot.astype(BF16)
     cw_ref[:, :CB] = sooner(cot).astype(BF16)
     cw_ref[:, 2 * CB :] = later(cot).astype(BF16)
-
-    def block(r, size, start):
-        back = dot_nt(cw_ref[r, :CB], two_ref[:CB, :])
-        back += dot_nt(cw_ref[r, CB : 2 * CB], two_ref[CB : 2 * CB, :])
-        back += dot_nt(cw_ref[r, 2 * CB :], two_ref[2 * CB :, :])
+    for n in range(2):
+        lanes = slice(n * CA, (n + 1) * CA)
+        back = dot_nt(cw_ref[:, :CB], two_ref[n * CA : (n + 1) * CA, :])
+        back += dot_nt(cw_ref[:, CB : 2 * CB], two_ref[CB + n * CA : CB + (n + 1) * CA, :])
+        back += dot_nt(cw_ref[:, 2 * CB :], two_ref[2 * CB + n * CA : 2 * CB + (n + 1) * CA, :])
+        back_ref[:, lanes] = back
+
+    @pl.loop(0, 3)
+    def _(i):
+        r = rows_of(i, STEP)
         c32 = co_ref[r, :].astype(F32)
         factor = rms(c32)
         normed = c32 * factor
         sig = sigmoid(normed)
-        q = back * (sig * (1.0 + normed * (1.0 - sig)))
+        q = back_ref[r, :] * (sig * (1.0 + normed * (1.0 - sig)))
         m = jnp.mean(q * normed, -1, keepdims=True)
         grad = cw_ref[r, CB : 2 * CB].astype(F32) + factor * (q - normed * m)
-        d_coarse = (grad * inside(idx_ref, start, size, 1)).astype(BF16)
-        dc_ref[r, :] = d_coarse
-        return dot_nt(d_coarse, down_ref[...])
-
-    @pl.loop(0, 2)
-    def _(i):
-        r = rows_of(i, 256)
-        dm = block(r, 256, i * 256)
-        dm_ref[r, :] = dm
-        dh_ref[r, :] = dm.astype(BF16)
-
-    dh_ref[S:, :] = block(slice(S, E), E - S, S).astype(BF16)
+        dc_ref[r, :] = (grad * inside(idx_ref, i * STEP, STEP, 1)).astype(BF16)
+
+    for n in range(4):
+        lanes = slice(n * CA, (n + 1) * CA)
+        dm = dot_nt(dc_ref[...], down_ref[lanes, :])
+        dm_ref[:, lanes] = dm[:S]
+        dh_ref[:, lanes] = dm.astype(BF16)
 
 
 def fine_kernel(
     idx_ref, xp_ref, dc_ref, dh_ref, dm_ref, mw_ref, uw_ref, temb_ref, emb_ref, one_ref,
     keep_ref, send_ref, sg_ref,
-    dhw_ref, ys_ref, dt_ref,
+    dhw_ref, ys_ref, dt_ref, at_ref, dt_all_ref,
 ):
     scaling = 1.0 / math.sqrt(16 * 32768)
     dhw_ref[:, CA : 5 * CA] = dh_ref[...]
     dhw_ref[:, :CA] = later(dh_ref[:, 3 * CA :].astype(F32)).astype(BF16)
     dhw_ref[:, 5 * CA :] = sooner(dh_ref[:, :CA].astype(F32)).astype(BF16)
     dt_ref[...] = jnp.zeros((8, CA), F32)
-
-    @pl.loop(0, 4)
+    for i in range(4):
+        lanes = slice(i * 128, (i + 1) * 128)
+        at_ref[lanes, :] = turned(dc_ref[:S, lanes])
+    for j in range(4):
+        for i in range(2):
+            lanes = slice(j * CA + i * 128, j * CA + (i + 1) * 128)
+            dt_all_ref[i * 128 : (i + 1) * 128, j * S : (j + 1) * S] = turned(dh_ref[:S, lanes])
+
+    @pl.loop(0, 2)
     def _(i):
-        r = rows_of(i, 128)
+        r = rows_of(i, 256)
         for j in range(4):
             lanes = slice(j * CA, (j + 1) * CA)
             back = dot_nt(dhw_ref[r, (j + 2) * CA : (j + 3) * CA], one_ref[:CA, :])
@@ -258,11 +270,11 @@
             pre = normed + temb_ref[...]
             sig = sigmoid(pre)
             d_pre = back * (sig * (1.0 + pre * (1.0 - sig)))
-            dt_ref[...] += d_pre.reshape(16, 8, CA).sum(0)
+            dt_ref[...] += d_pre.reshape(32, 8, CA).sum(0)
             m = jnp.mean(d_pre * normed, -1, keepdims=True)
             grad = dm_ref[r, lanes] + factor * (d_pre - normed * m)
-            ys_ref[0, pl.ds(i * 512 + j, 128, stride=4), :] = grad[:, :128]
-            ys_ref[1, pl.ds(i * 512 + j, 128, stride=4), :] = grad[:, 128:]
+            ys_ref[0, pl.ds(i * 1024 + j, 256, stride=4), :] = grad[:, :128]
+            ys_ref[1, pl.ds(i * 1024 + j, 256, stride=4), :] = grad[:, 128:]
 
     @pl.loop(0, 16)
     def _(i):
@@ -270,27 +282,25 @@
         sg_ref[r, :128] = ys_ref[0, r, :].astype(BF16)
         sg_ref[r, 128:] = ys_ref[1, r, :].astype(BF16)
 
-    @pl.loop(0, 4)
-    def _(i):
-        at = turned(dc_ref[:S, pl.ds(pl.multiple_of(i * 128, 128), 128)])
-        down = dot(at, mw_ref[:S, :]) * scaling
-        for c in range(2):
+    for n in range(4):
+        down = dot(at_ref[...], mw_ref[:S, n * CA : (n + 1) * CA]) * scaling
+        for c in range(8):
             even, odd = down[64 * c : 64 * c + 32], down[64 * c + 32 : 64 * c + 64]
-            put(idx_ref, keep_ref, send_ref, (2 * i + c) % 4, i // 2, slice(0, 32), even, odd)
-
-    dt = jnp.sum(dt_ref[...].T, axis=1, keepdims=True)
-    for i in range(2):
-        one = jnp.zeros((128, 3 * CA), F32)
-        for j in range(4):
-            at = turned(dh_ref[:S, j * CA + i * 128 : j * CA + (i + 1) * 128])
-            one += dot(at, uw_ref[:S, j * CA : (j + 3) * CA])
-        one *= scaling
-        time = dt[i * 128 : (i + 1) * 128] * (emb_ref[...] * scaling)
-        for xx in range(4):
-            even, odd = slice(32 * xx, 32 * xx + 16), slice(32 * xx + 16, 32 * xx + 32)
-            rows = slice(32, 48)
-            put(idx_ref, keep_ref, send_ref, xx, i, rows, one[even], one[odd])
-            put(idx_ref, keep_ref, send_ref, xx, i, rows, time[even], time[odd], 3 * CA)
+            put(idx_ref, keep_ref, send_ref, c % 4, c // 4, slice(0, 32), even, odd, n * CA)
+
+    for n in range(4):
+        if n < 3:
+            one = jnp.zeros((CA, CA), F32)
+            for j in range(4):
+                lanes = slice((j + n) * CA, (j + n + 1) * CA)
+                one += dot(dt_all_ref[:, j * S : (j + 1) * S], uw_ref[:S, lanes])
+            one *= scaling
+        else:
+            dt = jnp.sum(dt_ref[...].T, axis=1, keepdims=True)
+            one = dt * (emb_ref[...] * scaling)
+        for c in range(8):
+            even, odd = one[32 * c : 32 * c + 16], one[32 * c + 16 : 32 * c + 32]
+            put(idx_ref, keep_ref, send_ref, c % 4, c // 4, slice(32, 48), even, odd, n * CA)
 
 
 def encoded_kernel(co_ref, ab_ref, two_ref, enc_ref, ubw_ref):
@@ -299,11 +309,10 @@
     ubw_ref[:, :CB] = later(act_b).astype(BF16)
     ubw_ref[:, 2 * CB :] = sooner(act_b).astype(BF16)
 
-    @pl.loop(0, 2)
-    def _(i):
-        r = rows_of(i, 256)
-        enc = co_ref[r, :].astype(F32) + dot(ubw_ref[r, :], two_ref[...])
-        enc_ref[r, :] = enc.astype(BF16)
+    for n in range(2):
+        lanes = slice(n * CA, (n + 1) * CA)
+        enc = co_ref[:S, lanes].astype(F32) + dot(ubw_ref[:S, :], two_ref[:, lanes])
+        enc_ref[:, lanes] = enc.astype(BF16)
 
 
 def add_kernel(terms, *refs):
@@ -354,14 +363,11 @@
 def call(kernel, operands, outs, scratch=(), flops=0, nbytes=0, smem=False, far=0, sems=0,
          room=24):
     vmem = pl.BlockSpec(memory_space=pltpu.VMEM)
-    first = pl.BlockSpec(memory_space=pltpu.SMEM) if smem else vmem
     return pl.pallas_call(
         kernel,
-        in_specs=[pl.BlockSpec(memory_space=pltpu.HBM)] * far
-        + [vmem if far else first]
-        + [vmem] * (len(operands) - far - 1)
-        if far < len(operands)
-        else [pl.BlockSpec(memory_space=pltpu.HBM)] * far,
+        in_specs=[pl.BlockSpec(memory_space=pltpu.SMEM)] * smem
+        + [pl.BlockSpec(memory_space=pltpu.HBM)] * far
+        + [vmem] * (len(operands) - far - smem),
         out_specs=[vmem] * len(outs),
         out_shape=[jax.ShapeDtypeStruct(shape, kind) for shape, kind in outs],
         scratch_shapes=[pltpu.VMEM(shape, kind) for shape, kind in scratch]
@@ -423,21 +429,18 @@
 
 def per_device(signal, timesteps, cotangent, conv_one, down_proj, conv_two, time_proj):
     x, cot = signal[0], cotangent[0]
-    forward = [(i, i + 1) for i in range(15)]
-    backward = [(i + 1, i) for i in range(15)]
-    first, last = call(
-        edges_kernel, [x, cot], [((8, CA + CB), BF16)] * 2, nbytes=50_000, far=2, sems=4,
-        room=60,
-    )
-    left = lax.ppermute(last, "tm", forward)
-    right = lax.ppermute(first, "tm", backward)
-    emb = embed(timesteps, EMB)
-    temb = jnp.dot(emb, time_proj.astype(F32), precision=lax.Precision.HIGHEST)
     tm = lax.axis_index("tm")
     idx = jnp.stack(
         [tm & 1, (tm >> 1) & 3, tm >> 3, (tm == 0).astype(jnp.int32), (tm == 15).astype(jnp.int32)]
     ).astype(jnp.int32)
-
+    for_chip, for_core = call(
+        edges_kernel, [idx, x, cot], [((8, CA + CB), BF16)] * 2, nbytes=50_000,
+        smem=True, far=2, sems=4, room=60,
+    )
+    chip = lax.ppermute(for_chip, "tm", [(i, i + 1 if i % 2 else i - 1) for i in range(1, 15)])
+    core = lax.ppermute(for_core, "tm", [(i, i ^ 1) for i in range(16)])
+    emb = embed(timesteps, EMB)
+    temb = jnp.dot(emb, time_proj.astype(F32), precision=lax.Precision.HIGHEST)
     xp, act, cot, conv_one, down_proj = call(
         act_kernel, [x, cot, conv_one, down_proj, temb],
         [((S, 4 * CA), BF16)] * 2
@@ -447,24 +450,27 @@
     )
     a_keep, a_send, mw, uw, ab, co = call(
         forward_kernel,
-        [idx, xp, act, left, right, cot, temb, conv_one, down_proj],
+        [idx, xp, act, chip, core, cot, temb, conv_one, down_proj],
         [((16, 32, 3 * CB // 2), BF16)] * 2
         + [((E, 4 * CA), BF16), ((E, 6 * CA), BF16), ((E, CB), BF16), ((E, CB), BF16)],
-        [((2, 64, 128), F32), ((E - S, 4 * CA), F32), ((E, 3 * CB), BF16)],
+        [((2, 64, 128), F32), ((E, 3 * CB), BF16), ((CB, S), BF16)],
         2_200_000_000, 10_000_000, smem=True,
     )
     a_got = swap_core(a_send)
     dc, dh, dm = call(
-        coarse_kernel, [idx, co, cot, left, right, down_proj, conv_two],
+        coarse_kernel, [idx, co, cot, chip, core, down_proj, conv_two],
         [((E, CB), BF16), ((E, 4 * CA), BF16), ((S, 4 * CA), F32)],
-        [((E, 3 * CB), BF16)], 1_400_000_000, 7_000_000, smem=True,
+        [((E, 3 * CB), BF16), ((E, CB), F32)], 1_400_000_000, 7_000_000, smem=True,
     )
     a_parts = added([a_keep, a_got], (4, 4, 4, 4))
     a_own, a_got = ring(a_parts)
     b_keep, b_send, signal_grad = call(
         fine_kernel, [idx, xp, dc, dh, dm, mw, uw, temb, emb, conv_one],
         [((16, 48, 2 * CA), BF16)] * 2 + [((4 * S, CA), BF16)],
-        [((E, 6 * CA), BF16), ((2, 4 * S, 128), F32), ((8, CA), F32)],
+        [
+            ((E, 6 * CA), BF16), ((2, 4 * S, 128), F32), ((8, CA), F32), ((CB, S), BF16),
+            ((CA, 4 * S), BF16),
+        ],
         2_200_000_000, 11_000_000, smem=True,
     )
     b_got = swap_core(b_send)

time: 78.7 us -> 71.3 us (0.906)
  starting transfers between devices: 36.7 us -> 32.6 us
  Pallas kernels: 25.4 us -> 21.3 us
    ppermute x10, starting transfers between devices: 21.8 us -> 16.9 us  [moved(): return lax.ppermute(value, 'tm', pairs)]
    pallas_call x16, Pallas kernels: 25.4 us -> 21.3 us  [call(): pl.pallas_call(kernel, in_specs=[pl.BlockSpec(memory_space=pltpu.SMEM)] *...]
  transfers between devices with their start and end apart: 15 -> 15, of which waited for: 6 -> 5; matrix products, arithmetic and copies ran while one was open for 0% -> 0% of each run, Pallas kernels for 21% -> 19%
where the time goes in v3:
time: 71.3 us; the launch traced here: 71 us
  starting transfers between devices  32.6 us (46%)
  Pallas kernels  21.3 us (30%)
  waiting for transfers between devices  13.7 us (19%)
  local copies, waits for them, and re-layouts  1.67 us (2%)
  between operations  1.51 us (2%)
    pallas_call x16, Pallas kernels, call(): pl.pallas_call(kernel, in_specs=[pl.BlockSpec(memory_space=pltpu.SMEM)] *...  21.3 us
    ppermute x10, starting transfers between devices, moved(): return lax.ppermute(value, 'tm', pairs)  16.9 us
    all_to_all x1, starting transfers between devices, per_device(): lines = lax.all_to_all(lines, 'dp', 0, 0, tiled=True)  8.58 us
    all_to_all x1, waiting for transfers between devices, per_device(): lines = lax.all_to_all(lines, 'dp', 0, 0, tiled=True)  6.75 us
    ppermute x2, waiting for transfers between devices, swap_y(): return lax.ppermute(v, AXES, pairs)  4.63 us
    ppermute x2, starting transfers between devices, swap_y(): return lax.ppermute(v, AXES, pairs)  3.55 us
    ppermute x1, starting transfers between devices, per_device(): core = lax.ppermute(for_core, 'tm', [(i, i ^ 1) for i in range(16)])  2.94 us
    ppermute x10, waiting for transfers between devices, moved(): return lax.ppermute(value, 'tm', pairs)  2.3 us
  transfers between devices with their start and end apart: 15, of which 5 were waited for; matrix products, arithmetic and copies ran while one was open for 0% of the time, Pallas kernels for 19%

profile of v3, /device:TPU:32, one launch (start us, length us, event | category | flops | bytes accessed | tf_op | source)
XLA Modules:
  0.0 71.0 jit_solution(14843082443774328678)
XLA Ops:
  1.3 2.0 %shard_map.119 = (bf16[8,768]{1,0:T(8,128)(2,1)}, bf16[8,768]{1,0:T(8,128)(2,1)}) custom-call(s32[5]{0:T(128)} %stack.31.idx_ref, bf16[2048,256]{1,0:T(8,128)(2,1)} %bitcast.19, bf16[512,512]{1,0:T(8,128)(2,1)} %bitcast.21), custom_call_target="tpu_custom_call" | custom-call | bytes 50000 | tf_op jit(solution)/shard_map/pallas_call | solution.py:366
  3.3 0.7 collective-permute-start
  4.0 2.9 %collective-permute-start.1 = (bf16[8,768]{1,0:T(8,128)(2,1)}, bf16[8,768]{1,0:T(8,128)(2,1)S(1)}, u32[]{:S(2)}, u32[]{:S(2)}) collective-permute-start(bf16[8,768]{1,0:T(8,128)(2,1)} %get-tuple-element.52), channel_id=1, source_target_pairs={{0,1},{1,0},{2,3},{3,2},{4,5},{5,4},{6,7},{7,6},{8,9},{9,8},{10,11... | collective-permute-start | bytes 36872 | tf_op jit(solution)/shard_map/ppermute | solution.py:441
  7.9 1.0 %copy-done.4 = bf16[768,256]{1,0:T(8,128)(2,1)S(1)} copy-done((bf16[768,256]{1,0:T(8,128)(2,1)S(1)}, bf16[768,256]{1,0:T(8,128)(2,1)}, u32[]{:S(2)}) %copy-start.4) | copy-done | bytes 393240
  8.9 1.9 %shard_map.118 = (bf16[512,1024]{1,0:T(8,128)(2,1)S(1)}, bf16[512,1024]{1,0:T(8,128)(2,1)S(1)}, bf16[512,512]{1,0:T(8,128)(2,1)S(1)}, bf16[768,256]{1,0:T(8,128)(2,1)S(1)}, bf16[1024,512]{1,0:T(8,128)(2,1)S(1)}) custom-call(bf16[2048,256]{1,0:T(8,128)(2,1)S(1)} %bitcast.20, bf16[512,512]{1,0:T(8,128)(2,1)S(1)} %bitcast.22, bf16[768,256]{1,0:T(8,128)(2,1)S(1)} %copy-done.4, ...), custom_call_target="tpu_custom_call" | custom-call | flops 50000000 | bytes 6500000 | tf_op jit(solution)/shard_map/pallas_call | solution.py:366
  10.8 4.0 %shard_map.120 = (bf16[16,32,768]{2,1,0:T(8,128)(2,1)S(1)}, bf16[16,32,768]{2,1,0:T(8,128)(2,1)S(1)}, bf16[528,1024]{1,0:T(8,128)(2,1)S(1)}, bf16[528,1536]{1,0:...) custom-call(s32[5]{0:T(128)S(1)} %copy-done.5, ...), custom_call_target="tpu_custom_call" | custom-call | flops 2200000000 | bytes 10000000 | tf_op jit(solution)/shard_map/pallas_call | solution.py:366
  14.9 3.3 %shard_map.122 = (bf16[528,512]{1,0:T(8,128)(2,1)S(1)}, bf16[528,1024]{1,0:T(8,128)(2,1)S(1)}, f32[512,1024]{1,0:T(8,128)S(1)}) custom-call(s32[5]{0:T(128)S(1)} %copy-done.5, bf16[528,512]{1,0:T(8,128)(2,1)S(1)} %get-tuple-element.56.co_ref, bf16[512,512]{1,0:T(8,128)(2,1)S(1)} %get-tuple-element.53.cot_ref, ...), custom_call_target="tpu_custom_call" | custom-call | flops 1400000000 | bytes 7000000 | tf_op jit(solution)/shard_map/pallas_call | solution.py:366
  18.2 6.0 %shard_map.123 = (bf16[16,48,512]{2,1,0:T(8,128)(2,1)S(1)}, bf16[16,48,512]{2,1,0:T(8,128)(2,1)S(1)}, bf16[2048,256]{1,0:T(8,128)(2,1)}) custom-call(s32[5]{0:T(128)S(1)} %copy-done.5, bf16[512,1024]{1,0:T(8,128)(2,1)S(1)} %get-tuple-element.49.xp_ref, bf16[528,512]{1,0:T(8,128)(2,1)S(1)} %get-tuple-element.58.dc_ref, ...), custom_call_target="tpu_custom_call" | custom-call | flops 2200000000 | bytes 11000000 | tf_op jit(solution)/shard_map/pallas_call | solution.py:366
  24.9 1.6 %collective-permute-start.3 = (bf16[4,32,768]{2,1,0:T(8,128)(2,1)S(1)}, bf16[4,32,768]{2,1,0:T(8,128)(2,1)S(1)}, u32[]{:S(2)}, u32[]{:S(2)}) collective-permute-start(bf16[4,32,768]{2,1,0:T(8,128)(2,1)S(1)} %get-tuple-element.67), channel_id=1, source_target_pairs={{0,2},{1,3},{2,0},{3,1},{4,6},{5,7},{6,4},{7,5},{8,10},{9,11},{10,... | collective-permute-start | bytes 589832 | tf_op jit(solution)/shard_map/ppermute | solution.py:389
  26.5 3.0 %collective-permute-start.5 = (bf16[4,32,768]{2,1,0:T(8,128)(2,1)S(1)}, bf16[4,32,768]{2,1,0:T(8,128)(2,1)S(1)}, u32[]{:S(2)}, u32[]{:S(2)}) collective-permute-start(bf16[4,32,768]{2,1,0:T(8,128)(2,1)S(1)} %get-tuple-element.71), channel_id=1, source_target_pairs={{0,6},{1,7},{2,4},{3,5},{4,2},{5,3},{6,0},{7,1},{8,14},{9,15},{10,... | collective-permute-start | bytes 589832 | tf_op jit(solution)/shard_map/ppermute | solution.py:389
  29.7 1.6 %collective-permute-start.9 = (bf16[4,48,512]{2,1,0:T(8,128)(2,1)S(1)}, bf16[4,48,512]{2,1,0:T(8,128)(2,1)S(1)}, u32[]{:S(2)}, u32[]{:S(2)}) collective-permute-start(bf16[4,48,512]{2,1,0:T(8,128)(2,1)S(1)} %get-tuple-element.79), channel_id=1, source_target_pairs={{0,2},{1,3},{2,0},{3,1},{4,6},{5,7},{6,4},{7,5},{8,10},{9,11},{10,... | collective-permute-start | bytes 589832 | tf_op jit(solution)/shard_map/ppermute | solution.py:389
  31.3 0.6 collective-permute-start.11
  32.0 5.4 %collective-permute-start.4 = (bf16[2,32,768]{2,1,0:T(8,128)(2,1)S(1)}, bf16[2,32,768]{2,1,0:T(8,128)(2,1)S(1)}, u32[]{:S(2)}, u32[]{:S(2)}) collective-permute-start(bf16[2,32,768]{2,1,0:T(8,128)(2,1)S(1)} %get-tuple-element.69), channel_id=1, source_target_pairs={{0,6},{1,7},{2,4},{3,5},{4,2},{5,3},{6,0},{7,1},{8,14},{9,15},{10,... | collective-permute-start | bytes 294920 | tf_op jit(solution)/shard_map/ppermute | solution.py:389
  37.5 4.0 %collective-permute-start.10 = (bf16[2,48,512]{2,1,0:T(8,128)(2,1)S(1)}, bf16[2,48,512]{2,1,0:T(8,128)(2,1)S(1)}, u32[]{:S(2)}, u32[]{:S(2)}) collective-permute-start(bf16[2,48,512]{2,1,0:T(8,128)(2,1)S(1)} %get-tuple-element.81), channel_id=1, source_target_pairs={{0,6},{1,7},{2,4},{3,5},{4,2},{5,3},{6,0},{7,1},{8,14},{9,15},{10,... | collective-permute-start | bytes 294920 | tf_op jit(solution)/shard_map/ppermute | solution.py:389
  42.1 2.3 %collective-permute-start.7 = (bf16[32,1536]{1,0:T(8,128)(2,1)S(1)}, bf16[32,1536]{1,0:T(8,128)(2,1)S(1)}, u32[]{:S(2)}, u32[]{:S(2)}) collective-permute-start(bf16[32,1536]{1,0:T(8,128)(2,1)S(1)} %get-tuple-element.75), channel_id=1, source_target_pairs={{0,136},{1,137},{2,138},{3,139},{4,140},{5,141},{6,142},{7,143},{8... | collective-permute-start | bytes 294920 | tf_op jit(solution)/shard_map/ppermute | solution.py:402
  44.4 1.9 %collective-permute-done.12.got_v = bf16[2,48,512]{2,1,0:T(8,128)(2,1)S(1)} collective-permute-done((bf16[2,48,512]{2,1,0:T(8,128)(2,1)S(1)}, bf16[2,48,512]{2,1,0:T(8,128)(2,1)S(1)}, u32[]{:S(2)}, u32[]{:S(2)}) %collective-permute-start.12) | collective-permute-done | bytes 98336 | tf_op jit(solution)/shard_map/ppermute | solution.py:389
  46.3 1.3 %collective-permute-start.13 = (bf16[48,1024]{1,0:T(8,128)(2,1)S(1)}, bf16[48,1024]{1,0:T(8,128)(2,1)S(1)}, u32[]{:S(2)}, u32[]{:S(2)}) collective-permute-start(bf16[48,1024]{1,0:T(8,128)(2,1)S(1)} %get-tuple-element.87), channel_id=1, source_target_pairs={{0,136},{1,137},{2,138},{3,139},{4,140},{5,141},{6,142},{7,143},{8... | collective-permute-start | bytes 294920 | tf_op jit(solution)/shard_map/ppermute | solution.py:402
  47.6 0.9 %collective-permute-done.7.a_got = bf16[32,1536]{1,0:T(8,128)(2,1)S(1)} collective-permute-done((bf16[32,1536]{1,0:T(8,128)(2,1)S(1)}, bf16[32,1536]{1,0:T(8,128)(2,1)S(1)}, u32[]{:S(2)}, u32[]{:S(2)}) %collective-permute-start.7) | collective-permute-done | bytes 98336 | tf_op jit(solution)/shard_map/ppermute | solution.py:402
  48.5 3.8 %collective-permute-done.13.b_got = bf16[48,1024]{1,0:T(8,128)(2,1)S(1)} collective-permute-done((bf16[48,1024]{1,0:T(8,128)(2,1)S(1)}, bf16[48,1024]{1,0:T(8,128)(2,1)S(1)}, u32[]{:S(2)}, u32[]{:S(2)}) %collective-permute-start.13) | collective-permute-done | bytes 98336 | tf_op jit(solution)/shard_map/ppermute | solution.py:402
  52.3 0.9 %shard_map.132 = bf16[16,48,128]{2,1,0:T(8,128)(2,1)} custom-call(bf16[32,1536]{1,0:T(8,128)(2,1)S(1)} %get-tuple-element.74.a_ref, bf16[32,1536]{1,0:T(8,128)(2,1)S(1)} %collective-permute-done.7.a_got, bf16[48,1024]{1,0:T(8,128)(2,1)S(1)} %get-tuple-element.86.b_ref, bf16[48,1024]{1,0:T(8,128)(2,1)S(1)} %collective-permute-done.13.b_got), custom_call_target="tpu_custom_call" | custom-call | bytes 900000 | tf_op jit(solution)/shard_map/pallas_call | solution.py:366
  53.1 8.6 %all-to-all-start = ((bf16[16,48,128]{2,1,0:T(8,128)(2,1)}), bf16[16,48,128]{2,1,0:T(8,128)(2,1)S(1)}, u32[]{:S(2)}, u32[]{:S(2)}) async-start(bf16[16,48,128]{2,1,0:T(8,128)(2,1)} %shard_map.132), calls=%async_computation | async-start | bytes 393216 | tf_op jit(solution)/shard_map/all_to_all | solution.py:487
  61.7 1.8 %shard_map.121 = bf16[512,512]{1,0:T(8,128)(2,1)} custom-call(bf16[528,512]{1,0:T(8,128)(2,1)S(1)} %get-tuple-element.56.co_ref, bf16[528,512]{1,0:T(8,128)(2,1)S(1)} %get-tuple-element.57.ab_ref, bf16[1536,512]{1,0:T(8,128)(2,1)S(1)} %copy-done.3), custom_call_target="tpu_custom_call" | custom-call | flops 800000000 | bytes 3000000 | tf_op jit(solution)/shard_map/pallas_call | solution.py:366
  63.5 6.8 %all-to-all-done.in_ref = bf16[16,48,128]{2,1,0:T(8,128)(2,1)S(1)} async-done(((bf16[16,48,128]{2,1,0:T(8,128)(2,1)}), bf16[16,48,128]{2,1,0:T(8,128)(2,1)S(1)}, u32[]{:S(2)}, u32[]{:S(2)}) %all-to-all-start) | async-done | bytes 196640 | tf_op jit(solution)/shard_map/all_to_all | solution.py:487
  70.2 0.8 %shard_map.133 = (f32[16,48]{1,0:T(8,128)}, f32[32,64]{1,0:T(8,128)}, f32[32,96]{1,0:T(8,128)}, f32[16,16]{1,0:T(8,128)}) custom-call(bf16[16,48,128]{2,1,0:T(8,128)(2,1)S(1)} %all-to-all-done.in_ref), custom_call_target="tpu_custom_call" | custom-call | bytes 300000 | tf_op jit(solution)/shard_map/pallas_call | solution.py:366
  (38 shorter events, 2.7 us)
Async XLA Ops:
  0.6 7.0 %copy-start = (bf16[256,256]{1,0:T(8,128)(2,1)S(1)}, bf16[256,256]{1,0:T(8,128)(2,1)}, u32[]{:S(2)}) copy-start(bf16[256,256]{1,0:T(8,128)(2,1)} %param.13) | copy-start | bytes 393220
  0.6 7.2 %copy-start.2 = (bf16[1,512,512]{2,1,0:T(8,128)(2,1)S(1)}, bf16[1,512,512]{2,1,0:T(8,128)(2,1)}, u32[]{:S(2)}) copy-start(bf16[1,512,512]{2,1,0:T(8,128)(2,1)} %param.9) | copy-start | bytes 1572868
  0.7 7.2 %copy-start.1 = (bf16[1,2048,256]{2,1,0:T(8,128)(2,1)S(1)}, bf16[1,2048,256]{2,1,0:T(8,128)(2,1)}, u32[]{:S(2)}) copy-start(bf16[1,2048,256]{2,1,0:T(8,128)(2,1)} %param.7) | copy-start | bytes 3145732
  3.3 7.4 %collective-permute-start = (bf16[8,768]{1,0:T(8,128)(2,1)}, bf16[8,768]{1,0:T(8,128)(2,1)S(1)}, u32[]{:S(2)}, u32[]{:S(2)}) collective-permute-start(bf16[8,768]{1,0:T(8,128)(2,1)} %get-tuple-element.51), channel_id=1, source_target_pairs={{1,2},{2,1},{3,4},{4,3},{5,6},{6,5},{7,8},{8,7},{9,10},{10,9},{11,... | collective-permute-start | bytes 36872 | tf_op jit(solution)/shard_map/ppermute | solution.py:440
  4.0 6.8 %collective-permute-start.1 = (bf16[8,768]{1,0:T(8,128)(2,1)}, bf16[8,768]{1,0:T(8,128)(2,1)S(1)}, u32[]{:S(2)}, u32[]{:S(2)}) collective-permute-start(bf16[8,768]{1,0:T(8,128)(2,1)} %get-tuple-element.52), channel_id=1, source_target_pairs={{0,1},{1,0},{2,3},{3,2},{4,5},{5,4},{6,7},{7,6},{8,9},{9,8},{10,11... | collective-permute-start | bytes 36872 | tf_op jit(solution)/shard_map/ppermute | solution.py:441
  7.7 3.1 %copy-start.5 = (s32[5]{0:T(128)S(1)}, s32[5]{0:T(128)}, u32[]{:S(2)}) copy-start(s32[5]{0:T(128)} %stack.31.idx_ref) | copy-start | bytes 64
  7.9 1.0 %copy-start.4 = (bf16[768,256]{1,0:T(8,128)(2,1)S(1)}, bf16[768,256]{1,0:T(8,128)(2,1)}, u32[]{:S(2)}) copy-start(bf16[768,256]{1,0:T(8,128)(2,1)} %one_ref.1) | copy-start | bytes 1179652
  10.8 4.1 %copy-start.3 = (bf16[1536,512]{1,0:T(8,128)(2,1)S(1)}, bf16[1536,512]{1,0:T(8,128)(2,1)}, u32[]{:S(2)}) copy-start(bf16[1536,512]{1,0:T(8,128)(2,1)} %two_ref.3) | copy-start | bytes 4718596
  14.8 10.0 %collective-permute-start.2 = (bf16[16,32,768]{2,1,0:T(8,128)(2,1)S(1)}, bf16[16,32,768]{2,1,0:T(8,128)(2,1)S(1)}, u32[]{:S(2)}, u32[]{:S(2)}) collective-permute-start(bf16[16,32,768]{2,1,0:T(8,128)(2,1)S(1)} %get-tuple-element.65), channel_id=1, source_target_pairs={{0,1},{1,0},{2,3},{3,2},{4,5},{5,4},{6,7},{7,6},{8,9},{9,8},{10,11... | collective-permute-start | bytes 2359304 | tf_op jit(solution)/shard_map/ppermute | solution.py:389
  24.3 5.2 %collective-permute-start.8 = (bf16[16,48,512]{2,1,0:T(8,128)(2,1)S(1)}, bf16[16,48,512]{2,1,0:T(8,128)(2,1)S(1)}, u32[]{:S(2)}, u32[]{:S(2)}) collective-permute-start(bf16[16,48,512]{2,1,0:T(8,128)(2,1)S(1)} %get-tuple-element.77), channel_id=1, source_target_pairs={{0,1},{1,0},{2,3},{3,2},{4,5},{5,4},{6,7},{7,6},{8,9},{9,8},{10,11... | collective-permute-start | bytes 2359304 | tf_op jit(solution)/shard_map/ppermute | solution.py:389
  24.9 7.0 %collective-permute-start.3 = (bf16[4,32,768]{2,1,0:T(8,128)(2,1)S(1)}, bf16[4,32,768]{2,1,0:T(8,128)(2,1)S(1)}, u32[]{:S(2)}, u32[]{:S(2)}) collective-permute-start(bf16[4,32,768]{2,1,0:T(8,128)(2,1)S(1)} %get-tuple-element.67), channel_id=1, source_target_pairs={{0,2},{1,3},{2,0},{3,1},{4,6},{5,7},{6,4},{7,5},{8,10},{9,11},{10,... | collective-permute-start | bytes 589832 | tf_op jit(solution)/shard_map/ppermute | solution.py:389
  26.5 10.8 %collective-permute-start.5 = (bf16[4,32,768]{2,1,0:T(8,128)(2,1)S(1)}, bf16[4,32,768]{2,1,0:T(8,128)(2,1)S(1)}, u32[]{:S(2)}, u32[]{:S(2)}) collective-permute-start(bf16[4,32,768]{2,1,0:T(8,128)(2,1)S(1)} %get-tuple-element.71), channel_id=1, source_target_pairs={{0,6},{1,7},{2,4},{3,5},{4,2},{5,3},{6,0},{7,1},{8,14},{9,15},{10,... | collective-permute-start | bytes 589832 | tf_op jit(solution)/shard_map/ppermute | solution.py:389
  29.7 7.8 %collective-permute-start.9 = (bf16[4,48,512]{2,1,0:T(8,128)(2,1)S(1)}, bf16[4,48,512]{2,1,0:T(8,128)(2,1)S(1)}, u32[]{:S(2)}, u32[]{:S(2)}) collective-permute-start(bf16[4,48,512]{2,1,0:T(8,128)(2,1)S(1)} %get-tuple-element.79), channel_id=1, source_target_pairs={{0,2},{1,3},{2,0},{3,1},{4,6},{5,7},{6,4},{7,5},{8,10},{9,11},{10,... | collective-permute-start | bytes 589832 | tf_op jit(solution)/shard_map/ppermute | solution.py:389
  31.3 10.2 %collective-permute-start.11 = (bf16[4,48,512]{2,1,0:T(8,128)(2,1)S(1)}, bf16[4,48,512]{2,1,0:T(8,128)(2,1)S(1)}, u32[]{:S(2)}, u32[]{:S(2)}) collective-permute-start(bf16[4,48,512]{2,1,0:T(8,128)(2,1)S(1)} %get-tuple-element.83), channel_id=1, source_target_pairs={{0,6},{1,7},{2,4},{3,5},{4,2},{5,3},{6,0},{7,1},{8,14},{9,15},{10,... | collective-permute-start | bytes 589832 | tf_op jit(solution)/shard_map/ppermute | solution.py:389
  32.0 9.7 %collective-permute-start.4 = (bf16[2,32,768]{2,1,0:T(8,128)(2,1)S(1)}, bf16[2,32,768]{2,1,0:T(8,128)(2,1)S(1)}, u32[]{:S(2)}, u32[]{:S(2)}) collective-permute-start(bf16[2,32,768]{2,1,0:T(8,128)(2,1)S(1)} %get-tuple-element.69), channel_id=1, source_target_pairs={{0,6},{1,7},{2,4},{3,5},{4,2},{5,3},{6,0},{7,1},{8,14},{9,15},{10,... | collective-permute-start | bytes 294920 | tf_op jit(solution)/shard_map/ppermute | solution.py:389
  37.4 4.7 %collective-permute-start.6 = (bf16[2,32,768]{2,1,0:T(8,128)(2,1)S(1)}, bf16[2,32,768]{2,1,0:T(8,128)(2,1)S(1)}, u32[]{:S(2)}, u32[]{:S(2)}) collective-permute-start(bf16[2,32,768]{2,1,0:T(8,128)(2,1)S(1)} %get-tuple-element.73), channel_id=1, source_target_pairs={{0,2},{1,3},{2,0},{3,1},{4,6},{5,7},{6,4},{7,5},{8,10},{9,11},{10,... | collective-permute-start | bytes 294920 | tf_op jit(solution)/shard_map/ppermute | solution.py:389
  37.5 6.9 %collective-permute-start.10 = (bf16[2,48,512]{2,1,0:T(8,128)(2,1)S(1)}, bf16[2,48,512]{2,1,0:T(8,128)(2,1)S(1)}, u32[]{:S(2)}, u32[]{:S(2)}) collective-permute-start(bf16[2,48,512]{2,1,0:T(8,128)(2,1)S(1)} %get-tuple-element.81), channel_id=1, source_target_pairs={{0,6},{1,7},{2,4},{3,5},{4,2},{5,3},{6,0},{7,1},{8,14},{9,15},{10,... | collective-permute-start | bytes 294920 | tf_op jit(solution)/shard_map/ppermute | solution.py:389
  41.6 4.7 %collective-permute-start.12 = (bf16[2,48,512]{2,1,0:T(8,128)(2,1)S(1)}, bf16[2,48,512]{2,1,0:T(8,128)(2,1)S(1)}, u32[]{:S(2)}, u32[]{:S(2)}) collective-permute-start(bf16[2,48,512]{2,1,0:T(8,128)(2,1)S(1)} %get-tuple-element.85), channel_id=1, source_target_pairs={{0,2},{1,3},{2,0},{3,1},{4,6},{5,7},{6,4},{7,5},{8,10},{9,11},{10,... | collective-permute-start | bytes 294920 | tf_op jit(solution)/shard_map/ppermute | solution.py:389
  42.1 6.4 %collective-permute-start.7 = (bf16[32,1536]{1,0:T(8,128)(2,1)S(1)}, bf16[32,1536]{1,0:T(8,128)(2,1)S(1)}, u32[]{:S(2)}, u32[]{:S(2)}) collective-permute-start(bf16[32,1536]{1,0:T(8,128)(2,1)S(1)} %get-tuple-element.75), channel_id=1, source_target_pairs={{0,136},{1,137},{2,138},{3,139},{4,140},{5,141},{6,142},{7,143},{8... | collective-permute-start | bytes 294920 | tf_op jit(solution)/shard_map/ppermute | solution.py:402
  46.3 5.9 %collective-permute-start.13 = (bf16[48,1024]{1,0:T(8,128)(2,1)S(1)}, bf16[48,1024]{1,0:T(8,128)(2,1)S(1)}, u32[]{:S(2)}, u32[]{:S(2)}) collective-permute-start(bf16[48,1024]{1,0:T(8,128)(2,1)S(1)} %get-tuple-element.87), channel_id=1, source_target_pairs={{0,136},{1,137},{2,138},{3,139},{4,140},{5,141},{6,142},{7,143},{8... | collective-permute-start | bytes 294920 | tf_op jit(solution)/shard_map/ppermute | solution.py:402
  53.1 17.1 %all-to-all-start = ((bf16[16,48,128]{2,1,0:T(8,128)(2,1)}), bf16[16,48,128]{2,1,0:T(8,128)(2,1)S(1)}, u32[]{:S(2)}, u32[]{:S(2)}) async-start(bf16[16,48,128]{2,1,0:T(8,128)(2,1)} %shard_map.132), calls=%async_computation | async-start | bytes 393216 | tf_op jit(solution)/shard_map/all_to_all | solution.py:487

commit v4 on v3

--- a/solution.py
+++ b/solution.py
@@ -39,7 +39,7 @@
     past = jnp.logical_and(row >= S, row < S + margin)
     before = row >= E - margin
     off = jnp.logical_or(
-        jnp.logical_and(past, idx_ref[4] == 1), jnp.logical_and(before, idx_ref[3] == 1)
+        jnp.logical_and(past, idx_ref[0] == 15), jnp.logical_and(before, idx_ref[0] == 0)
     )
     return jnp.where(off, 0.0, 1.0)
 
@@ -57,15 +57,15 @@
 
 
 def places(idx_ref, xx, y):
-    apart = xx ^ idx_ref[1]
-    side = y ^ idx_ref[2]
+    apart = xx ^ ((idx_ref[0] >> 1) & 3)
+    side = y ^ (idx_ref[0] >> 3)
     first = jnp.where(apart == 3, 1, jnp.where(apart == 0, 0, apart + 1))
     second = jnp.where(apart < 2, apart, 5 - apart)
     return first * 2 + side, 8 + second * 2 + side
 
 
 def put(idx_ref, keep_ref, send_ref, xx, y, rows, even, odd, at=0):
-    core, half = idx_ref[0], keep_ref.shape[2]
+    core, half = idx_ref[0] & 1, keep_ref.shape[2]
     keep = jnp.where(core == 0, even, odd).astype(BF16)
     send = jnp.where(core == 0, odd, even).astype(BF16)
     for h, where in enumerate(places(idx_ref, xx, y)):
@@ -87,7 +87,7 @@
 def edges_kernel(idx_ref, x_ref, cot_ref, one_ref, two_ref, sem):
     copies = []
     for n, out in enumerate((one_ref, two_ref)):
-        last = idx_ref[0] ^ n
+        last = (idx_ref[0] & 1) ^ n
         rows = pl.ds(pl.multiple_of(last * (4 * S - 8), 8), 8)
         copies.append(pltpu.make_async_copy(x_ref.at[rows, :], out.at[:, :CA], sem.at[2 * n]))
         rows = pl.ds(pl.multiple_of(last * (S - 8), 8), 8)
@@ -103,14 +103,14 @@
 def sides(idx_ref, chip_ref, core_ref, rows, lanes):
     chip = chip_ref[:, lanes].astype(F32)
     core = core_ref[:, lanes].astype(F32)
-    even = idx_ref[0] == 0
+    even = (idx_ref[0] & 1) == 0
     before, behind = jnp.where(even, chip, core), jnp.where(even, core, chip)
     return before[8 - rows :], behind[:rows]
 
 
 def act_kernel(
-    x_ref, cot_ref, one_ref, down_ref, temb_ref,
-    xp_ref, act_ref, cot_out, one_out, down_out,
+    x_ref, cot_ref, down_ref, temb_ref,
+    xp_ref, act_ref, cot_out, down_out,
     xs_ref, xb_ref, sem,
 ):
     parts = []
@@ -118,9 +118,8 @@
         rows = pl.ds(512 * k, 512)
         parts.append(pltpu.make_async_copy(x_ref.at[rows, :], xb_ref.at[rows, :], sem.at[k]))
     whole = [
-        pltpu.make_async_copy(one_ref, one_out, sem.at[4]),
-        pltpu.make_async_copy(cot_ref, cot_out, sem.at[5]),
-        pltpu.make_async_copy(down_ref, down_out, sem.at[6]),
+        pltpu.make_async_copy(cot_ref, cot_out, sem.at[4]),
+        pltpu.make_async_copy(down_ref, down_out, sem.at[5]),
     ]
     for copy in parts + whole:
         copy.start()
@@ -239,9 +238,9 @@
 
 
 def fine_kernel(
-    idx_ref, xp_ref, dc_ref, dh_ref, dm_ref, mw_ref, uw_ref, temb_ref, emb_ref, one_ref,
-    keep_ref, send_ref, sg_ref,
-    dhw_ref, ys_ref, dt_ref, at_ref, dt_all_ref,
+    idx_ref, xp_ref, dc_ref, dh_ref, mw_ref, uw_ref, temb_ref, emb_ref, one_ref,
+    keep_ref, send_ref, dp_ref,
+    dhw_ref, dt_ref, at_ref, dt_all_ref,
 ):
     scaling = 1.0 / math.sqrt(16 * 32768)
     dhw_ref[:, CA : 5 * CA] = dh_ref[...]
@@ -265,22 +264,11 @@
             back += dot_nt(dhw_ref[r, (j + 1) * CA : (j + 2) * CA], one_ref[CA : 2 * CA, :])
             back += dot_nt(dhw_ref[r, lanes], one_ref[2 * CA :, :])
             v = xp_ref[r, lanes].astype(F32)
-            factor = rms(v)
-            normed = v * factor
-            pre = normed + temb_ref[...]
+            pre = v * rms(v) + temb_ref[...]
             sig = sigmoid(pre)
             d_pre = back * (sig * (1.0 + pre * (1.0 - sig)))
             dt_ref[...] += d_pre.reshape(32, 8, CA).sum(0)
-            m = jnp.mean(d_pre * normed, -1, keepdims=True)
-            grad = dm_ref[r, lanes] + factor * (d_pre - normed * m)
-            ys_ref[0, pl.ds(i * 1024 + j, 256, stride=4), :] = grad[:, :128]
-            ys_ref[1, pl.ds(i * 1024 + j, 256, stride=4), :] = grad[:, 128:]
-
-    @pl.loop(0, 16)
-    def _(i):
-        r = rows_of(i, 128)
-        sg_ref[r, :128] = ys_ref[0, r, :].astype(BF16)
-        sg_ref[r, 128:] = ys_ref[1, r, :].astype(BF16)
+            dp_ref[r, lanes] = d_pre
 
     for n in range(4):
         down = dot(at_ref[...], mw_ref[:S, n * CA : (n + 1) * CA]) * scaling
@@ -303,6 +291,25 @@
             put(idx_ref, keep_ref, send_ref, c % 4, c // 4, slice(32, 48), even, odd, n * CA)
 
 
+def signal_kernel(xp_ref, dm_ref, dp_ref, sg_ref, ys_ref):
+    @pl.loop(0, 8)
+    def _(i):
+        r = rows_of(i, 64)
+        for j in range(4):
+            lanes = slice(j * CA, (j + 1) * CA)
+            v = xp_ref[r, lanes].astype(F32)
+            factor = rms(v)
+            normed = v * factor
+            d_pre = dp_ref[r, lanes]
+            m = jnp.mean(d_pre * normed, -1, keepdims=True)
+            grad = dm_ref[r, lanes] + factor * (d_pre - normed * m)
+            ys_ref[0, pl.ds(i * 256 + j, 64, stride=4), :] = grad[:, :128]
+            ys_ref[1, pl.ds(i * 256 + j, 64, stride=4), :] = grad[:, 128:]
+        r = rows_of(i, 256)
+        sg_ref[r, :128] = ys_ref[0, r, :].astype(BF16)
+        sg_ref[r, 128:] = ys_ref[1, r, :].astype(BF16)
+
+
 def encoded_kernel(co_ref, ab_ref, two_ref, enc_ref, ubw_ref):
     act_b = ab_ref[...].astype(F32)
     ubw_ref[:, CB : 2 * CB] = ab_ref[...]
@@ -337,7 +344,7 @@
 
 
 def lines_kernel(a_ref, a_got, b_ref, b_got, out_ref):
-    two = a_ref[...].astype(F32) + a_got[...].astype(F32)
+    two = a_ref[0].astype(F32) + a_got[0].astype(F32)
     rest = b_ref[...].astype(F32) + b_got[...].astype(F32)
     for d in range(16):
         down = rest[:32, 64 * d : 64 * d + 64]
@@ -430,9 +437,7 @@
 def per_device(signal, timesteps, cotangent, conv_one, down_proj, conv_two, time_proj):
     x, cot = signal[0], cotangent[0]
     tm = lax.axis_index("tm")
-    idx = jnp.stack(
-        [tm & 1, (tm >> 1) & 3, tm >> 3, (tm == 0).astype(jnp.int32), (tm == 15).astype(jnp.int32)]
-    ).astype(jnp.int32)
+    idx = tm.astype(jnp.int32).reshape(1)
     for_chip, for_core = call(
         edges_kernel, [idx, x, cot], [((8, CA + CB), BF16)] * 2, nbytes=50_000,
         smem=True, far=2, sems=4, room=60,
@@ -441,17 +446,17 @@
     core = lax.ppermute(for_core, "tm", [(i, i ^ 1) for i in range(16)])
     emb = embed(timesteps, EMB)
     temb = jnp.dot(emb, time_proj.astype(F32), precision=lax.Precision.HIGHEST)
-    xp, act, cot, conv_one, down_proj = call(
-        act_kernel, [x, cot, conv_one, down_proj, temb],
+    xp, act, cot, down_proj = call(
+        act_kernel, [x, cot, down_proj, temb],
         [((S, 4 * CA), BF16)] * 2
-        + [(v.shape, BF16) for v in (cot, conv_one, down_proj)],
-        [((2, 4 * S, 128), F32), ((4 * S, CA), BF16)], 50_000_000, 6_500_000, far=4, sems=7,
+        + [(v.shape, BF16) for v in (cot, down_proj)],
+        [((2, 4 * S, 128), F32), ((4 * S, CA), BF16)], 50_000_000, 6_500_000, far=3, sems=6,
         room=48,
     )
     a_keep, a_send, mw, uw, ab, co = call(
         forward_kernel,
         [idx, xp, act, chip, core, cot, temb, conv_one, down_proj],
-        [((16, 32, 3 * CB // 2), BF16)] * 2
+        [((8, 32, 3 * CB), BF16)] * 2
         + [((E, 4 * CA), BF16), ((E, 6 * CA), BF16), ((E, CB), BF16), ((E, CB), BF16)],
         [((2, 64, 128), F32), ((E, 3 * CB), BF16), ((CB, S), BF16)],
         2_200_000_000, 10_000_000, smem=True,
@@ -462,15 +467,12 @@
         [((E, CB), BF16), ((E, 4 * CA), BF16), ((S, 4 * CA), F32)],
         [((E, 3 * CB), BF16), ((E, CB), F32)], 1_400_000_000, 7_000_000, smem=True,
     )
-    a_parts = added([a_keep, a_got], (4, 4, 4, 4))
-    a_own, a_got = ring(a_parts)
-    b_keep, b_send, signal_grad = call(
-        fine_kernel, [idx, xp, dc, dh, dm, mw, uw, temb, emb, conv_one],
-        [((16, 48, 2 * CA), BF16)] * 2 + [((4 * S, CA), BF16)],
-        [
-            ((E, 6 * CA), BF16), ((2, 4 * S, 128), F32), ((8, CA), F32), ((CB, S), BF16),
-            ((CA, 4 * S), BF16),
-        ],
+    a_own, a_send = added([a_keep, a_got], (4, 4))
+    a_got = swap_x(a_send, 1)
+    b_keep, b_send, d_pre = call(
+        fine_kernel, [idx, xp, dc, dh, mw, uw, temb, emb, conv_one],
+        [((16, 48, 2 * CA), BF16)] * 2 + [((S, 4 * CA), F32)],
+        [((E, 6 * CA), BF16), ((8, CA), F32), ((CB, S), BF16), ((CA, 4 * S), BF16)],
         2_200_000_000, 11_000_000, smem=True,
     )
     b_got = swap_core(b_send)
@@ -478,7 +480,15 @@
         encoded_kernel, [co, ab, conv_two], [((S, CB), BF16)],
         [((E, 3 * CB), BF16)], 800_000_000, 3_000_000,
     )
+    (signal_grad,) = call(
+        signal_kernel, [xp, dm, d_pre], [((4 * S, CA), BF16)],
+        [((2, 4 * S, 128), F32)], 20_000_000, 6_000_000,
+    )
     b_parts = added([b_keep, b_got], (4, 4, 4, 4))
+    a_own, a_send = added([a_own, a_got], (2, 2))
+    a_got = swap_x(a_send, 3)
+    a_own, a_send = added([a_own, a_got], (1, 1))
+    a_got = swap_y(a_send)
     b_own, b_got = ring(b_parts)
     (lines,) = call(
         lines_kernel, [a_own, a_got, b_own, b_got],

time: 71.3 us -> 72.5 us (1.017)
  waiting for transfers between devices: 13.7 us -> 16.3 us
  Pallas kernels: 21.3 us -> 19.5 us
  local copies, waits for them, and re-layouts: 1.67 us -> 3.15 us
  starting transfers between devices: 32.6 us -> 31.6 us
    ppermute x10 -> x8, waiting for transfers between devices: 2.3 us -> 9.69 us  [moved(): return lax.ppermute(value, 'tm', pairs)]
    all_to_all x1, waiting for transfers between devices: 6.75 us -> 2.32 us  [per_device(): lines = lax.all_to_all(lines, 'dp', 0, 0, tiled=True)]
    unnamed x12 -> x26, local copies, waits for them, and re-layouts: 1.07 us -> 3.15 us
    pallas_call x16, Pallas kernels: 21.3 us -> 19.5 us  [call(): pl.pallas_call(kernel, in_specs=[pl.BlockSpec(memory_space=pltpu.SMEM)] *...]
    ppermute x10 -> x8, starting transfers between devices: 16.9 us -> 15.9 us  [moved(): return lax.ppermute(value, 'tm', pairs)]
  transfers between devices with their start and end apart: 15 -> 13, of which waited for: 5 -> 7; matrix products, arithmetic and copies ran while one was open for 0% -> 0% of each run, Pallas kernels for 19% -> 19%
where the time goes in v4:
time: 72.5 us; the launch traced here: 72.2 us
  starting transfers between devices  31.6 us (44%)
  Pallas kernels  19.5 us (27%)
  waiting for transfers between devices  16.3 us (22%)
  local copies, waits for them, and re-layouts  3.15 us (4%)
  between operations  1.52 us (2%)
    pallas_call x16, Pallas kernels, call(): pl.pallas_call(kernel, in_specs=[pl.BlockSpec(memory_space=pltpu.SMEM)] *...  19.5 us
    ppermute x8, starting transfers between devices, moved(): return lax.ppermute(value, 'tm', pairs)  15.9 us
    ppermute x8, waiting for transfers between devices, moved(): return lax.ppermute(value, 'tm', pairs)  9.69 us
    all_to_all x1, starting transfers between devices, per_device(): lines = lax.all_to_all(lines, 'dp', 0, 0, tiled=True)  8.59 us
    ppermute x2, waiting for transfers between devices, swap_y(): return lax.ppermute(v, AXES, pairs)  4.26 us
    ppermute x2, starting transfers between devices, swap_y(): return lax.ppermute(v, AXES, pairs)  3.41 us
    unnamed x26, local copies, waits for them, and re-layouts  3.15 us
    ppermute x1, starting transfers between devices, per_device(): core = lax.ppermute(for_core, 'tm', [(i, i ^ 1) for i in range(16)])  2.94 us
  transfers between devices with their start and end apart: 13, of which 7 were waited for; matrix products, arithmetic and copies ran while one was open for 0% of the time, Pallas kernels for 19%

profile of v4, /device:TPU:32, one launch (start us, length us, event | category | flops | bytes accessed | tf_op | source)
XLA Modules:
  0.0 72.2 jit_solution(8750138188596900015)
XLA Ops:
  0.7 1.5 %shard_map.119 = (bf16[8,768]{1,0:T(8,128)(2,1)}, bf16[8,768]{1,0:T(8,128)(2,1)}) custom-call(s32[1]{0:T(128)} %bitcast.idx_ref, bf16[2048,256]{1,0:T(8,128)(2,1)} %bitcast.15, bf16[512,512]{1,0:T(8,128)(2,1)} %bitcast.17), custom_call_target="tpu_custom_call" | custom-call | bytes 50000 | tf_op jit(solution)/shard_map/pallas_call | solution.py:373
  3.0 2.9 %collective-permute-start.1 = (bf16[8,768]{1,0:T(8,128)(2,1)}, bf16[8,768]{1,0:T(8,128)(2,1)S(1)}, u32[]{:S(2)}, u32[]{:S(2)}) collective-permute-start(bf16[8,768]{1,0:T(8,128)(2,1)} %get-tuple-element.47), channel_id=1, source_target_pairs={{0,1},{1,0},{2,3},{3,2},{4,5},{5,4},{6,7},{7,6},{8,9},{9,8},{10,11... | collective-permute-start | bytes 36872 | tf_op jit(solution)/shard_map/ppermute | solution.py:446
  6.9 1.7 %shard_map.118 = (bf16[512,1024]{1,0:T(8,128)(2,1)S(1)}, bf16[512,1024]{1,0:T(8,128)(2,1)S(1)}, bf16[512,512]{1,0:T(8,128)(2,1)S(1)}, bf16[1024,512]{1,0:T(8,128)(2,1)S(1)}) custom-call(bf16[2048,256]{1,0:T(8,128)(2,1)S(1)} %bitcast.16, bf16[512,512]{1,0:T(8,128)(2,1)S(1)} %bitcast.18, bf16[1024,512]{1,0:T(8,128)(2,1)} %down_ref.1, f32[1,256]{1,0:T(1,128)S(1)} %fusion.temb_ref), custom_call_target="tpu_custom_call" | custom-call | flops 50000000 | bytes 6500000 | tf_op jit(solution)/shard_map/pallas_call | solution.py:373
  8.6 3.4 %shard_map.120 = (bf16[8,32,1536]{2,1,0:T(8,128)(2,1)S(1)}, bf16[8,32,1536]{2,1,0:T(8,128)(2,1)S(1)}, bf16[528,1024]{1,0:T(8,128)(2,1)S(1)}, bf16[528,1536]{1,0:...) custom-call(s32[1]{0:T(128)} %bitcast.idx_ref, ...), custom_call_target="tpu_custom_call" | custom-call | flops 2200000000 | bytes 10000000 | tf_op jit(solution)/shard_map/pallas_call | solution.py:373
  12.0 0.8 %copy-done.8 = bf16[528,512]{1,0:T(8,128)(2,1)} copy-done((bf16[528,512]{1,0:T(8,128)(2,1)}, bf16[528,512]{1,0:T(8,128)(2,1)S(1)}, u32[]{:S(2)}) %copy-start.8) | copy-done | bytes 540696
  12.9 2.8 %shard_map.122 = (bf16[528,512]{1,0:T(8,128)(2,1)S(1)}, bf16[528,1024]{1,0:T(8,128)(2,1)S(1)}, f32[512,1024]{1,0:T(8,128)S(1)}) custom-call(s32[1]{0:T(128)} %bitcast.idx_ref, bf16[528,512]{1,0:T(8,128)(2,1)S(1)} %get-tuple-element.50.co_ref, bf16[512,512]{1,0:T(8,128)(2,1)S(1)} %get-tuple-element.48.cot_ref, ...), custom_call_target="tpu_custom_call" | custom-call | flops 1400000000 | bytes 7000000 | tf_op jit(solution)/shard_map/pallas_call | solution.py:373
  15.7 3.8 %shard_map.123 = (bf16[16,48,512]{2,1,0:T(8,128)(2,1)S(1)}, bf16[16,48,512]{2,1,0:T(8,128)(2,1)S(1)}, f32[512,1024]{1,0:T(8,128)S(1)}) custom-call(s32[1]{0:T(128)} %bitcast.idx_ref, bf16[512,1024]{1,0:T(8,128)(2,1)S(1)} %get-tuple-element.44.xp_ref, bf16[528,512]{1,0:T(8,128)(2,1)S(1)} %get-tuple-element.53.dc_ref, ...), custom_call_target="tpu_custom_call" | custom-call | flops 2200000000 | bytes 11000000 | tf_op jit(solution)/shard_map/pallas_call | solution.py:373
  20.3 1.6 %collective-permute-start.3 = (bf16[4,32,1536]{2,1,0:T(8,128)(2,1)S(1)}, bf16[4,32,1536]{2,1,0:T(8,128)(2,1)S(1)}, u32[]{:S(2)}, u32[]{:S(2)}) collective-permute-start(bf16[4,32,1536]{2,1,0:T(8,128)(2,1)S(1)} %get-tuple-element.61), channel_id=1, source_target_pairs={{0,2},{1,3},{2,0},{3,1},{4,6},{5,7},{6,4},{7,5},{8,10},{9,11},{10,... | collective-permute-start | bytes 1179656 | tf_op jit(solution)/shard_map/ppermute | solution.py:396
  22.2 1.6 %collective-permute-start.7 = (bf16[4,48,512]{2,1,0:T(8,128)(2,1)S(1)}, bf16[4,48,512]{2,1,0:T(8,128)(2,1)S(1)}, u32[]{:S(2)}, u32[]{:S(2)}) collective-permute-start(bf16[4,48,512]{2,1,0:T(8,128)(2,1)S(1)} %get-tuple-element.69), channel_id=1, source_target_pairs={{0,2},{1,3},{2,0},{3,1},{4,6},{5,7},{6,4},{7,5},{8,10},{9,11},{10,... | collective-permute-start | bytes 589832 | tf_op jit(solution)/shard_map/ppermute | solution.py:396
  23.8 3.7 %collective-permute-start.9 = (bf16[4,48,512]{2,1,0:T(8,128)(2,1)S(1)}, bf16[4,48,512]{2,1,0:T(8,128)(2,1)S(1)}, u32[]{:S(2)}, u32[]{:S(2)}) collective-permute-start(bf16[4,48,512]{2,1,0:T(8,128)(2,1)S(1)} %get-tuple-element.73), channel_id=1, source_target_pairs={{0,6},{1,7},{2,4},{3,5},{4,2},{5,3},{6,0},{7,1},{8,14},{9,15},{10,... | collective-permute-start | bytes 589832 | tf_op jit(solution)/shard_map/ppermute | solution.py:396
  27.5 4.9 %collective-permute-done.3.refs_1_ = bf16[4,32,1536]{2,1,0:T(8,128)(2,1)S(1)} collective-permute-done((bf16[4,32,1536]{2,1,0:T(8,128)(2,1)S(1)}, bf16[4,32,1536]{2,1,0:T(8,128)(2,1)S(1)}, u32[]{:S(2)}, u32[]{:S(2)}) %collective-permute-start.3) | collective-permute-done | bytes 393248 | tf_op jit(solution)/shard_map/ppermute | solution.py:396
  32.5 5.0 %collective-permute-start.4 = (bf16[2,32,1536]{2,1,0:T(8,128)(2,1)S(1)}, bf16[2,32,1536]{2,1,0:T(8,128)(2,1)S(1)}, u32[]{:S(2)}, u32[]{:S(2)}) collective-permute-start(bf16[2,32,1536]{2,1,0:T(8,128)(2,1)S(1)} %get-tuple-element.63), channel_id=1, source_target_pairs={{0,6},{1,7},{2,4},{3,5},{4,2},{5,3},{6,0},{7,1},{8,14},{9,15},{10,... | collective-permute-start | bytes 589832 | tf_op jit(solution)/shard_map/ppermute | solution.py:396
  37.5 3.4 %collective-permute-start.8 = (bf16[2,48,512]{2,1,0:T(8,128)(2,1)S(1)}, bf16[2,48,512]{2,1,0:T(8,128)(2,1)S(1)}, u32[]{:S(2)}, u32[]{:S(2)}) collective-permute-start(bf16[2,48,512]{2,1,0:T(8,128)(2,1)S(1)} %get-tuple-element.71), channel_id=1, source_target_pairs={{0,6},{1,7},{2,4},{3,5},{4,2},{5,3},{6,0},{7,1},{8,14},{9,15},{10,... | collective-permute-start | bytes 294920 | tf_op jit(solution)/shard_map/ppermute | solution.py:396
  41.1 2.7 %collective-permute-done.8.got_u = bf16[2,48,512]{2,1,0:T(8,128)(2,1)S(1)} collective-permute-done((bf16[2,48,512]{2,1,0:T(8,128)(2,1)S(1)}, bf16[2,48,512]{2,1,0:T(8,128)(2,1)S(1)}, u32[]{:S(2)}, u32[]{:S(2)}) %collective-permute-start.8) | collective-permute-done | bytes 98336 | tf_op jit(solution)/shard_map/ppermute | solution.py:396
  43.8 1.9 %collective-permute-done.10.got_v = bf16[2,48,512]{2,1,0:T(8,128)(2,1)S(1)} collective-permute-done((bf16[2,48,512]{2,1,0:T(8,128)(2,1)S(1)}, bf16[2,48,512]{2,1,0:T(8,128)(2,1)S(1)}, u32[]{:S(2)}, u32[]{:S(2)}) %collective-permute-start.10) | collective-permute-done | bytes 98336 | tf_op jit(solution)/shard_map/ppermute | solution.py:396
  45.8 1.7 %collective-permute-start.11 = (bf16[48,1024]{1,0:T(8,128)(2,1)S(1)}, bf16[48,1024]{1,0:T(8,128)(2,1)S(1)}, u32[]{:S(2)}, u32[]{:S(2)}) collective-permute-start(bf16[48,1024]{1,0:T(8,128)(2,1)S(1)} %get-tuple-element.77), channel_id=1, source_target_pairs={{0,136},{1,137},{2,138},{3,139},{4,140},{5,141},{6,142},{7,143},{8... | collective-permute-start | bytes 294920 | tf_op jit(solution)/shard_map/ppermute | solution.py:409
  47.5 1.7 %collective-permute-start.5 = (bf16[1,32,1536]{2,1,0:T(8,128)(2,1)S(1)}, bf16[1,32,1536]{2,1,0:T(8,128)(2,1)S(1)}, u32[]{:S(2)}, u32[]{:S(2)}) collective-permute-start(bf16[1,32,1536]{2,1,0:T(8,128)(2,1)S(1)} %get-tuple-element.65), channel_id=1, source_target_pairs={{0,136},{1,137},{2,138},{3,139},{4,140},{5,141},{6,142},{7,143},{8... | collective-permute-start | bytes 294920 | tf_op jit(solution)/shard_map/ppermute | solution.py:409
  49.2 3.2 %collective-permute-done.11.b_got = bf16[48,1024]{1,0:T(8,128)(2,1)S(1)} collective-permute-done((bf16[48,1024]{1,0:T(8,128)(2,1)S(1)}, bf16[48,1024]{1,0:T(8,128)(2,1)S(1)}, u32[]{:S(2)}, u32[]{:S(2)}) %collective-permute-start.11) | collective-permute-done | bytes 98336 | tf_op jit(solution)/shard_map/ppermute | solution.py:409
  52.4 1.1 %collective-permute-done.5.a_got = bf16[1,32,1536]{2,1,0:T(8,128)(2,1)S(1)} collective-permute-done((bf16[1,32,1536]{2,1,0:T(8,128)(2,1)S(1)}, bf16[1,32,1536]{2,1,0:T(8,128)(2,1)S(1)}, u32[]{:S(2)}, u32[]{:S(2)}) %collective-permute-start.5) | collective-permute-done | bytes 98336 | tf_op jit(solution)/shard_map/ppermute | solution.py:409
  54.4 8.6 %all-to-all-start = ((bf16[16,48,128]{2,1,0:T(8,128)(2,1)}), bf16[16,48,128]{2,1,0:T(8,128)(2,1)S(1)}, u32[]{:S(2)}, u32[]{:S(2)}) async-start(bf16[16,48,128]{2,1,0:T(8,128)(2,1)} %copy-done.7), calls=%async_computation | async-start | bytes 393216 | tf_op jit(solution)/shard_map/all_to_all | solution.py:497
  63.0 1.6 %copy-done.3 = f32[512,1024]{1,0:T(8,128)S(1)} copy-done((f32[512,1024]{1,0:T(8,128)S(1)}, f32[512,1024]{1,0:T(8,128)}, u32[]{:S(2)}) %copy-start.3) | copy-done | bytes 2097176
  64.5 2.8 %shard_map.124 = bf16[2048,256]{1,0:T(8,128)(2,1)} custom-call(bf16[512,1024]{1,0:T(8,128)(2,1)S(1)} %get-tuple-element.44.xp_ref, f32[512,1024]{1,0:T(8,128)S(1)} %get-tuple-element.52.dm_ref, f32[512,1024]{1,0:T(8,128)S(1)} %copy-done.3), custom_call_target="tpu_custom_call" | custom-call | flops 20000000 | bytes 6000000 | tf_op jit(solution)/shard_map/pallas_call | solution.py:373
  67.4 1.8 %shard_map.121 = bf16[512,512]{1,0:T(8,128)(2,1)} custom-call(bf16[528,512]{1,0:T(8,128)(2,1)S(1)} %copy-done.11, bf16[528,512]{1,0:T(8,128)(2,1)S(1)} %copy-done.9, bf16[1536,512]{1,0:T(8,128)(2,1)S(1)} %copy-done.6), custom_call_target="tpu_custom_call" | custom-call | flops 800000000 | bytes 3000000 | tf_op jit(solution)/shard_map/pallas_call | solution.py:373
  69.2 2.3 %all-to-all-done.in_ref = bf16[16,48,128]{2,1,0:T(8,128)(2,1)S(1)} async-done(((bf16[16,48,128]{2,1,0:T(8,128)(2,1)}), bf16[16,48,128]{2,1,0:T(8,128)(2,1)S(1)}, u32[]{:S(2)}, u32[]{:S(2)}) %all-to-all-start) | async-done | bytes 196640 | tf_op jit(solution)/shard_map/all_to_all | solution.py:497
  (47 shorter events, 4.2 us)
Async XLA Ops:
  0.6 6.0 %copy-start = (bf16[256,256]{1,0:T(8,128)(2,1)S(1)}, bf16[256,256]{1,0:T(8,128)(2,1)}, u32[]{:S(2)}) copy-start(bf16[256,256]{1,0:T(8,128)(2,1)} %param.13) | copy-start | bytes 393220
  0.6 6.2 %copy-start.4 = (bf16[1,512,512]{2,1,0:T(8,128)(2,1)S(1)}, bf16[1,512,512]{2,1,0:T(8,128)(2,1)}, u32[]{:S(2)}) copy-start(bf16[1,512,512]{2,1,0:T(8,128)(2,1)} %param.9) | copy-start | bytes 1572868
  0.7 6.2 %copy-start.1 = (bf16[1,2048,256]{2,1,0:T(8,128)(2,1)S(1)}, bf16[1,2048,256]{2,1,0:T(8,128)(2,1)}, u32[]{:S(2)}) copy-start(bf16[1,2048,256]{2,1,0:T(8,128)(2,1)} %param.7) | copy-start | bytes 3145732
  2.2 6.4 %copy-start.12 = (bf16[768,256]{1,0:T(8,128)(2,1)S(1)}, bf16[768,256]{1,0:T(8,128)(2,1)}, u32[]{:S(2)}) copy-start(bf16[768,256]{1,0:T(8,128)(2,1)} %one_ref.3) | copy-start | bytes 1179652
  2.2 6.4 %collective-permute-start = (bf16[8,768]{1,0:T(8,128)(2,1)}, bf16[8,768]{1,0:T(8,128)(2,1)S(1)}, u32[]{:S(2)}, u32[]{:S(2)}) collective-permute-start(bf16[8,768]{1,0:T(8,128)(2,1)} %get-tuple-element.46), channel_id=1, source_target_pairs={{1,2},{2,1},{3,4},{4,3},{5,6},{6,5},{7,8},{8,7},{9,10},{10,9},{11,... | collective-permute-start | bytes 36872 | tf_op jit(solution)/shard_map/ppermute | solution.py:445
  3.0 5.6 %collective-permute-start.1 = (bf16[8,768]{1,0:T(8,128)(2,1)}, bf16[8,768]{1,0:T(8,128)(2,1)S(1)}, u32[]{:S(2)}, u32[]{:S(2)}) collective-permute-start(bf16[8,768]{1,0:T(8,128)(2,1)} %get-tuple-element.47), channel_id=1, source_target_pairs={{0,1},{1,0},{2,3},{3,2},{4,5},{5,4},{6,7},{7,6},{8,9},{9,8},{10,11... | collective-permute-start | bytes 36872 | tf_op jit(solution)/shard_map/ppermute | solution.py:446
  8.6 4.3 %copy-start.5 = (bf16[1536,512]{1,0:T(8,128)(2,1)S(1)}, bf16[1536,512]{1,0:T(8,128)(2,1)}, u32[]{:S(2)}) copy-start(bf16[1536,512]{1,0:T(8,128)(2,1)} %two_ref.3) | copy-start | bytes 4718596
  12.9 2.8 %copy-start.10 = (bf16[528,512]{1,0:T(8,128)(2,1)}, bf16[528,512]{1,0:T(8,128)(2,1)S(1)}, u32[]{:S(2)}) copy-start(bf16[528,512]{1,0:T(8,128)(2,1)S(1)} %get-tuple-element.50.co_ref) | copy-start | bytes 1622020
  12.9 7.3 %collective-permute-start.2 = (bf16[8,32,1536]{2,1,0:T(8,128)(2,1)S(1)}, bf16[8,32,1536]{2,1,0:T(8,128)(2,1)S(1)}, u32[]{:S(2)}, u32[]{:S(2)}) collective-permute-start(bf16[8,32,1536]{2,1,0:T(8,128)(2,1)S(1)} %get-tuple-element.59), channel_id=1, source_target_pairs={{0,1},{1,0},{2,3},{3,2},{4,5},{5,4},{6,7},{7,6},{8,9},{9,8},{10,11... | collective-permute-start | bytes 2359304 | tf_op jit(solution)/shard_map/ppermute | solution.py:396
  19.5 13.0 %copy-start.2 = (f32[512,1024]{1,0:T(8,128)}, f32[512,1024]{1,0:T(8,128)S(1)}, u32[]{:S(2)}) copy-start(f32[512,1024]{1,0:T(8,128)S(1)} %get-tuple-element.57.dp_ref) | copy-start | bytes 6291460
  19.5 2.5 %collective-permute-start.6 = (bf16[16,48,512]{2,1,0:T(8,128)(2,1)S(1)}, bf16[16,48,512]{2,1,0:T(8,128)(2,1)S(1)}, u32[]{:S(2)}, u32[]{:S(2)}) collective-permute-start(bf16[16,48,512]{2,1,0:T(8,128)(2,1)S(1)} %get-tuple-element.67), channel_id=1, source_target_pairs={{0,1},{1,0},{2,3},{3,2},{4,5},{5,4},{6,7},{7,6},{8,9},{9,8},{10,11... | collective-permute-start | bytes 2359304 | tf_op jit(solution)/shard_map/ppermute | solution.py:396
  20.3 12.1 %collective-permute-start.3 = (bf16[4,32,1536]{2,1,0:T(8,128)(2,1)S(1)}, bf16[4,32,1536]{2,1,0:T(8,128)(2,1)S(1)}, u32[]{:S(2)}, u32[]{:S(2)}) collective-permute-start(bf16[4,32,1536]{2,1,0:T(8,128)(2,1)S(1)} %get-tuple-element.61), channel_id=1, source_target_pairs={{0,2},{1,3},{2,0},{3,1},{4,6},{5,7},{6,4},{7,5},{8,10},{9,11},{10,... | collective-permute-start | bytes 1179656 | tf_op jit(solution)/shard_map/ppermute | solution.py:396
  22.2 15.2 %collective-permute-start.7 = (bf16[4,48,512]{2,1,0:T(8,128)(2,1)S(1)}, bf16[4,48,512]{2,1,0:T(8,128)(2,1)S(1)}, u32[]{:S(2)}, u32[]{:S(2)}) collective-permute-start(bf16[4,48,512]{2,1,0:T(8,128)(2,1)S(1)} %get-tuple-element.69), channel_id=1, source_target_pairs={{0,2},{1,3},{2,0},{3,1},{4,6},{5,7},{6,4},{7,5},{8,10},{9,11},{10,... | collective-permute-start | bytes 589832 | tf_op jit(solution)/shard_map/ppermute | solution.py:396
  23.8 17.2 %collective-permute-start.9 = (bf16[4,48,512]{2,1,0:T(8,128)(2,1)S(1)}, bf16[4,48,512]{2,1,0:T(8,128)(2,1)S(1)}, u32[]{:S(2)}, u32[]{:S(2)}) collective-permute-start(bf16[4,48,512]{2,1,0:T(8,128)(2,1)S(1)} %get-tuple-element.73), channel_id=1, source_target_pairs={{0,6},{1,7},{2,4},{3,5},{4,2},{5,3},{6,0},{7,1},{8,14},{9,15},{10,... | collective-permute-start | bytes 589832 | tf_op jit(solution)/shard_map/ppermute | solution.py:396
  32.5 15.0 %collective-permute-start.4 = (bf16[2,32,1536]{2,1,0:T(8,128)(2,1)S(1)}, bf16[2,32,1536]{2,1,0:T(8,128)(2,1)S(1)}, u32[]{:S(2)}, u32[]{:S(2)}) collective-permute-start(bf16[2,32,1536]{2,1,0:T(8,128)(2,1)S(1)} %get-tuple-element.63), channel_id=1, source_target_pairs={{0,6},{1,7},{2,4},{3,5},{4,2},{5,3},{6,0},{7,1},{8,14},{9,15},{10,... | collective-permute-start | bytes 589832 | tf_op jit(solution)/shard_map/ppermute | solution.py:396
  37.5 6.3 %collective-permute-start.8 = (bf16[2,48,512]{2,1,0:T(8,128)(2,1)S(1)}, bf16[2,48,512]{2,1,0:T(8,128)(2,1)S(1)}, u32[]{:S(2)}, u32[]{:S(2)}) collective-permute-start(bf16[2,48,512]{2,1,0:T(8,128)(2,1)S(1)} %get-tuple-element.71), channel_id=1, source_target_pairs={{0,6},{1,7},{2,4},{3,5},{4,2},{5,3},{6,0},{7,1},{8,14},{9,15},{10,... | collective-permute-start | bytes 294920 | tf_op jit(solution)/shard_map/ppermute | solution.py:396
  41.0 4.7 %collective-permute-start.10 = (bf16[2,48,512]{2,1,0:T(8,128)(2,1)S(1)}, bf16[2,48,512]{2,1,0:T(8,128)(2,1)S(1)}, u32[]{:S(2)}, u32[]{:S(2)}) collective-permute-start(bf16[2,48,512]{2,1,0:T(8,128)(2,1)S(1)} %get-tuple-element.75), channel_id=1, source_target_pairs={{0,2},{1,3},{2,0},{3,1},{4,6},{5,7},{6,4},{7,5},{8,10},{9,11},{10,... | collective-permute-start | bytes 294920 | tf_op jit(solution)/shard_map/ppermute | solution.py:396
  45.8 6.7 %collective-permute-start.11 = (bf16[48,1024]{1,0:T(8,128)(2,1)S(1)}, bf16[48,1024]{1,0:T(8,128)(2,1)S(1)}, u32[]{:S(2)}, u32[]{:S(2)}) collective-permute-start(bf16[48,1024]{1,0:T(8,128)(2,1)S(1)} %get-tuple-element.77), channel_id=1, source_target_pairs={{0,136},{1,137},{2,138},{3,139},{4,140},{5,141},{6,142},{7,143},{8... | collective-permute-start | bytes 294920 | tf_op jit(solution)/shard_map/ppermute | solution.py:409
  47.5 6.0 %collective-permute-start.5 = (bf16[1,32,1536]{2,1,0:T(8,128)(2,1)S(1)}, bf16[1,32,1536]{2,1,0:T(8,128)(2,1)S(1)}, u32[]{:S(2)}, u32[]{:S(2)}) collective-permute-start(bf16[1,32,1536]{2,1,0:T(8,128)(2,1)S(1)} %get-tuple-element.65), channel_id=1, source_target_pairs={{0,136},{1,137},{2,138},{3,139},{4,140},{5,141},{6,142},{7,143},{8... | collective-permute-start | bytes 294920 | tf_op jit(solution)/shard_map/ppermute | solution.py:409
  54.4 17.1 %all-to-all-start = ((bf16[16,48,128]{2,1,0:T(8,128)(2,1)}), bf16[16,48,128]{2,1,0:T(8,128)(2,1)S(1)}, u32[]{:S(2)}, u32[]{:S(2)}) async-start(bf16[16,48,128]{2,1,0:T(8,128)(2,1)} %copy-done.7), calls=%async_computation | async-start | bytes 393216 | tf_op jit(solution)/shard_map/all_to_all | solution.py:497
  62.9 1.6 %copy-start.3 = (f32[512,1024]{1,0:T(8,128)S(1)}, f32[512,1024]{1,0:T(8,128)}, u32[]{:S(2)}) copy-start(f32[512,1024]{1,0:T(8,128)} %copy-done.2) | copy-start | bytes 6291460
  64.5 2.8 %copy-start.6 = (bf16[1536,512]{1,0:T(8,128)(2,1)S(1)}, bf16[1536,512]{1,0:T(8,128)(2,1)}, u32[]{:S(2)}) copy-start(bf16[1536,512]{1,0:T(8,128)(2,1)} %two_ref.3) | copy-start | bytes 4718596
  64.5 2.8 %copy-start.9 = (bf16[528,512]{1,0:T(8,128)(2,1)S(1)}, bf16[528,512]{1,0:T(8,128)(2,1)}, u32[]{:S(2)}) copy-start(bf16[528,512]{1,0:T(8,128)(2,1)} %copy-done.8) | copy-start | bytes 1622020
  64.5 2.8 %copy-start.11 = (bf16[528,512]{1,0:T(8,128)(2,1)S(1)}, bf16[528,512]{1,0:T(8,128)(2,1)}, u32[]{:S(2)}) copy-start(bf16[528,512]{1,0:T(8,128)(2,1)} %copy-done.10) | copy-start | bytes 1622020
  (2 other events, 1.5 us)

commit v5 on v4

--- a/solution.py
+++ b/solution.py
@@ -344,7 +344,7 @@
 
 
 def lines_kernel(a_ref, a_got, b_ref, b_got, out_ref):
-    two = a_ref[0].astype(F32) + a_got[0].astype(F32)
+    two = a_ref[...].astype(F32) + a_got[...].astype(F32)
     rest = b_ref[...].astype(F32) + b_got[...].astype(F32)
     for d in range(16):
         down = rest[:32, 64 * d : 64 * d + 64]
@@ -456,7 +456,7 @@
     a_keep, a_send, mw, uw, ab, co = call(
         forward_kernel,
         [idx, xp, act, chip, core, cot, temb, conv_one, down_proj],
-        [((8, 32, 3 * CB), BF16)] * 2
+        [((16, 32, 3 * CB // 2), BF16)] * 2
         + [((E, 4 * CA), BF16), ((E, 6 * CA), BF16), ((E, CB), BF16), ((E, CB), BF16)],
         [((2, 64, 128), F32), ((E, 3 * CB), BF16), ((CB, S), BF16)],
         2_200_000_000, 10_000_000, smem=True,
@@ -467,8 +467,8 @@
         [((E, CB), BF16), ((E, 4 * CA), BF16), ((S, 4 * CA), F32)],
         [((E, 3 * CB), BF16), ((E, CB), F32)], 1_400_000_000, 7_000_000, smem=True,
     )
-    a_own, a_send = added([a_keep, a_got], (4, 4))
-    a_got = swap_x(a_send, 1)
+    a_parts = added([a_keep, a_got], (4, 4, 4, 4))
+    a_own, a_got = ring(a_parts)
     b_keep, b_send, d_pre = call(
         fine_kernel, [idx, xp, dc, dh, mw, uw, temb, emb, conv_one],
         [((16, 48, 2 * CA), BF16)] * 2 + [((S, 4 * CA), F32)],
@@ -485,10 +485,6 @@
         [((2, 4 * S, 128), F32)], 20_000_000, 6_000_000,
     )
     b_parts = added([b_keep, b_got], (4, 4, 4, 4))
-    a_own, a_send = added([a_own, a_got], (2, 2))
-    a_got = swap_x(a_send, 3)
-    a_own, a_send = added([a_own, a_got], (1, 1))
-    a_got = swap_y(a_send)
     b_own, b_got = ring(b_parts)
     (lines,) = call(
         lines_kernel, [a_own, a_got, b_own, b_got],

time: 72.5 us -> 67 us (0.924)
  waiting for transfers between devices: 16.3 us -> 7.55 us
  starting transfers between devices: 31.6 us -> 34.8 us
    ppermute x8 -> x10, waiting for transfers between devices: 9.69 us -> 1.48 us  [moved(): return lax.ppermute(value, 'tm', pairs)]
    ppermute x2, starting transfers between devices: 3.41 us -> 5.24 us  [swap_y(): return lax.ppermute(v, AXES, pairs)]
    ppermute x8 -> x10, starting transfers between devices: 15.9 us -> 17.2 us  [moved(): return lax.ppermute(value, 'tm', pairs)]
    pallas_call x16 -> x17, Pallas kernels: 19.5 us -> 19.5 us  [call(): pl.pallas_call(kernel, in_specs=[pl.BlockSpec(memory_space=pltpu.SMEM)] *...]
  transfers between devices with their start and end apart: 13 -> 15, of which waited for: 7 -> 4; matrix products, arithmetic and copies ran while one was open for 0% -> 0% of each run, Pallas kernels for 19% -> 20%
where the time goes in v5:
time: 67 us; the launch traced here: 66.7 us
  starting transfers between devices  34.8 us (52%)
  Pallas kernels  19.5 us (29%)
  waiting for transfers between devices  7.55 us (11%)
  local copies, waits for them, and re-layouts  3.17 us (5%)
  between operations  1.56 us (2%)
    pallas_call x17, Pallas kernels, call(): pl.pallas_call(kernel, in_specs=[pl.BlockSpec(memory_space=pltpu.SMEM)] *...  19.5 us
    ppermute x10, starting transfers between devices, moved(): return lax.ppermute(value, 'tm', pairs)  17.2 us
    all_to_all x1, starting transfers between devices, per_device(): lines = lax.all_to_all(lines, 'dp', 0, 0, tiled=True)  8.59 us
    ppermute x2, starting transfers between devices, swap_y(): return lax.ppermute(v, AXES, pairs)  5.24 us
    ppermute x2, waiting for transfers between devices, swap_y(): return lax.ppermute(v, AXES, pairs)  3.75 us
    unnamed x26, local copies, waits for them, and re-layouts  3.17 us
    ppermute x1, starting transfers between devices, per_device(): core = lax.ppermute(for_core, 'tm', [(i, i ^ 1) for i in range(16)])  2.94 us
    all_to_all x1, waiting for transfers between devices, per_device(): lines = lax.all_to_all(lines, 'dp', 0, 0, tiled=True)  2.32 us
  transfers between devices with their start and end apart: 15, of which 4 were waited for; matrix products, arithmetic and copies ran while one was open for 0% of the time, Pallas kernels for 20%

profile of v5, /device:TPU:32, one launch (start us, length us, event | category | flops | bytes accessed | tf_op | source)
XLA Modules:
  0.0 66.7 jit_solution(6873623228603382926)
XLA Ops:
  0.7 1.5 %shard_map.119 = (bf16[8,768]{1,0:T(8,128)(2,1)}, bf16[8,768]{1,0:T(8,128)(2,1)}) custom-call(s32[1]{0:T(128)} %bitcast.idx_ref, bf16[2048,256]{1,0:T(8,128)(2,1)} %bitcast.15, bf16[512,512]{1,0:T(8,128)(2,1)} %bitcast.17), custom_call_target="tpu_custom_call" | custom-call | bytes 50000 | tf_op jit(solution)/shard_map/pallas_call | solution.py:373
  2.2 0.8 %collective-permute-start = (bf16[8,768]{1,0:T(8,128)(2,1)}, bf16[8,768]{1,0:T(8,128)(2,1)S(1)}, u32[]{:S(2)}, u32[]{:S(2)}) collective-permute-start(bf16[8,768]{1,0:T(8,128)(2,1)} %get-tuple-element.50), channel_id=1, source_target_pairs={{1,2},{2,1},{3,4},{4,3},{5,6},{6,5},{7,8},{8,7},{9,10},{10,9},{11,... | collective-permute-start | bytes 36872 | tf_op jit(solution)/shard_map/ppermute | solution.py:445
  3.0 2.9 %collective-permute-start.1 = (bf16[8,768]{1,0:T(8,128)(2,1)}, bf16[8,768]{1,0:T(8,128)(2,1)S(1)}, u32[]{:S(2)}, u32[]{:S(2)}) collective-permute-start(bf16[8,768]{1,0:T(8,128)(2,1)} %get-tuple-element.51), channel_id=1, source_target_pairs={{0,1},{1,0},{2,3},{3,2},{4,5},{5,4},{6,7},{7,6},{8,9},{9,8},{10,11... | collective-permute-start | bytes 36872 | tf_op jit(solution)/shard_map/ppermute | solution.py:446
  6.9 1.7 %shard_map.118 = (bf16[512,1024]{1,0:T(8,128)(2,1)S(1)}, bf16[512,1024]{1,0:T(8,128)(2,1)S(1)}, bf16[512,512]{1,0:T(8,128)(2,1)S(1)}, bf16[1024,512]{1,0:T(8,128)(2,1)S(1)}) custom-call(bf16[2048,256]{1,0:T(8,128)(2,1)S(1)} %bitcast.16, bf16[512,512]{1,0:T(8,128)(2,1)S(1)} %bitcast.18, bf16[1024,512]{1,0:T(8,128)(2,1)} %down_ref.1, f32[1,256]{1,0:T(1,128)S(1)} %fusion.temb_ref), custom_call_target="tpu_custom_call" | custom-call | flops 50000000 | bytes 6500000 | tf_op jit(solution)/shard_map/pallas_call | solution.py:373
  8.6 3.4 %shard_map.120 = (bf16[16,32,768]{2,1,0:T(8,128)(2,1)S(1)}, bf16[16,32,768]{2,1,0:T(8,128)(2,1)S(1)}, bf16[528,1024]{1,0:T(8,128)(2,1)S(1)}, bf16[528,1536]{1,0:...) custom-call(s32[1]{0:T(128)} %bitcast.idx_ref, ...), custom_call_target="tpu_custom_call" | custom-call | flops 2200000000 | bytes 10000000 | tf_op jit(solution)/shard_map/pallas_call | solution.py:373
  12.1 0.8 %copy-done.8 = bf16[528,512]{1,0:T(8,128)(2,1)} copy-done((bf16[528,512]{1,0:T(8,128)(2,1)}, bf16[528,512]{1,0:T(8,128)(2,1)S(1)}, u32[]{:S(2)}) %copy-start.8) | copy-done | bytes 540696
  12.9 2.8 %shard_map.122 = (bf16[528,512]{1,0:T(8,128)(2,1)S(1)}, bf16[528,1024]{1,0:T(8,128)(2,1)S(1)}, f32[512,1024]{1,0:T(8,128)S(1)}) custom-call(s32[1]{0:T(128)} %bitcast.idx_ref, bf16[528,512]{1,0:T(8,128)(2,1)S(1)} %get-tuple-element.54.co_ref, bf16[512,512]{1,0:T(8,128)(2,1)S(1)} %get-tuple-element.52.cot_ref, ...), custom_call_target="tpu_custom_call" | custom-call | flops 1400000000 | bytes 7000000 | tf_op jit(solution)/shard_map/pallas_call | solution.py:373
  15.7 3.9 %shard_map.123 = (bf16[16,48,512]{2,1,0:T(8,128)(2,1)S(1)}, bf16[16,48,512]{2,1,0:T(8,128)(2,1)S(1)}, f32[512,1024]{1,0:T(8,128)S(1)}) custom-call(s32[1]{0:T(128)} %bitcast.idx_ref, bf16[512,1024]{1,0:T(8,128)(2,1)S(1)} %get-tuple-element.48.xp_ref, bf16[528,512]{1,0:T(8,128)(2,1)S(1)} %get-tuple-element.57.dc_ref, ...), custom_call_target="tpu_custom_call" | custom-call | flops 2200000000 | bytes 11000000 | tf_op jit(solution)/shard_map/pallas_call | solution.py:373
  20.3 1.6 %collective-permute-start.3 = (bf16[4,32,768]{2,1,0:T(8,128)(2,1)S(1)}, bf16[4,32,768]{2,1,0:T(8,128)(2,1)S(1)}, u32[]{:S(2)}, u32[]{:S(2)}) collective-permute-start(bf16[4,32,768]{2,1,0:T(8,128)(2,1)S(1)} %get-tuple-element.65), channel_id=1, source_target_pairs={{0,2},{1,3},{2,0},{3,1},{4,6},{5,7},{6,4},{7,5},{8,10},{9,11},{10,... | collective-permute-start | bytes 589832 | tf_op jit(solution)/shard_map/ppermute | solution.py:396
  21.9 3.3 %collective-permute-start.5 = (bf16[4,32,768]{2,1,0:T(8,128)(2,1)S(1)}, bf16[4,32,768]{2,1,0:T(8,128)(2,1)S(1)}, u32[]{:S(2)}, u32[]{:S(2)}) collective-permute-start(bf16[4,32,768]{2,1,0:T(8,128)(2,1)S(1)} %get-tuple-element.69), channel_id=1, source_target_pairs={{0,6},{1,7},{2,4},{3,5},{4,2},{5,3},{6,0},{7,1},{8,14},{9,15},{10,... | collective-permute-start | bytes 589832 | tf_op jit(solution)/shard_map/ppermute | solution.py:396
  25.4 1.4 %collective-permute-start.9 = (bf16[4,48,512]{2,1,0:T(8,128)(2,1)S(1)}, bf16[4,48,512]{2,1,0:T(8,128)(2,1)S(1)}, u32[]{:S(2)}, u32[]{:S(2)}) collective-permute-start(bf16[4,48,512]{2,1,0:T(8,128)(2,1)S(1)} %get-tuple-element.77), channel_id=1, source_target_pairs={{0,2},{1,3},{2,0},{3,1},{4,6},{5,7},{6,4},{7,5},{8,10},{9,11},{10,... | collective-permute-start | bytes 589832 | tf_op jit(solution)/shard_map/ppermute | solution.py:396
  26.8 0.8 %collective-permute-start.11 = (bf16[4,48,512]{2,1,0:T(8,128)(2,1)S(1)}, bf16[4,48,512]{2,1,0:T(8,128)(2,1)S(1)}, u32[]{:S(2)}, u32[]{:S(2)}) collective-permute-start(bf16[4,48,512]{2,1,0:T(8,128)(2,1)S(1)} %get-tuple-element.81), channel_id=1, source_target_pairs={{0,6},{1,7},{2,4},{3,5},{4,2},{5,3},{6,0},{7,1},{8,14},{9,15},{10,... | collective-permute-start | bytes 589832 | tf_op jit(solution)/shard_map/ppermute | solution.py:396
  27.7 5.3 %collective-permute-start.4 = (bf16[2,32,768]{2,1,0:T(8,128)(2,1)S(1)}, bf16[2,32,768]{2,1,0:T(8,128)(2,1)S(1)}, u32[]{:S(2)}, u32[]{:S(2)}) collective-permute-start(bf16[2,32,768]{2,1,0:T(8,128)(2,1)S(1)} %get-tuple-element.67), channel_id=1, source_target_pairs={{0,6},{1,7},{2,4},{3,5},{4,2},{5,3},{6,0},{7,1},{8,14},{9,15},{10,... | collective-permute-start | bytes 294920 | tf_op jit(solution)/shard_map/ppermute | solution.py:396
  33.2 4.0 %collective-permute-start.10 = (bf16[2,48,512]{2,1,0:T(8,128)(2,1)S(1)}, bf16[2,48,512]{2,1,0:T(8,128)(2,1)S(1)}, u32[]{:S(2)}, u32[]{:S(2)}) collective-permute-start(bf16[2,48,512]{2,1,0:T(8,128)(2,1)S(1)} %get-tuple-element.79), channel_id=1, source_target_pairs={{0,6},{1,7},{2,4},{3,5},{4,2},{5,3},{6,0},{7,1},{8,14},{9,15},{10,... | collective-permute-start | bytes 294920 | tf_op jit(solution)/shard_map/ppermute | solution.py:396
  37.8 3.1 %collective-permute-start.7 = (bf16[32,1536]{1,0:T(8,128)(2,1)S(1)}, bf16[32,1536]{1,0:T(8,128)(2,1)S(1)}, u32[]{:S(2)}, u32[]{:S(2)}) collective-permute-start(bf16[32,1536]{1,0:T(8,128)(2,1)S(1)} %get-tuple-element.73), channel_id=1, source_target_pairs={{0,136},{1,137},{2,138},{3,139},{4,140},{5,141},{6,142},{7,143},{8... | collective-permute-start | bytes 294920 | tf_op jit(solution)/shard_map/ppermute | solution.py:409
  40.9 1.1 %collective-permute-done.12.got_v = bf16[2,48,512]{2,1,0:T(8,128)(2,1)S(1)} collective-permute-done((bf16[2,48,512]{2,1,0:T(8,128)(2,1)S(1)}, bf16[2,48,512]{2,1,0:T(8,128)(2,1)S(1)}, u32[]{:S(2)}, u32[]{:S(2)}) %collective-permute-start.12) | collective-permute-done | bytes 98336 | tf_op jit(solution)/shard_map/ppermute | solution.py:396
  42.0 2.2 %collective-permute-start.13 = (bf16[48,1024]{1,0:T(8,128)(2,1)S(1)}, bf16[48,1024]{1,0:T(8,128)(2,1)S(1)}, u32[]{:S(2)}, u32[]{:S(2)}) collective-permute-start(bf16[48,1024]{1,0:T(8,128)(2,1)S(1)} %get-tuple-element.85), channel_id=1, source_target_pairs={{0,136},{1,137},{2,138},{3,139},{4,140},{5,141},{6,142},{7,143},{8... | collective-permute-start | bytes 294920 | tf_op jit(solution)/shard_map/ppermute | solution.py:409
  44.2 3.8 %collective-permute-done.13.b_got = bf16[48,1024]{1,0:T(8,128)(2,1)S(1)} collective-permute-done((bf16[48,1024]{1,0:T(8,128)(2,1)S(1)}, bf16[48,1024]{1,0:T(8,128)(2,1)S(1)}, u32[]{:S(2)}, u32[]{:S(2)}) %collective-permute-start.13) | collective-permute-done | bytes 98336 | tf_op jit(solution)/shard_map/ppermute | solution.py:409
  48.8 8.6 %all-to-all-start = ((bf16[16,48,128]{2,1,0:T(8,128)(2,1)}), bf16[16,48,128]{2,1,0:T(8,128)(2,1)S(1)}, u32[]{:S(2)}, u32[]{:S(2)}) async-start(bf16[16,48,128]{2,1,0:T(8,128)(2,1)} %copy-done.7), calls=%async_computation | async-start | bytes 393216 | tf_op jit(solution)/shard_map/all_to_all | solution.py:493
  57.4 1.6 %copy-done.3 = f32[512,1024]{1,0:T(8,128)S(1)} copy-done((f32[512,1024]{1,0:T(8,128)S(1)}, f32[512,1024]{1,0:T(8,128)}, u32[]{:S(2)}) %copy-start.3) | copy-done | bytes 2097176
  59.0 2.8 %shard_map.124 = bf16[2048,256]{1,0:T(8,128)(2,1)} custom-call(bf16[512,1024]{1,0:T(8,128)(2,1)S(1)} %get-tuple-element.48.xp_ref, f32[512,1024]{1,0:T(8,128)S(1)} %get-tuple-element.56.dm_ref, f32[512,1024]{1,0:T(8,128)S(1)} %copy-done.3), custom_call_target="tpu_custom_call" | custom-call | flops 20000000 | bytes 6000000 | tf_op jit(solution)/shard_map/pallas_call | solution.py:373
  61.9 1.8 %shard_map.121 = bf16[512,512]{1,0:T(8,128)(2,1)} custom-call(bf16[528,512]{1,0:T(8,128)(2,1)S(1)} %copy-done.11, bf16[528,512]{1,0:T(8,128)(2,1)S(1)} %copy-done.9, bf16[1536,512]{1,0:T(8,128)(2,1)S(1)} %copy-done.6), custom_call_target="tpu_custom_call" | custom-call | flops 800000000 | bytes 3000000 | tf_op jit(solution)/shard_map/pallas_call | solution.py:373
  63.6 2.3 %all-to-all-done.in_ref = bf16[16,48,128]{2,1,0:T(8,128)(2,1)S(1)} async-done(((bf16[16,48,128]{2,1,0:T(8,128)(2,1)}), bf16[16,48,128]{2,1,0:T(8,128)(2,1)S(1)}, u32[]{:S(2)}, u32[]{:S(2)}) %all-to-all-start) | async-done | bytes 196640 | tf_op jit(solution)/shard_map/all_to_all | solution.py:493
  65.9 0.8 %shard_map.134 = (f32[16,48]{1,0:T(8,128)}, f32[32,64]{1,0:T(8,128)}, f32[32,96]{1,0:T(8,128)}, f32[16,16]{1,0:T(8,128)}) custom-call(bf16[16,48,128]{2,1,0:T(8,128)(2,1)S(1)} %all-to-all-done.in_ref), custom_call_target="tpu_custom_call" | custom-call | bytes 300000 | tf_op jit(solution)/shard_map/pallas_call | solution.py:373
  (52 shorter events, 3.0 us)
Async XLA Ops:
  0.6 6.0 %copy-start = (bf16[256,256]{1,0:T(8,128)(2,1)S(1)}, bf16[256,256]{1,0:T(8,128)(2,1)}, u32[]{:S(2)}) copy-start(bf16[256,256]{1,0:T(8,128)(2,1)} %param.13) | copy-start | bytes 393220
  0.6 6.2 %copy-start.4 = (bf16[1,512,512]{2,1,0:T(8,128)(2,1)S(1)}, bf16[1,512,512]{2,1,0:T(8,128)(2,1)}, u32[]{:S(2)}) copy-start(bf16[1,512,512]{2,1,0:T(8,128)(2,1)} %param.9) | copy-start | bytes 1572868
  0.7 6.2 %copy-start.1 = (bf16[1,2048,256]{2,1,0:T(8,128)(2,1)S(1)}, bf16[1,2048,256]{2,1,0:T(8,128)(2,1)}, u32[]{:S(2)}) copy-start(bf16[1,2048,256]{2,1,0:T(8,128)(2,1)} %param.7) | copy-start | bytes 3145732
  2.2 6.4 %copy-start.12 = (bf16[768,256]{1,0:T(8,128)(2,1)S(1)}, bf16[768,256]{1,0:T(8,128)(2,1)}, u32[]{:S(2)}) copy-start(bf16[768,256]{1,0:T(8,128)(2,1)} %one_ref.3) | copy-start | bytes 1179652
  2.2 6.4 %collective-permute-start = (bf16[8,768]{1,0:T(8,128)(2,1)}, bf16[8,768]{1,0:T(8,128)(2,1)S(1)}, u32[]{:S(2)}, u32[]{:S(2)}) collective-permute-start(bf16[8,768]{1,0:T(8,128)(2,1)} %get-tuple-element.50), channel_id=1, source_target_pairs={{1,2},{2,1},{3,4},{4,3},{5,6},{6,5},{7,8},{8,7},{9,10},{10,9},{11,... | collective-permute-start | bytes 36872 | tf_op jit(solution)/shard_map/ppermute | solution.py:445
  3.0 5.6 %collective-permute-start.1 = (bf16[8,768]{1,0:T(8,128)(2,1)}, bf16[8,768]{1,0:T(8,128)(2,1)S(1)}, u32[]{:S(2)}, u32[]{:S(2)}) collective-permute-start(bf16[8,768]{1,0:T(8,128)(2,1)} %get-tuple-element.51), channel_id=1, source_target_pairs={{0,1},{1,0},{2,3},{3,2},{4,5},{5,4},{6,7},{7,6},{8,9},{9,8},{10,11... | collective-permute-start | bytes 36872 | tf_op jit(solution)/shard_map/ppermute | solution.py:446
  8.6 4.3 %copy-start.5 = (bf16[1536,512]{1,0:T(8,128)(2,1)S(1)}, bf16[1536,512]{1,0:T(8,128)(2,1)}, u32[]{:S(2)}) copy-start(bf16[1536,512]{1,0:T(8,128)(2,1)} %two_ref.3) | copy-start | bytes 4718596
  12.9 7.3 %collective-permute-start.2 = (bf16[16,32,768]{2,1,0:T(8,128)(2,1)S(1)}, bf16[16,32,768]{2,1,0:T(8,128)(2,1)S(1)}, u32[]{:S(2)}, u32[]{:S(2)}) collective-permute-start(bf16[16,32,768]{2,1,0:T(8,128)(2,1)S(1)} %get-tuple-element.63), channel_id=1, source_target_pairs={{0,1},{1,0},{2,3},{3,2},{4,5},{5,4},{6,7},{7,6},{8,9},{9,8},{10,11... | collective-permute-start | bytes 2359304 | tf_op jit(solution)/shard_map/ppermute | solution.py:396
  19.5 8.2 %copy-start.2 = (f32[512,1024]{1,0:T(8,128)}, f32[512,1024]{1,0:T(8,128)S(1)}, u32[]{:S(2)}) copy-start(f32[512,1024]{1,0:T(8,128)S(1)} %get-tuple-element.61.dp_ref) | copy-start | bytes 6291460
  19.5 5.7 %collective-permute-start.8 = (bf16[16,48,512]{2,1,0:T(8,128)(2,1)S(1)}, bf16[16,48,512]{2,1,0:T(8,128)(2,1)S(1)}, u32[]{:S(2)}, u32[]{:S(2)}) collective-permute-start(bf16[16,48,512]{2,1,0:T(8,128)(2,1)S(1)} %get-tuple-element.75), channel_id=1, source_target_pairs={{0,1},{1,0},{2,3},{3,2},{4,5},{5,4},{6,7},{7,6},{8,9},{9,8},{10,11... | collective-permute-start | bytes 2359304 | tf_op jit(solution)/shard_map/ppermute | solution.py:396
  20.3 7.3 %collective-permute-start.3 = (bf16[4,32,768]{2,1,0:T(8,128)(2,1)S(1)}, bf16[4,32,768]{2,1,0:T(8,128)(2,1)S(1)}, u32[]{:S(2)}, u32[]{:S(2)}) collective-permute-start(bf16[4,32,768]{2,1,0:T(8,128)(2,1)S(1)} %get-tuple-element.65), channel_id=1, source_target_pairs={{0,2},{1,3},{2,0},{3,1},{4,6},{5,7},{6,4},{7,5},{8,10},{9,11},{10,... | collective-permute-start | bytes 589832 | tf_op jit(solution)/shard_map/ppermute | solution.py:396
  21.9 11.1 %collective-permute-start.5 = (bf16[4,32,768]{2,1,0:T(8,128)(2,1)S(1)}, bf16[4,32,768]{2,1,0:T(8,128)(2,1)S(1)}, u32[]{:S(2)}, u32[]{:S(2)}) collective-permute-start(bf16[4,32,768]{2,1,0:T(8,128)(2,1)S(1)} %get-tuple-element.69), channel_id=1, source_target_pairs={{0,6},{1,7},{2,4},{3,5},{4,2},{5,3},{6,0},{7,1},{8,14},{9,15},{10,... | collective-permute-start | bytes 589832 | tf_op jit(solution)/shard_map/ppermute | solution.py:396
  25.4 7.8 %collective-permute-start.9 = (bf16[4,48,512]{2,1,0:T(8,128)(2,1)S(1)}, bf16[4,48,512]{2,1,0:T(8,128)(2,1)S(1)}, u32[]{:S(2)}, u32[]{:S(2)}) collective-permute-start(bf16[4,48,512]{2,1,0:T(8,128)(2,1)S(1)} %get-tuple-element.77), channel_id=1, source_target_pairs={{0,2},{1,3},{2,0},{3,1},{4,6},{5,7},{6,4},{7,5},{8,10},{9,11},{10,... | collective-permute-start | bytes 589832 | tf_op jit(solution)/shard_map/ppermute | solution.py:396
  26.8 10.4 %collective-permute-start.11 = (bf16[4,48,512]{2,1,0:T(8,128)(2,1)S(1)}, bf16[4,48,512]{2,1,0:T(8,128)(2,1)S(1)}, u32[]{:S(2)}, u32[]{:S(2)}) collective-permute-start(bf16[4,48,512]{2,1,0:T(8,128)(2,1)S(1)} %get-tuple-element.81), channel_id=1, source_target_pairs={{0,6},{1,7},{2,4},{3,5},{4,2},{5,3},{6,0},{7,1},{8,14},{9,15},{10,... | collective-permute-start | bytes 589832 | tf_op jit(solution)/shard_map/ppermute | solution.py:396
  27.7 9.7 %collective-permute-start.4 = (bf16[2,32,768]{2,1,0:T(8,128)(2,1)S(1)}, bf16[2,32,768]{2,1,0:T(8,128)(2,1)S(1)}, u32[]{:S(2)}, u32[]{:S(2)}) collective-permute-start(bf16[2,32,768]{2,1,0:T(8,128)(2,1)S(1)} %get-tuple-element.67), channel_id=1, source_target_pairs={{0,6},{1,7},{2,4},{3,5},{4,2},{5,3},{6,0},{7,1},{8,14},{9,15},{10,... | collective-permute-start | bytes 294920 | tf_op jit(solution)/shard_map/ppermute | solution.py:396
  33.1 4.7 %collective-permute-start.6 = (bf16[2,32,768]{2,1,0:T(8,128)(2,1)S(1)}, bf16[2,32,768]{2,1,0:T(8,128)(2,1)S(1)}, u32[]{:S(2)}, u32[]{:S(2)}) collective-permute-start(bf16[2,32,768]{2,1,0:T(8,128)(2,1)S(1)} %get-tuple-element.71), channel_id=1, source_target_pairs={{0,2},{1,3},{2,0},{3,1},{4,6},{5,7},{6,4},{7,5},{8,10},{9,11},{10,... | collective-permute-start | bytes 294920 | tf_op jit(solution)/shard_map/ppermute | solution.py:396
  33.2 7.7 %collective-permute-start.10 = (bf16[2,48,512]{2,1,0:T(8,128)(2,1)S(1)}, bf16[2,48,512]{2,1,0:T(8,128)(2,1)S(1)}, u32[]{:S(2)}, u32[]{:S(2)}) collective-permute-start(bf16[2,48,512]{2,1,0:T(8,128)(2,1)S(1)} %get-tuple-element.79), channel_id=1, source_target_pairs={{0,6},{1,7},{2,4},{3,5},{4,2},{5,3},{6,0},{7,1},{8,14},{9,15},{10,... | collective-permute-start | bytes 294920 | tf_op jit(solution)/shard_map/ppermute | solution.py:396
  37.3 4.7 %collective-permute-start.12 = (bf16[2,48,512]{2,1,0:T(8,128)(2,1)S(1)}, bf16[2,48,512]{2,1,0:T(8,128)(2,1)S(1)}, u32[]{:S(2)}, u32[]{:S(2)}) collective-permute-start(bf16[2,48,512]{2,1,0:T(8,128)(2,1)S(1)} %get-tuple-element.83), channel_id=1, source_target_pairs={{0,2},{1,3},{2,0},{3,1},{4,6},{5,7},{6,4},{7,5},{8,10},{9,11},{10,... | collective-permute-start | bytes 294920 | tf_op jit(solution)/shard_map/ppermute | solution.py:396
  37.8 6.4 %collective-permute-start.7 = (bf16[32,1536]{1,0:T(8,128)(2,1)S(1)}, bf16[32,1536]{1,0:T(8,128)(2,1)S(1)}, u32[]{:S(2)}, u32[]{:S(2)}) collective-permute-start(bf16[32,1536]{1,0:T(8,128)(2,1)S(1)} %get-tuple-element.73), channel_id=1, source_target_pairs={{0,136},{1,137},{2,138},{3,139},{4,140},{5,141},{6,142},{7,143},{8... | collective-permute-start | bytes 294920 | tf_op jit(solution)/shard_map/ppermute | solution.py:409
  42.0 5.9 %collective-permute-start.13 = (bf16[48,1024]{1,0:T(8,128)(2,1)S(1)}, bf16[48,1024]{1,0:T(8,128)(2,1)S(1)}, u32[]{:S(2)}, u32[]{:S(2)}) collective-permute-start(bf16[48,1024]{1,0:T(8,128)(2,1)S(1)} %get-tuple-element.85), channel_id=1, source_target_pairs={{0,136},{1,137},{2,138},{3,139},{4,140},{5,141},{6,142},{7,143},{8... | collective-permute-start | bytes 294920 | tf_op jit(solution)/shard_map/ppermute | solution.py:409
  48.8 17.1 %all-to-all-start = ((bf16[16,48,128]{2,1,0:T(8,128)(2,1)}), bf16[16,48,128]{2,1,0:T(8,128)(2,1)S(1)}, u32[]{:S(2)}, u32[]{:S(2)}) async-start(bf16[16,48,128]{2,1,0:T(8,128)(2,1)} %copy-done.7), calls=%async_computation | async-start | bytes 393216 | tf_op jit(solution)/shard_map/all_to_all | solution.py:493
  59.0 2.8 %copy-start.6 = (bf16[1536,512]{1,0:T(8,128)(2,1)S(1)}, bf16[1536,512]{1,0:T(8,128)(2,1)}, u32[]{:S(2)}) copy-start(bf16[1536,512]{1,0:T(8,128)(2,1)} %two_ref.3) | copy-start | bytes 4718596
  59.0 2.8 %copy-start.9 = (bf16[528,512]{1,0:T(8,128)(2,1)S(1)}, bf16[528,512]{1,0:T(8,128)(2,1)}, u32[]{:S(2)}) copy-start(bf16[528,512]{1,0:T(8,128)(2,1)} %copy-done.8) | copy-start | bytes 1622020
  59.0 2.8 %copy-start.11 = (bf16[528,512]{1,0:T(8,128)(2,1)S(1)}, bf16[528,512]{1,0:T(8,128)(2,1)}, u32[]{:S(2)}) copy-start(bf16[528,512]{1,0:T(8,128)(2,1)} %copy-done.10) | copy-start | bytes 1622020
  (4 other events, 5.9 us)

commit v6 on v5

--- a/solution.py
+++ b/solution.py
@@ -276,19 +276,25 @@
             even, odd = down[64 * c : 64 * c + 32], down[64 * c + 32 : 64 * c + 64]
             put(idx_ref, keep_ref, send_ref, c % 4, c // 4, slice(0, 32), even, odd, n * CA)
 
-    for n in range(4):
-        if n < 3:
-            one = jnp.zeros((CA, CA), F32)
-            for j in range(4):
-                lanes = slice((j + n) * CA, (j + n + 1) * CA)
-                one += dot(dt_all_ref[:, j * S : (j + 1) * S], uw_ref[:S, lanes])
-            one *= scaling
+    def place(value, at):
+        for c in range(8):
+            even, odd = value[32 * c : 32 * c + 16], value[32 * c + 16 : 32 * c + 32]
+            put(idx_ref, keep_ref, send_ref, c % 4, c // 4, slice(32, 48), even, odd, at)
+
+    for n in range(3):
+        one = jnp.zeros((CA, CA), F32)
+        for j in range(4):
+            lanes = slice((j + n) * CA, (j + n + 1) * CA)
+            one += dot(dt_all_ref[:, j * S : (j + 1) * S], uw_ref[:S, lanes])
+        one *= scaling
+        if n == 1:
+            place(one[:, :128], 256)
+            place(one[:, 128:], 512)
         else:
-            dt = jnp.sum(dt_ref[...].T, axis=1, keepdims=True)
-            one = dt * (emb_ref[...] * scaling)
-        for c in range(8):
-            even, odd = one[32 * c : 32 * c + 16], one[32 * c + 16 : 32 * c + 32]
-            put(idx_ref, keep_ref, send_ref, c % 4, c // 4, slice(32, 48), even, odd, n * CA)
+            place(one, 320 * n)
+    time = jnp.sum(dt_ref[...].T, axis=1, keepdims=True) * (emb_ref[...] * scaling)
+    place(time[:, :128], 384)
+    place(time[:, 128:], 896)
 
 
 def signal_kernel(xp_ref, dm_ref, dp_ref, sg_ref, ys_ref):
@@ -333,31 +339,43 @@
         at += out.shape[0]
 
 
-def join_kernel(own_u, got_u, own_v, got_v, own_ref, send_ref):
-    half = own_u.shape[2]
-    for own, got, lanes in (
-        (own_u, got_u, slice(0, half)),
-        (own_v, got_v, slice(half, 2 * half)),
-    ):
-        own_ref[:, lanes] = (own[0].astype(F32) + got[0].astype(F32)).astype(BF16)
-        send_ref[:, lanes] = (own[1].astype(F32) + got[1].astype(F32)).astype(BF16)
-
-
-def lines_kernel(a_ref, a_got, b_ref, b_got, out_ref):
-    two = a_ref[...].astype(F32) + a_got[...].astype(F32)
-    rest = b_ref[...].astype(F32) + b_got[...].astype(F32)
-    for d in range(16):
-        down = rest[:32, 64 * d : 64 * d + 64]
-        last = rest[32:, 48 * d : 48 * d + 48]
-        time = rest[32:, 3 * CA + 16 * d : 3 * CA + 16 * d + 16]
+def join_kernel(dp_ref, *refs):
+    parts, outs = refs[:8], refs[8:]
+
+    def packed(side, half):
+        a, b = (
+            parts[k][side].astype(F32) + parts[k + 1][side].astype(F32)
+            for k in (2 * half, 4 + 2 * half)
+        )
+        top = jnp.concatenate([a, b[:32, :CA]], axis=1)
+        low = jnp.concatenate([b[:16, CA:], b[16:32, CA:], b[32:]], axis=1)
+        return jnp.concatenate([top, low], axis=0)
+
+    first = dp_ref[0] < 8
+    for side in range(2):
+        zero, one = packed(side, 0), packed(side, 1)
+        outs[2 * side][...] = jnp.where(first, zero, one).astype(BF16)
+        outs[2 * side + 1][...] = jnp.where(first, one, zero).astype(BF16)
+
+
+def lines_kernel(own_ref, lo_ref, hi_ref, both_ref, out_ref):
+    total = own_ref[...].astype(F32) + lo_ref[...].astype(F32)
+    total = total + hi_ref[...].astype(F32) + both_ref[...].astype(F32)
+    two, last = total[:32, : 3 * CA], total[32:, 2 * CA :]
+    rest = jnp.concatenate([total[32:, :CA], total[32:, CA : 2 * CA]], axis=0)
+    rest = jnp.concatenate([total[:32, 3 * CA :], rest], axis=1)
+    for d in range(8):
+        down = rest[:, 64 * d : 64 * d + 64]
+        one = last[:, 48 * d : 48 * d + 48]
+        time = last[:, 384 + 16 * d : 384 + 16 * d + 16]
         top = jnp.concatenate([two[:, 96 * d : 96 * d + 96], down[:, :32]], axis=1)
-        low = jnp.concatenate([down[:16, 32:], down[16:, 32:], last, time], axis=1)
+        low = jnp.concatenate([down[:16, 32:], down[16:, 32:], one, time], axis=1)
         out_ref[d] = jnp.concatenate([top, low], axis=0).astype(BF16)
 
 
 def last_kernel(in_ref, one_ref, down_ref, two_ref, time_ref):
     line = in_ref[0].astype(F32)
-    for d in range(1, 16):
+    for d in range(1, 8):
         line = line + in_ref[d].astype(F32)
     two_ref[...] = line[:32, :96]
     down_ref[:, :32] = line[:32, 96:]
@@ -404,9 +422,9 @@
     return moved(v, lambda y, x, c: y * 8 + (x ^ apart) * 2 + c)
 
 
-def swap_y(v):
-    pairs = [(i, i ^ (8 * 16 + 8)) for i in range(256)]
-    return lax.ppermute(v, AXES, pairs)
+def swap_y(v, apart):
+    flip = 128 * (apart & 1) + 8 * (apart >> 1)
+    return lax.ppermute(v, AXES, [(i, i ^ flip) for i in range(256)])
 
 
 def ring(parts):
@@ -417,12 +435,7 @@
     v, sv = added([v, gv], (2, 2))
     gu = swap_x(su, 3)
     gv = swap_x(sv, 1)
-    rows, half = u.shape[1:]
-    own, send = call(
-        join_kernel, [u, gu, v, gv], [((rows, 2 * half), BF16)] * 2,
-        nbytes=600_000,
-    )
-    return own, swap_y(send)
+    return [u, gu, v, gv]
 
 
 def added(terms, cuts):
@@ -430,7 +443,7 @@
     size = math.prod(terms[0].shape) * 2
     return call(
         lambda *refs: add_kernel(len(terms), *refs), terms,
-        [((n,) + tail, BF16) for n in cuts], nbytes=size * (len(terms) + 1),
+        [((n,) + tail, BF16) for n in cuts], nbytes=size * (len(terms) + 1), room=12,
     )
 
 
@@ -468,7 +481,7 @@
         [((E, 3 * CB), BF16), ((E, CB), F32)], 1_400_000_000, 7_000_000, smem=True,
     )
     a_parts = added([a_keep, a_got], (4, 4, 4, 4))
-    a_own, a_got = ring(a_parts)
+    a_parts = ring(a_parts)
     b_keep, b_send, d_pre = call(
         fine_kernel, [idx, xp, dc, dh, mw, uw, temb, emb, conv_one],
         [((16, 48, 2 * CA), BF16)] * 2 + [((S, 4 * CA), F32)],
@@ -485,12 +498,16 @@
         [((2, 4 * S, 128), F32)], 20_000_000, 6_000_000,
     )
     b_parts = added([b_keep, b_got], (4, 4, 4, 4))
-    b_own, b_got = ring(b_parts)
-    (lines,) = call(
-        lines_kernel, [a_own, a_got, b_own, b_got],
-        [((16, 48, 128), BF16)], nbytes=900_000,
-    )
-    lines = lax.all_to_all(lines, "dp", 0, 0, tiled=True)
+    b_parts = ring(b_parts)
+    dp = lax.axis_index("dp").astype(jnp.int32).reshape(1)
+    parts = call(
+        join_kernel, [dp, *a_parts, *b_parts], [((48, 4 * CA), BF16)] * 4,
+        nbytes=1_200_000, smem=True, room=12,
+    )
+    got = [swap_y(parts[k], k) for k in (1, 2, 3)]
+    (lines,) = call(lines_kernel, [parts[0], *got], [((8, 48, 128), BF16)], nbytes=500_000, room=12)
+    groups = [list(range(8)), list(range(8, 16))]
+    lines = lax.all_to_all(lines, "dp", 0, 0, tiled=True, axis_index_groups=groups)
     outs = call(
         last_kernel, [lines],
         [((16, 48), F32), ((32, 64), F32), ((32, 96), F32), ((16, 16), F32)], nbytes=300_000,

time: 67 us -> 74.8 us (1.12); the launches traced: 66.7 us -> 73.4 us
  Pallas kernels: 19.5 us -> 23.6 us
  waiting for transfers between devices: 7.55 us -> 10.6 us
  starting transfers between devices: 34.8 us -> 32.5 us
  local copies, waits for them, and re-layouts: 3.17 us -> 5.02 us
    pallas_call x17 -> x16, Pallas kernels: 19.5 us -> 23.6 us  [call(): pl.pallas_call(kernel, in_specs=[pl.BlockSpec(memory_space=pltpu.SMEM)] *...]
    ppermute x10, waiting for transfers between devices: 1.48 us -> 4.94 us  [moved(): return lax.ppermute(value, 'tm', pairs)]
    unnamed x26 -> x36, local copies, waits for them, and re-layouts: 3.17 us -> 5.02 us
    ppermute x10, starting transfers between devices: 17.2 us -> 15.4 us  [moved(): return lax.ppermute(value, 'tm', pairs)]
    all_to_all x1, waiting for transfers between devices: 2.32 us -> 1.04 us  [per_device(): lax.all_to_all(lines, 'dp', 0, 0, tiled=True, axis_index_groups=groups)]
    ppermute x2 -> x3, waiting for transfers between devices: 3.75 us -> 4.61 us  [swap_y(): return lax.ppermute(v, AXES, [(i, i ^ flip) for i in range(256)])]
    ppermute x2 -> x3, starting transfers between devices: 5.24 us -> 4.79 us  [swap_y(): return lax.ppermute(v, AXES, [(i, i ^ flip) for i in range(256)])]
  transfers between devices with their start and end apart: 15 -> 16, of which waited for: 4 -> 6; matrix products, arithmetic and copies ran while one was open for 0% -> 0% of each run, Pallas kernels for 20% -> 22%
where the time goes in v6:
time: 74.8 us; the launch traced here: 73.4 us
  starting transfers between devices  32.5 us (43%)
  Pallas kernels  23.6 us (32%)
  waiting for transfers between devices  10.6 us (14%)
  local copies, waits for them, and re-layouts  5.02 us (7%)
  between operations  1.52 us (2%)
    pallas_call x16, Pallas kernels, call(): pl.pallas_call(kernel, in_specs=[pl.BlockSpec(memory_space=pltpu.SMEM)] *...  23.6 us
    ppermute x10, starting transfers between devices, moved(): return lax.ppermute(value, 'tm', pairs)  15.4 us
    all_to_all x1, starting transfers between devices, per_device(): lax.all_to_all(lines, 'dp', 0, 0, tiled=True, axis_index_groups=groups)  8.57 us
    unnamed x36, local copies, waits for them, and re-layouts  5.02 us
    ppermute x10, waiting for transfers between devices, moved(): return lax.ppermute(value, 'tm', pairs)  4.94 us
    ppermute x3, starting transfers between devices, swap_y(): return lax.ppermute(v, AXES, [(i, i ^ flip) for i in range(256)])  4.79 us
    ppermute x3, waiting for transfers between devices, swap_y(): return lax.ppermute(v, AXES, [(i, i ^ flip) for i in range(256)])  4.61 us
    ppermute x1, starting transfers between devices, per_device(): core = lax.ppermute(for_core, 'tm', [(i, i ^ 1) for i in range(16)])  2.94 us
  transfers between devices with their start and end apart: 16, of which 6 were waited for; matrix products, arithmetic and copies ran while one was open for 0% of the time, Pallas kernels for 22%

profile of v6, /device:TPU:32, one launch (start us, length us, event | category | flops | bytes accessed | tf_op | source)
XLA Modules:
  0.0 73.4 jit_solution(15955887611035996169)
XLA Ops:
  0.7 1.5 %shard_map.119 = (bf16[8,768]{1,0:T(8,128)(2,1)}, bf16[8,768]{1,0:T(8,128)(2,1)}) custom-call(s32[1]{0:T(128)} %bitcast.idx_ref, bf16[2048,256]{1,0:T(8,128)(2,1)} %bitcast.16, bf16[512,512]{1,0:T(8,128)(2,1)} %bitcast.18), custom_call_target="tpu_custom_call" | custom-call | bytes 50000 | tf_op jit(solution)/shard_map/pallas_call | solution.py:391
  3.0 2.9 %collective-permute-start.1 = (bf16[8,768]{1,0:T(8,128)(2,1)}, bf16[8,768]{1,0:T(8,128)(2,1)S(1)}, u32[]{:S(2)}, u32[]{:S(2)}) collective-permute-start(bf16[8,768]{1,0:T(8,128)(2,1)} %get-tuple-element.51), channel_id=1, source_target_pairs={{0,1},{1,0},{2,3},{3,2},{4,5},{5,4},{6,7},{7,6},{8,9},{9,8},{10,11... | collective-permute-start | bytes 36872 | tf_op jit(solution)/shard_map/ppermute | solution.py:459
  6.9 1.7 %shard_map.118 = (bf16[512,1024]{1,0:T(8,128)(2,1)S(1)}, bf16[512,1024]{1,0:T(8,128)(2,1)S(1)}, bf16[512,512]{1,0:T(8,128)(2,1)S(1)}, bf16[1024,512]{1,0:T(8,128)(2,1)S(1)}) custom-call(bf16[2048,256]{1,0:T(8,128)(2,1)S(1)} %bitcast.17, bf16[512,512]{1,0:T(8,128)(2,1)S(1)} %bitcast.19, bf16[1024,512]{1,0:T(8,128)(2,1)} %down_ref.1, f32[1,256]{1,0:T(1,128)S(1)} %fusion.temb_ref), custom_call_target="tpu_custom_call" | custom-call | flops 50000000 | bytes 6500000 | tf_op jit(solution)/shard_map/pallas_call | solution.py:391
  8.6 3.4 %shard_map.120 = (bf16[16,32,768]{2,1,0:T(8,128)(2,1)S(1)}, bf16[16,32,768]{2,1,0:T(8,128)(2,1)S(1)}, bf16[528,1024]{1,0:T(8,128)(2,1)S(1)}, bf16[528,1536]{1,0:...) custom-call(s32[1]{0:T(128)} %bitcast.idx_ref, ...), custom_call_target="tpu_custom_call" | custom-call | flops 2200000000 | bytes 10000000 | tf_op jit(solution)/shard_map/pallas_call | solution.py:391
  12.2 2.8 %shard_map.122 = (bf16[528,512]{1,0:T(8,128)(2,1)S(1)}, bf16[528,1024]{1,0:T(8,128)(2,1)S(1)}, f32[512,1024]{1,0:T(8,128)S(1)}) custom-call(s32[1]{0:T(128)} %bitcast.idx_ref, bf16[528,512]{1,0:T(8,128)(2,1)S(1)} %get-tuple-element.54.co_ref, bf16[512,512]{1,0:T(8,128)(2,1)S(1)} %get-tuple-element.52.cot_ref, ...), custom_call_target="tpu_custom_call" | custom-call | flops 1400000000 | bytes 7000000 | tf_op jit(solution)/shard_map/pallas_call | solution.py:391
  15.0 3.9 %shard_map.123 = (bf16[16,48,512]{2,1,0:T(8,128)(2,1)S(1)}, bf16[16,48,512]{2,1,0:T(8,128)(2,1)S(1)}, f32[512,1024]{1,0:T(8,128)S(1)}) custom-call(s32[1]{0:T(128)} %bitcast.idx_ref, bf16[512,1024]{1,0:T(8,128)(2,1)S(1)} %get-tuple-element.48.xp_ref, bf16[528,512]{1,0:T(8,128)(2,1)S(1)} %get-tuple-element.57.dc_ref, ...), custom_call_target="tpu_custom_call" | custom-call | flops 2200000000 | bytes 11000000 | tf_op jit(solution)/shard_map/pallas_call | solution.py:391
  19.6 1.6 %collective-permute-start.3 = (bf16[4,32,768]{2,1,0:T(8,128)(2,1)S(1)}, bf16[4,32,768]{2,1,0:T(8,128)(2,1)S(1)}, u32[]{:S(2)}, u32[]{:S(2)}) collective-permute-start(bf16[4,32,768]{2,1,0:T(8,128)(2,1)S(1)} %get-tuple-element.65), channel_id=1, source_target_pairs={{0,2},{1,3},{2,0},{3,1},{4,6},{5,7},{6,4},{7,5},{8,10},{9,11},{10,... | collective-permute-start | bytes 589832 | tf_op jit(solution)/shard_map/ppermute | solution.py:414
  21.2 3.3 %collective-permute-start.5 = (bf16[4,32,768]{2,1,0:T(8,128)(2,1)S(1)}, bf16[4,32,768]{2,1,0:T(8,128)(2,1)S(1)}, u32[]{:S(2)}, u32[]{:S(2)}) collective-permute-start(bf16[4,32,768]{2,1,0:T(8,128)(2,1)S(1)} %get-tuple-element.69), channel_id=1, source_target_pairs={{0,6},{1,7},{2,4},{3,5},{4,2},{5,3},{6,0},{7,1},{8,14},{9,15},{10,... | collective-permute-start | bytes 589832 | tf_op jit(solution)/shard_map/ppermute | solution.py:414
  24.7 1.4 %collective-permute-start.8 = (bf16[4,48,512]{2,1,0:T(8,128)(2,1)S(1)}, bf16[4,48,512]{2,1,0:T(8,128)(2,1)S(1)}, u32[]{:S(2)}, u32[]{:S(2)}) collective-permute-start(bf16[4,48,512]{2,1,0:T(8,128)(2,1)S(1)} %get-tuple-element.75), channel_id=1, source_target_pairs={{0,2},{1,3},{2,0},{3,1},{4,6},{5,7},{6,4},{7,5},{8,10},{9,11},{10,... | collective-permute-start | bytes 589832 | tf_op jit(solution)/shard_map/ppermute | solution.py:414
  27.6 5.2 %collective-permute-start.4 = (bf16[2,32,768]{2,1,0:T(8,128)(2,1)}, bf16[2,32,768]{2,1,0:T(8,128)(2,1)S(1)}, u32[]{:S(2)}, u32[]{:S(2)}) collective-permute-start(bf16[2,32,768]{2,1,0:T(8,128)(2,1)} %get-tuple-element.67), channel_id=1, source_target_pairs={{0,6},{1,7},{2,4},{3,5},{4,2},{5,3},{6,0},{7,1},{8,14},{9,15},{10,... | collective-permute-start | bytes 294920 | tf_op jit(solution)/shard_map/ppermute | solution.py:414
  34.2 2.4 %collective-permute-start.9 = (bf16[2,48,512]{2,1,0:T(8,128)(2,1)}, bf16[2,48,512]{2,1,0:T(8,128)(2,1)}, u32[]{:S(2)}, u32[]{:S(2)}) collective-permute-start(bf16[2,48,512]{2,1,0:T(8,128)(2,1)} %get-tuple-element.77), channel_id=1, source_target_pairs={{0,6},{1,7},{2,4},{3,5},{4,2},{5,3},{6,0},{7,1},{8,14},{9,15},{10,... | collective-permute-start | bytes 294920 | tf_op jit(solution)/shard_map/ppermute | solution.py:414
  38.4 1.9 %collective-permute-done.9.refs_5_ = bf16[2,48,512]{2,1,0:T(8,128)(2,1)} collective-permute-done((bf16[2,48,512]{2,1,0:T(8,128)(2,1)}, bf16[2,48,512]{2,1,0:T(8,128)(2,1)}, u32[]{:S(2)}, u32[]{:S(2)}) %collective-permute-start.9) | collective-permute-done | bytes 98336 | tf_op jit(solution)/shard_map/ppermute | solution.py:414
  40.3 2.5 %collective-permute-done.11.refs_7_ = bf16[2,48,512]{2,1,0:T(8,128)(2,1)} collective-permute-done((bf16[2,48,512]{2,1,0:T(8,128)(2,1)}, bf16[2,48,512]{2,1,0:T(8,128)(2,1)}, u32[]{:S(2)}, u32[]{:S(2)}) %collective-permute-start.11) | collective-permute-done | bytes 98336 | tf_op jit(solution)/shard_map/ppermute | solution.py:414
  45.5 1.1 %shard_map.131 = (bf16[48,1024]{1,0:T(8,128)(2,1)S(1)}, bf16[48,1024]{1,0:T(8,128)(2,1)S(1)}, bf16[48,1024]{1,0:T(8,128)(2,1)S(1)}, bf16[48,1024]{1,0:T(8,128)(2,1)S(1)}) custom-call(s32[1]{0:T(128)} %bitcast.9.dp_ref, bf16[2,32,768]{2,1,0:T(8,128)(2,1)S(1)} %get-tuple-element.66.refs_0_, bf16[2,32,768]{2,1,0:T(8,128)(2,1)S(1)} %collective-permute-done.4.refs_1_, ...), custom_call_target="tpu_custom_call" | custom-call | bytes 1200000 | tf_op jit(solution)/shard_map/pallas_call | solution.py:391
  46.6 1.7 %collective-permute-start.12 = (bf16[48,1024]{1,0:T(8,128)(2,1)S(1)}, bf16[48,1024]{1,0:T(8,128)(2,1)S(1)}, u32[]{:S(2)}, u32[]{:S(2)}) collective-permute-start(bf16[48,1024]{1,0:T(8,128)(2,1)S(1)} %get-tuple-element.83), channel_id=1, source_target_pairs={{0,128},{1,129},{2,130},{3,131},{4,132},{5,133},{6,134},{7,135},{8... | collective-permute-start | bytes 294920 | tf_op jit(solution)/shard_map/ppermute | solution.py:427
  48.3 1.9 %collective-permute-start.13 = (bf16[48,1024]{1,0:T(8,128)(2,1)S(1)}, bf16[48,1024]{1,0:T(8,128)(2,1)S(1)}, u32[]{:S(2)}, u32[]{:S(2)}) collective-permute-start(bf16[48,1024]{1,0:T(8,128)(2,1)S(1)} %get-tuple-element.84), channel_id=1, source_target_pairs={{0,8},{1,9},{2,10},{3,11},{4,12},{5,13},{6,14},{7,15},{8,0},{9,1},... | collective-permute-start | bytes 294920 | tf_op jit(solution)/shard_map/ppermute | solution.py:427
  50.2 1.2 %collective-permute-start.14 = (bf16[48,1024]{1,0:T(8,128)(2,1)S(1)}, bf16[48,1024]{1,0:T(8,128)(2,1)S(1)}, u32[]{:S(2)}, u32[]{:S(2)}) collective-permute-start(bf16[48,1024]{1,0:T(8,128)(2,1)S(1)} %get-tuple-element.85), channel_id=1, source_target_pairs={{0,136},{1,137},{2,138},{3,139},{4,140},{5,141},{6,142},{7,143},{8... | collective-permute-start | bytes 294920 | tf_op jit(solution)/shard_map/ppermute | solution.py:427
  51.4 3.0 %collective-permute-done.13.hi_ref = bf16[48,1024]{1,0:T(8,128)(2,1)S(1)} collective-permute-done((bf16[48,1024]{1,0:T(8,128)(2,1)S(1)}, bf16[48,1024]{1,0:T(8,128)(2,1)S(1)}, u32[]{:S(2)}, u32[]{:S(2)}) %collective-permute-start.13) | collective-permute-done | bytes 98336 | tf_op jit(solution)/shard_map/ppermute | solution.py:427
  54.4 1.6 %collective-permute-done.14.both_ref = bf16[48,1024]{1,0:T(8,128)(2,1)S(1)} collective-permute-done((bf16[48,1024]{1,0:T(8,128)(2,1)S(1)}, bf16[48,1024]{1,0:T(8,128)(2,1)S(1)}, u32[]{:S(2)}, u32[]{:S(2)}) %collective-permute-start.14) | collective-permute-done | bytes 98336 | tf_op jit(solution)/shard_map/ppermute | solution.py:427
  56.8 8.6 %all-to-all-start = ((bf16[8,48,128]{2,1,0:T(8,128)(2,1)}), bf16[8,48,128]{2,1,0:T(8,128)(2,1)S(1)}, u32[]{:S(2)}, u32[]{:S(2)}) async-start(bf16[8,48,128]{2,1,0:T(8,128)(2,1)} %shard_map.132), calls=%async_computation | async-start | bytes 196608 | tf_op jit(solution)/shard_map/all_to_all | solution.py:510
  65.4 1.6 %copy-done.3 = f32[512,1024]{1,0:T(8,128)S(1)} copy-done((f32[512,1024]{1,0:T(8,128)S(1)}, f32[512,1024]{1,0:T(8,128)}, u32[]{:S(2)}) %copy-start.3) | copy-done | bytes 2097176
  67.0 2.8 %shard_map.124 = bf16[2048,256]{1,0:T(8,128)(2,1)} custom-call(bf16[512,1024]{1,0:T(8,128)(2,1)S(1)} %get-tuple-element.48.xp_ref, f32[512,1024]{1,0:T(8,128)S(1)} %get-tuple-element.56.dm_ref, f32[512,1024]{1,0:T(8,128)S(1)} %copy-done.3), custom_call_target="tpu_custom_call" | custom-call | flops 20000000 | bytes 6000000 | tf_op jit(solution)/shard_map/pallas_call | solution.py:391
  69.8 1.8 %shard_map.121 = bf16[512,512]{1,0:T(8,128)(2,1)} custom-call(bf16[528,512]{1,0:T(8,128)(2,1)S(1)} %copy-done.10, bf16[528,512]{1,0:T(8,128)(2,1)S(1)} %copy-done.8, bf16[1536,512]{1,0:T(8,128)(2,1)S(1)} %copy-done.6), custom_call_target="tpu_custom_call" | custom-call | flops 800000000 | bytes 3000000 | tf_op jit(solution)/shard_map/pallas_call | solution.py:391
  71.6 1.0 %all-to-all-done.in_ref = bf16[8,48,128]{2,1,0:T(8,128)(2,1)S(1)} async-done(((bf16[8,48,128]{2,1,0:T(8,128)(2,1)}), bf16[8,48,128]{2,1,0:T(8,128)(2,1)S(1)}, u32[]{:S(2)}, u32[]{:S(2)}) %all-to-all-start) | async-done | bytes 98336 | tf_op jit(solution)/shard_map/all_to_all | solution.py:510
  (63 shorter events, 11.1 us)
Async XLA Ops:
  0.6 6.0 %copy-start = (bf16[256,256]{1,0:T(8,128)(2,1)S(1)}, bf16[256,256]{1,0:T(8,128)(2,1)}, u32[]{:S(2)}) copy-start(bf16[256,256]{1,0:T(8,128)(2,1)} %param.13) | copy-start | bytes 393220
  0.6 6.2 %copy-start.4 = (bf16[1,512,512]{2,1,0:T(8,128)(2,1)S(1)}, bf16[1,512,512]{2,1,0:T(8,128)(2,1)}, u32[]{:S(2)}) copy-start(bf16[1,512,512]{2,1,0:T(8,128)(2,1)} %param.9) | copy-start | bytes 1572868
  0.7 6.2 %copy-start.1 = (bf16[1,2048,256]{2,1,0:T(8,128)(2,1)S(1)}, bf16[1,2048,256]{2,1,0:T(8,128)(2,1)}, u32[]{:S(2)}) copy-start(bf16[1,2048,256]{2,1,0:T(8,128)(2,1)} %param.7) | copy-start | bytes 3145732
  2.2 6.4 %copy-start.17 = (bf16[768,256]{1,0:T(8,128)(2,1)S(1)}, bf16[768,256]{1,0:T(8,128)(2,1)}, u32[]{:S(2)}) copy-start(bf16[768,256]{1,0:T(8,128)(2,1)} %one_ref.3) | copy-start | bytes 1179652
  2.2 6.4 %collective-permute-start = (bf16[8,768]{1,0:T(8,128)(2,1)}, bf16[8,768]{1,0:T(8,128)(2,1)S(1)}, u32[]{:S(2)}, u32[]{:S(2)}) collective-permute-start(bf16[8,768]{1,0:T(8,128)(2,1)} %get-tuple-element.50), channel_id=1, source_target_pairs={{1,2},{2,1},{3,4},{4,3},{5,6},{6,5},{7,8},{8,7},{9,10},{10,9},{11,... | collective-permute-start | bytes 36872 | tf_op jit(solution)/shard_map/ppermute | solution.py:458
  3.0 5.6 %collective-permute-start.1 = (bf16[8,768]{1,0:T(8,128)(2,1)}, bf16[8,768]{1,0:T(8,128)(2,1)S(1)}, u32[]{:S(2)}, u32[]{:S(2)}) collective-permute-start(bf16[8,768]{1,0:T(8,128)(2,1)} %get-tuple-element.51), channel_id=1, source_target_pairs={{0,1},{1,0},{2,3},{3,2},{4,5},{5,4},{6,7},{7,6},{8,9},{9,8},{10,11... | collective-permute-start | bytes 36872 | tf_op jit(solution)/shard_map/ppermute | solution.py:459
  8.6 3.6 %copy-start.5 = (bf16[1536,512]{1,0:T(8,128)(2,1)S(1)}, bf16[1536,512]{1,0:T(8,128)(2,1)}, u32[]{:S(2)}) copy-start(bf16[1536,512]{1,0:T(8,128)(2,1)} %two_ref.3) | copy-start | bytes 4718596
  12.1 7.4 %collective-permute-start.2 = (bf16[16,32,768]{2,1,0:T(8,128)(2,1)S(1)}, bf16[16,32,768]{2,1,0:T(8,128)(2,1)S(1)}, u32[]{:S(2)}, u32[]{:S(2)}) collective-permute-start(bf16[16,32,768]{2,1,0:T(8,128)(2,1)S(1)} %get-tuple-element.63), channel_id=1, source_target_pairs={{0,1},{1,0},{2,3},{3,2},{4,5},{5,4},{6,7},{7,6},{8,9},{9,8},{10,11... | collective-permute-start | bytes 2359304 | tf_op jit(solution)/shard_map/ppermute | solution.py:414
  18.8 8.8 %copy-start.2 = (f32[512,1024]{1,0:T(8,128)}, f32[512,1024]{1,0:T(8,128)S(1)}, u32[]{:S(2)}) copy-start(f32[512,1024]{1,0:T(8,128)S(1)} %get-tuple-element.61.dp_ref) | copy-start | bytes 6291460
  18.8 5.6 %collective-permute-start.7 = (bf16[16,48,512]{2,1,0:T(8,128)(2,1)S(1)}, bf16[16,48,512]{2,1,0:T(8,128)(2,1)S(1)}, u32[]{:S(2)}, u32[]{:S(2)}) collective-permute-start(bf16[16,48,512]{2,1,0:T(8,128)(2,1)S(1)} %get-tuple-element.73), channel_id=1, source_target_pairs={{0,1},{1,0},{2,3},{3,2},{4,5},{5,4},{6,7},{7,6},{8,9},{9,8},{10,11... | collective-permute-start | bytes 2359304 | tf_op jit(solution)/shard_map/ppermute | solution.py:414
  19.6 7.3 %collective-permute-start.3 = (bf16[4,32,768]{2,1,0:T(8,128)(2,1)S(1)}, bf16[4,32,768]{2,1,0:T(8,128)(2,1)S(1)}, u32[]{:S(2)}, u32[]{:S(2)}) collective-permute-start(bf16[4,32,768]{2,1,0:T(8,128)(2,1)S(1)} %get-tuple-element.65), channel_id=1, source_target_pairs={{0,2},{1,3},{2,0},{3,1},{4,6},{5,7},{6,4},{7,5},{8,10},{9,11},{10,... | collective-permute-start | bytes 589832 | tf_op jit(solution)/shard_map/ppermute | solution.py:414
  21.2 11.6 %collective-permute-start.5 = (bf16[4,32,768]{2,1,0:T(8,128)(2,1)S(1)}, bf16[4,32,768]{2,1,0:T(8,128)(2,1)S(1)}, u32[]{:S(2)}, u32[]{:S(2)}) collective-permute-start(bf16[4,32,768]{2,1,0:T(8,128)(2,1)S(1)} %get-tuple-element.69), channel_id=1, source_target_pairs={{0,6},{1,7},{2,4},{3,5},{4,2},{5,3},{6,0},{7,1},{8,14},{9,15},{10,... | collective-permute-start | bytes 589832 | tf_op jit(solution)/shard_map/ppermute | solution.py:414
  24.7 8.8 %collective-permute-start.8 = (bf16[4,48,512]{2,1,0:T(8,128)(2,1)S(1)}, bf16[4,48,512]{2,1,0:T(8,128)(2,1)S(1)}, u32[]{:S(2)}, u32[]{:S(2)}) collective-permute-start(bf16[4,48,512]{2,1,0:T(8,128)(2,1)S(1)} %get-tuple-element.75), channel_id=1, source_target_pairs={{0,2},{1,3},{2,0},{3,1},{4,6},{5,7},{6,4},{7,5},{8,10},{9,11},{10,... | collective-permute-start | bytes 589832 | tf_op jit(solution)/shard_map/ppermute | solution.py:414
  26.1 10.5 %collective-permute-start.10 = (bf16[4,48,512]{2,1,0:T(8,128)(2,1)S(1)}, bf16[4,48,512]{2,1,0:T(8,128)(2,1)S(1)}, u32[]{:S(2)}, u32[]{:S(2)}) collective-permute-start(bf16[4,48,512]{2,1,0:T(8,128)(2,1)S(1)} %get-tuple-element.79), channel_id=1, source_target_pairs={{0,6},{1,7},{2,4},{3,5},{4,2},{5,3},{6,0},{7,1},{8,14},{9,15},{10,... | collective-permute-start | bytes 589832 | tf_op jit(solution)/shard_map/ppermute | solution.py:414
  27.6 10.3 %collective-permute-start.4 = (bf16[2,32,768]{2,1,0:T(8,128)(2,1)}, bf16[2,32,768]{2,1,0:T(8,128)(2,1)S(1)}, u32[]{:S(2)}, u32[]{:S(2)}) collective-permute-start(bf16[2,32,768]{2,1,0:T(8,128)(2,1)} %get-tuple-element.67), channel_id=1, source_target_pairs={{0,6},{1,7},{2,4},{3,5},{4,2},{5,3},{6,0},{7,1},{8,14},{9,15},{10,... | collective-permute-start | bytes 294920 | tf_op jit(solution)/shard_map/ppermute | solution.py:414
  33.5 3.7 %copy-start.11 = (bf16[2,32,768]{2,1,0:T(8,128)(2,1)}, bf16[2,32,768]{2,1,0:T(8,128)(2,1)S(1)}, u32[]{:S(2)}) copy-start(bf16[2,32,768]{2,1,0:T(8,128)(2,1)S(1)} %get-tuple-element.70.refs_2_) | copy-start | bytes 294916
  33.5 4.9 %collective-permute-start.6 = (bf16[2,32,768]{2,1,0:T(8,128)(2,1)}, bf16[2,32,768]{2,1,0:T(8,128)(2,1)}, u32[]{:S(2)}, u32[]{:S(2)}) collective-permute-start(bf16[2,32,768]{2,1,0:T(8,128)(2,1)} %get-tuple-element.71), channel_id=1, source_target_pairs={{0,2},{1,3},{2,0},{3,1},{4,6},{5,7},{6,4},{7,5},{8,10},{9,11},{10,... | collective-permute-start | bytes 294920 | tf_op jit(solution)/shard_map/ppermute | solution.py:414
  34.2 3.7 %copy-start.13 = (bf16[2,48,512]{2,1,0:T(8,128)(2,1)}, bf16[2,48,512]{2,1,0:T(8,128)(2,1)S(1)}, u32[]{:S(2)}) copy-start(bf16[2,48,512]{2,1,0:T(8,128)(2,1)S(1)} %get-tuple-element.76.refs_4_) | copy-start | bytes 294916
  34.2 6.1 %collective-permute-start.9 = (bf16[2,48,512]{2,1,0:T(8,128)(2,1)}, bf16[2,48,512]{2,1,0:T(8,128)(2,1)}, u32[]{:S(2)}, u32[]{:S(2)}) collective-permute-start(bf16[2,48,512]{2,1,0:T(8,128)(2,1)} %get-tuple-element.77), channel_id=1, source_target_pairs={{0,6},{1,7},{2,4},{3,5},{4,2},{5,3},{6,0},{7,1},{8,14},{9,15},{10,... | collective-permute-start | bytes 294920 | tf_op jit(solution)/shard_map/ppermute | solution.py:414
  37.9 4.9 %collective-permute-start.11 = (bf16[2,48,512]{2,1,0:T(8,128)(2,1)}, bf16[2,48,512]{2,1,0:T(8,128)(2,1)}, u32[]{:S(2)}, u32[]{:S(2)}) collective-permute-start(bf16[2,48,512]{2,1,0:T(8,128)(2,1)} %get-tuple-element.81), channel_id=1, source_target_pairs={{0,2},{1,3},{2,0},{3,1},{4,6},{5,7},{6,4},{7,5},{8,10},{9,11},{10,... | collective-permute-start | bytes 294920 | tf_op jit(solution)/shard_map/ppermute | solution.py:414
  46.6 4.8 %collective-permute-start.12 = (bf16[48,1024]{1,0:T(8,128)(2,1)S(1)}, bf16[48,1024]{1,0:T(8,128)(2,1)S(1)}, u32[]{:S(2)}, u32[]{:S(2)}) collective-permute-start(bf16[48,1024]{1,0:T(8,128)(2,1)S(1)} %get-tuple-element.83), channel_id=1, source_target_pairs={{0,128},{1,129},{2,130},{3,131},{4,132},{5,133},{6,134},{7,135},{8... | collective-permute-start | bytes 294920 | tf_op jit(solution)/shard_map/ppermute | solution.py:427
  48.3 6.1 %collective-permute-start.13 = (bf16[48,1024]{1,0:T(8,128)(2,1)S(1)}, bf16[48,1024]{1,0:T(8,128)(2,1)S(1)}, u32[]{:S(2)}, u32[]{:S(2)}) collective-permute-start(bf16[48,1024]{1,0:T(8,128)(2,1)S(1)} %get-tuple-element.84), channel_id=1, source_target_pairs={{0,8},{1,9},{2,10},{3,11},{4,12},{5,13},{6,14},{7,15},{8,0},{9,1},... | collective-permute-start | bytes 294920 | tf_op jit(solution)/shard_map/ppermute | solution.py:427
  50.2 5.8 %collective-permute-start.14 = (bf16[48,1024]{1,0:T(8,128)(2,1)S(1)}, bf16[48,1024]{1,0:T(8,128)(2,1)S(1)}, u32[]{:S(2)}, u32[]{:S(2)}) collective-permute-start(bf16[48,1024]{1,0:T(8,128)(2,1)S(1)} %get-tuple-element.85), channel_id=1, source_target_pairs={{0,136},{1,137},{2,138},{3,139},{4,140},{5,141},{6,142},{7,143},{8... | collective-permute-start | bytes 294920 | tf_op jit(solution)/shard_map/ppermute | solution.py:427
  56.8 15.8 %all-to-all-start = ((bf16[8,48,128]{2,1,0:T(8,128)(2,1)}), bf16[8,48,128]{2,1,0:T(8,128)(2,1)S(1)}, u32[]{:S(2)}, u32[]{:S(2)}) async-start(bf16[8,48,128]{2,1,0:T(8,128)(2,1)} %shard_map.132), calls=%async_computation | async-start | bytes 196608 | tf_op jit(solution)/shard_map/all_to_all | solution.py:510
  (10 other events, 19.3 us)
